TPU v7x, 32 devices: a whole 2x2x4 slice. The times are simulated.
32 devices in a mesh: row: 2 (over y), circ: 4 (over x, core), span: 4 (over z).
Axes of the slice: x: 2, y: 2, z: 4, core: 2. Of those that a mesh axis runs over, the one named last changes fastest.
Arguments:
- density: float32 [2, 32, 64, 256], P('row', 'circ', 'span'), may hold values from 0.6 to 1.6
- velocity: float32 [2, 3, 32, 64, 256], P('row', None, 'circ', 'span'), may hold values from -1.2 to 1.2
- pressure: float32 [2, 32, 64, 256], P('row', 'circ', 'span'), may hold values from 0.6 to 1.6
- blade_force: float32 [2, 3, 32, 64, 256], P('row', None, 'circ', 'span'), may hold values from -4 to 4
- offsets: int32 [2], replicated, may hold values from 0 to 31
- weights: float32 [2, 4], replicated, may hold values from 0.1 to 1
Outputs:
- state: float32 [2, 5, 32, 64, 256], P('row', None, 'circ', 'span')
- plane_flux: float32 [2, 2, 5, 32, 64], P('row', None, None, 'circ', 'span')
All inputs are finite; a program needn't handle non-finite values.
Results may differ from a plain program's by a relative error of at most 0.0003.
Values sent between devices are 32-bit elements; how exact they have to be, the bound alone decides.
No kernel may reach another device: no remote copies, remote signals or barrier semaphores. Data moves between devices by JAX's collectives and lax.ppermute only.
A program may use at most 64 MiB of HBM per device.

v0:
```python
import jax
import jax.numpy as jnp
from jax import lax
from jax.sharding import PartitionSpec as P

HEAT_RATIO = 1.4
TIME_STEP = 0.04


def from_partner(block, axis, apart):
    count = lax.axis_size(axis)
    route = []
    for low in range(count):
        high = low | 1 << apart
        if high != low and high < count:
            route += [(low, high), (high, low)]
    return lax.ppermute(block, axis, route)


def extended(cells, sides, width):
    for axis, dim in sides:
        count = lax.axis_size(axis)
        head = lax.slice_in_dim(cells, 0, width, axis=dim)
        tail = lax.slice_in_dim(cells, cells.shape[dim] - width, cells.shape[dim], axis=dim)
        cells = jnp.concatenate(
            [
                lax.ppermute(tail, axis, [(i, (i + 1) % count) for i in range(count)]),
                cells,
                lax.ppermute(head, axis, [((i + 1) % count, i) for i in range(count)]),
            ],
            axis=dim,
        )
    return cells


def direction_flux(cells, direction):
    density_here = cells[0]
    momentum = cells[1:4]
    energy = cells[4]
    kinetic = (
        0.5
        * (momentum[0] * momentum[0] + momentum[1] * momentum[1] + momentum[2] * momentum[2])
        / density_here
    )
    pressure_now = (HEAT_RATIO - 1.0) * (energy - kinetic)
    normal = momentum[direction] / density_here
    components = [
        momentum[direction],
        momentum[0] * normal,
        momentum[1] * normal,
        momentum[2] * normal,
        (energy + pressure_now) * normal,
    ]
    components[1 + direction] = components[1 + direction] + pressure_now
    wave_speed = jnp.abs(normal) + jnp.sqrt(HEAT_RATIO * pressure_now / density_here)
    return (jnp.stack(components), wave_speed)


def face_flux(left_state, right_state, direction):
    left_flux, left_speed = direction_flux(left_state, direction)
    right_flux, right_speed = direction_flux(right_state, direction)
    top_speed = jnp.maximum(left_speed, right_speed)
    return 0.5 * (left_flux + right_flux) - 0.5 * top_speed * (right_state - left_state)


def region_step(padded, force, lower_ghost, upper_ghost):
    region = padded[:, 1:-1, 1:-1]
    circ_flux = face_flux(padded[:, :-1, 1:-1], padded[:, 1:, 1:-1], 1)
    span_flux = face_flux(padded[:, 1:-1, :-1], padded[:, 1:-1, 1:], 2)
    axial_row = jnp.concatenate([lower_ghost, region, upper_ghost], 3)
    axial_flux = face_flux(axial_row[..., :-1], axial_row[..., 1:], 0)
    divergence = (
        axial_flux[..., 1:]
        - axial_flux[..., :-1]
        + (circ_flux[:, 1:] - circ_flux[:, :-1])
        + (span_flux[:, :, 1:] - span_flux[:, :, :-1])
    )
    source = jnp.stack(
        [
            jnp.zeros_like(region[0]),
            region[0] * force[0],
            region[0] * force[1],
            region[0] * force[2],
            jnp.sum(region[1:4] * force, axis=0),
        ]
    )
    updated = region - TIME_STEP * divergence + TIME_STEP * source
    return (updated, axial_flux[..., 0], axial_flux[..., -1])


def conserved(density_row, velocity_row, pressure_row):
    momentum = density_row[None] * velocity_row
    energy = pressure_row / (HEAT_RATIO - 1.0) + 0.5 * density_row * jnp.sum(
        velocity_row * velocity_row, axis=0
    )
    return jnp.concatenate([density_row[None], momentum, energy[None]], 0)


def apply_walls(padded, margin, at_hub, at_casing):
    flip_sign = jnp.array([1.0, 1.0, 1.0, -1.0, 1.0], jnp.float32).reshape(5, 1, 1, 1)
    width_total = padded.shape[2]
    hub_mirror = jnp.flip(padded[:, :, margin : 2 * margin], axis=2) * flip_sign
    casing_mirror = (
        jnp.flip(padded[:, :, width_total - 2 * margin : width_total - margin], axis=2) * flip_sign
    )
    hub_part = jnp.where(at_hub, hub_mirror, padded[:, :, :margin])
    casing_part = jnp.where(at_casing, casing_mirror, padded[:, :, width_total - margin :])
    return jnp.concatenate([hub_part, padded[:, :, margin : width_total - margin], casing_part], 2)


def interface(plane_layer, turn_cells, tap_weights, extent):
    partner = from_partner(plane_layer, "row", 0)
    sector_cells = plane_layer.shape[1]
    sectors = lax.axis_size("circ")
    cycle_cells = sector_cells * sectors
    length = sector_cells + 2 * extent
    whole_cycle = lax.all_gather(partner, "circ", axis=1, tiled=True)
    doubled = jnp.concatenate([whole_cycle, whole_cycle], 1)
    start = (lax.axis_index("circ") * sector_cells - extent + turn_cells - 1) % cycle_cells
    window = lax.dynamic_slice_in_dim(doubled, start, length + 3, 1)
    ghost_layer = jnp.zeros_like(window[:, :length])
    for tap_index in range(4):
        ghost_layer = (
            ghost_layer + tap_weights[tap_index] * window[:, tap_index : tap_index + length]
        )
    return ghost_layer


def advance(padded, force, extent, row_index, turn_cells, tap_weights):
    circ_total = padded.shape[1]
    span_total = padded.shape[2]
    own_cells = padded[:, extent + 1 : circ_total - extent - 1, 1 : span_total - 1]
    plane_layer = jnp.where(row_index == 0, own_cells[..., -1], own_cells[..., 0])
    ghost_layer = interface(plane_layer, turn_cells, tap_weights, extent)[..., None]
    region = padded[:, 1:-1, 1:-1]
    inlet = jnp.array([1.0, 0.5, 0.0, 0.0, 2.625], jnp.float32).reshape(5, 1, 1, 1)
    lower_ghost = jnp.where(row_index == 0, jnp.broadcast_to(inlet, ghost_layer.shape), ghost_layer)
    upper_ghost = jnp.where(row_index == 0, ghost_layer, region[..., -1:])
    updated, first_face, last_face = region_step(padded, force, lower_ghost, upper_ghost)
    plane = jnp.where(row_index == 0, last_face, first_face)
    return (updated, plane)


def body(density, velocity, pressure, blade_force, offsets, weights):
    cells = conserved(density[0], velocity[0], pressure[0])
    force = blade_force[0]
    sector_cells = cells.shape[1]
    cycle_cells = sector_cells * lax.axis_size("circ")
    row_index = lax.axis_index("row")
    at_hub = lax.axis_index("span") == 0
    at_casing = lax.axis_index("span") == lax.axis_size("span") - 1
    tap_weights = weights / jnp.sum(weights, axis=1, keepdims=True)
    step_count = offsets.shape[0]
    turns = []
    for step_index in range(step_count):
        turn = offsets[step_index]
        turns.append(jnp.where(row_index == 0, turn, (cycle_cells - turn) % cycle_cells))
    planes = []
    for step_index in range(step_count):
        padded = extended(cells, (("circ", 1), ("span", 2)), 1)
        padded = apply_walls(padded, 1, at_hub, at_casing)
        cells, plane = advance(
            padded, force, 0, row_index, turns[step_index], tap_weights[step_index]
        )
        planes.append(plane)
    return (cells[None], jnp.stack(planes)[None])


def solution(mesh):
    placed = (
        P("row", "circ", "span", None),
        P("row", None, "circ", "span", None),
        P("row", "circ", "span", None),
        P("row", None, "circ", "span", None),
        P(),
        P(),
    )
    return jax.shard_map(
        body,
        mesh=mesh,
        in_specs=placed,
        out_specs=(P("row", None, "circ", "span", None), P("row", None, None, "circ", "span")),
        check_vma=False,
    )
```

profile of v0, /device:TPU:0, one launch (start us, length us, event | category | flops | bytes accessed | tf_op | source)
XLA Modules:
  0.0 70.5 jit_solution(2010250041633689988)
XLA Ops:
  0.7 0.9 %copy-done = f32[1,8,16,256]{3,2,1,0:T(8,128)S(1)} copy-done((f32[1,8,16,256]{3,2,1,0:T(8,128)S(1)}, f32[1,8,16,256]{3,2,1,0:T(8,128)}, u32[]{:S(2)}) %copy-start) | copy-done | bytes 131096
  1.5 1.0 %constant_dynamic-update-slice_fusion.7 = f32[5,8,16,256]{3,2,1,0:T(8,128)S(1)} fusion(f32[5,8,16,256]{3,2,1,0:T(8,128)S(1)} %constant_dynamic-update-slice_fusion.8, f32[1,8,16,256]{3,2,1,0:T(8,128)S(1)} %copy-done, f32[1,3,8,16,256]{4,3,2,1,0:T(8,128)} %param.13), kind=kLoop, calls=%fused_computation.234 | loop fusion | flops 32768 | bytes 393216
  2.7 0.8 %copy-done.6 = f32[1,8,16,256]{3,2,1,0:T(8,128)S(1)} copy-done((f32[1,8,16,256]{3,2,1,0:T(8,128)S(1)}, f32[1,8,16,256]{3,2,1,0:T(8,128)}, u32[]{:S(2)}) %copy-start.6) | copy-done | bytes 131096
  3.6 0.8 %copy-done.3 = f32[5,8,16,256]{3,2,1,0:T(8,128)} copy-done((f32[5,8,16,256]{3,2,1,0:T(8,128)}, f32[5,8,16,256]{3,2,1,0:T(8,128)S(1)}, u32[]{:S(2)}) %copy-start.3) | copy-done | bytes 655384
  4.8 3.1 %collective-permute-start = (f32[5,8,16]{2,1,0:T(8,128)S(1)}, f32[5,8,16]{2,1,0:T(8,128)S(1)}, u32[]{:S(2)}, u32[]{:S(2)}) collective-permute-start(f32[5,8,16]{2,1,0:T(8,128)S(1)} %fusion.29), channel_id=1, source_target_pairs={{0,16},{16,0},{1,17},{17,1},{2,18},{18,2},{3,19},{19,3},{4,20},{20... | collective-permute-start | bytes 7688 | tf_op jit(solution)/shard_map/ppermute | solution.py:17
  7.9 1.7 %collective-permute-start.2 = (f32[5,1,16,256]{3,2,1,0:T(8,128)S(1)}, f32[5,1,16,256]{3,2,1,0:T(8,128)S(1)}, u32[]{:S(2)}, u32[]{:S(2)}) collective-permute-start(f32[5,1,16,256]{3,2,1,0:T(8,128)S(1)} %get-tuple-element.85), channel_id=1, source_target_pairs={{4,0},{8,4},{12,8},{0,12},{5,1},{9,5},{13,9},{1,13},{6,2},{10,6},{... | collective-permute-start | bytes 245768 | tf_op jit(solution)/shard_map/ppermute | solution.py:29
  9.7 0.6 fusion.76
  10.8 0.7 constant_dynamic-update-slice_fusion.19
  12.0 0.7 copy-done.8
  12.9 0.7 fusion.75
  14.4 0.7 constant_dynamic-update-slice_fusion.4
  16.4 5.3 %all_gather.6 = f32[5,32,16]{2,1,0:T(8,128)S(1)} all-gather(f32[5,8,16]{2,1,0:T(8,128)S(1)} %collective-permute-done), channel_id=1, replica_groups=mesh['row'=2,'circ'=4,'span'=4] {'circ'}, dimensions={1}, use_global_device_ids=true | all-gather | bytes 12800 | tf_op jit(solution)/shard_map/all_gather | solution.py:117
  21.7 0.6 copy-done.9
  22.4 2.6 %select_bitcast_fusion.1 = (f32[5,8,16,1]{2,1,0,3:T(8,128)S(1)}, f32[5,8,16]{2,1,0:T(8,128)S(1)}) fusion(f32[5]{0:T(128)S(1)} %copy-done.9, pred[]{:T(512)S(6)} %eq.11, f32[5,11,16]{2,1,0:T(8,128)S(1)} %fusion.52, f32[]{:T(128)} %bitcast.7, f32[]{:T(128)} %bitcast.6, f32[]{:T(128)} %bitcast.5, f32[]{:T(128)} %bitcast.3), kind=kLoop, calls=%fused_computation.287 | loop fusion | flops 5120 | bytes 15397 | tf_op jit(solution)/shard_map/jit(_where)/select_n | solution.py:137
  26.7 0.4 multiply_subtract_fusion
  28.0 3.7 %collective-permute-start.4 = (f32[5,10,1,256]{3,2,1,0:T(1,128)S(1)}, f32[5,10,1,256]{3,2,1,0:T(1,128)S(1)}, u32[]{:S(2)}, u32[]{:S(2)}) collective-permute-start(f32[5,10,1,256]{3,2,1,0:T(1,128)S(1)} %pad_maximum_fusion.50), channel_id=1, source_target_pairs={{1,0},{2,1},{3,2},{0,3},{5,4},{6,5},{7,6},{4,7},{9,8},{10,9},{11,1... | collective-permute-start | bytes 153608 | tf_op jit(solution)/shard_map/ppermute | solution.py:29
  31.7 1.7 %collective-permute-done.4 = f32[5,10,1,256]{3,2,1,0:T(1,128)S(1)} collective-permute-done((f32[5,10,1,256]{3,2,1,0:T(1,128)S(1)}, f32[5,10,1,256]{3,2,1,0:T(1,128)S(1)}, u32[]{:S(2)}, u32[]{:S(2)}) %collective-permute-start.4) | collective-permute-done | bytes 51232 | tf_op jit(solution)/shard_map/ppermute | solution.py:29
  34.2 5.6 %collective-permute-done.3 = f32[5,10,1,256]{3,2,1,0:T(1,128)S(1)} collective-permute-done((f32[5,10,1,256]{3,2,1,0:T(1,128)S(1)}, f32[5,10,1,256]{3,2,1,0:T(1,128)S(1)}, u32[]{:S(2)}, u32[]{:S(2)}) %collective-permute-start.3) | collective-permute-done | bytes 51232 | tf_op jit(solution)/shard_map/ppermute | solution.py:27
  41.1 0.7 %copy-done.4 = f32[5,8,16,256]{3,2,1,0:T(8,128)S(1)} copy-done((f32[5,8,16,256]{3,2,1,0:T(8,128)S(1)}, f32[5,8,16,256]{3,2,1,0:T(8,128)}, u32[]{:S(2)}) %copy-start.4) | copy-done | bytes 655384
  41.9 0.5 fusion.21
  42.8 0.6 collective-permute-start.5
  43.4 0.4 copy-done.2
  44.7 1.7 %collective-permute-start.7 = (f32[5,1,16,256]{3,2,1,0:T(8,128)S(1)}, f32[5,1,16,256]{3,2,1,0:T(8,128)S(1)}, u32[]{:S(2)}, u32[]{:S(2)}) collective-permute-start(f32[5,1,16,256]{3,2,1,0:T(8,128)S(1)} %get-tuple-element.79), channel_id=1, source_target_pairs={{4,0},{8,4},{12,8},{0,12},{5,1},{9,5},{13,9},{1,13},{6,2},{10,6},{... | collective-permute-start | bytes 245768 | tf_op jit(solution)/shard_map/ppermute | solution.py:29
  46.6 5.3 %all_gather.7 = f32[5,32,16]{2,1,0:T(8,128)S(1)} all-gather(f32[5,8,16]{2,1,0:T(8,128)S(1)} %collective-permute-done.5), channel_id=1, replica_groups=mesh['row'=2,'circ'=4,'span'=4] {'circ'}, dimensions={1}, use_global_device_ids=true | all-gather | bytes 12800 | tf_op jit(solution)/shard_map/all_gather | solution.py:117
  51.9 2.5 %select_bitcast_fusion = (f32[5,8,16,1]{2,1,0,3:T(8,128)S(1)}, f32[5,8,16]{2,1,0:T(8,128)S(1)}) fusion(f32[5]{0:T(128)S(1)} %copy-done.9, pred[]{:T(512)S(6)} %eq.11, f32[5,11,16]{2,1,0:T(8,128)S(1)} %fusion.51, f32[]{:T(128)} %bitcast.22, f32[]{:T(128)} %bitcast.21, f32[]{:T(128)} %bitcast.20, f32[]{:T(128)} %bitcast.18), kind=kLoop, calls=%fused_computation.286 | loop fusion | flops 5120 | bytes 15397 | tf_op jit(solution)/shard_map/jit(_where)/select_n | solution.py:137
  55.2 0.4 multiply_bitcast_fusion.1
  56.2 0.4 fusion.2
  56.8 0.6 maximum_bitcast_fusion
  57.6 2.1 %collective-permute-start.9 = (f32[5,10,1,256]{3,2,1,0:T(1,128)S(1)}, f32[5,10,1,256]{3,2,1,0:T(1,128)S(1)}, u32[]{:S(2)}, u32[]{:S(2)}) collective-permute-start(f32[5,10,1,256]{3,2,1,0:T(1,128)S(1)} %pad_maximum_fusion.45), channel_id=1, source_target_pairs={{1,0},{2,1},{3,2},{0,3},{5,4},{6,5},{7,6},{4,7},{9,8},{10,9},{11,1... | collective-permute-start | bytes 153608 | tf_op jit(solution)/shard_map/ppermute | solution.py:29
  60.0 1.8 %collective-permute-done.9 = f32[5,10,1,256]{3,2,1,0:T(1,128)S(1)} collective-permute-done((f32[5,10,1,256]{3,2,1,0:T(1,128)S(1)}, f32[5,10,1,256]{3,2,1,0:T(1,128)S(1)}, u32[]{:S(2)}, u32[]{:S(2)}) %collective-permute-start.9) | collective-permute-done | bytes 51232 | tf_op jit(solution)/shard_map/ppermute | solution.py:29
  62.3 5.6 %collective-permute-done.8 = f32[5,10,1,256]{3,2,1,0:T(1,128)S(1)} collective-permute-done((f32[5,10,1,256]{3,2,1,0:T(1,128)S(1)}, f32[5,10,1,256]{3,2,1,0:T(1,128)S(1)}, u32[]{:S(2)}, u32[]{:S(2)}) %collective-permute-start.8) | collective-permute-done | bytes 51232 | tf_op jit(solution)/shard_map/ppermute | solution.py:27
  69.2 1.3 %fusion.16 = f32[1,5,8,16,256]{4,3,2,1,0:T(8,128)} fusion(f32[5,8,16,256]{3,2,1,0:T(8,128)S(1)} %fusion.21, f32[5,8,17,256]{3,2,1,0:T(8,128)S(1)} %fusion.5, f32[5,9,16,256]{3,2,1,0:T(8,128)S(1)} %fusion.11, f32[5,8,16,257]{3,2,1,0:T(8,128)S(1)} %fusion.2, f32[5,8,16,256]{3,2,1,0:T(8,128)S(1)} %constant_dynamic-update-slice_fusion.15), kind=kLoop, calls=%fused_computation.83 | loop fusion | flops 1474560 | bytes 5898240 | tf_op jit(solution)/shard_map/broadcast_in_dim | solution.py:166
  (123 shorter events, 11.2 us)
Async XLA Ops:
  0.6 0.9 %copy-start = (f32[1,8,16,256]{3,2,1,0:T(8,128)S(1)}, f32[1,8,16,256]{3,2,1,0:T(8,128)}, u32[]{:S(2)}) copy-start(f32[1,8,16,256]{3,2,1,0:T(8,128)} %param.10) | copy-start | bytes 393220
  0.6 1.9 %copy-start.1 = (f32[1,3,8,16,256]{4,3,2,1,0:T(8,128)S(1)}, f32[1,3,8,16,256]{4,3,2,1,0:T(8,128)}, u32[]{:S(2)}) copy-start(f32[1,3,8,16,256]{4,3,2,1,0:T(8,128)} %param.13) | copy-start | bytes 1179652
  1.5 1.1 %copy-start.5 = (f32[1,3,8,16,256]{4,3,2,1,0:T(8,128)S(1)}, f32[1,3,8,16,256]{4,3,2,1,0:T(8,128)}, u32[]{:S(2)}) copy-start(f32[1,3,8,16,256]{4,3,2,1,0:T(8,128)} %param.11) | copy-start | bytes 1179652
  2.6 0.9 %copy-start.6 = (f32[1,8,16,256]{3,2,1,0:T(8,128)S(1)}, f32[1,8,16,256]{3,2,1,0:T(8,128)}, u32[]{:S(2)}) copy-start(f32[1,8,16,256]{3,2,1,0:T(8,128)} %param.12) | copy-start | bytes 393220
  3.6 0.8 %copy-start.3 = (f32[5,8,16,256]{3,2,1,0:T(8,128)}, f32[5,8,16,256]{3,2,1,0:T(8,128)S(1)}, u32[]{:S(2)}) copy-start(f32[5,8,16,256]{3,2,1,0:T(8,128)S(1)} %get-tuple-element.87) | copy-start | bytes 1966084
  4.8 11.6 %collective-permute-start = (f32[5,8,16]{2,1,0:T(8,128)S(1)}, f32[5,8,16]{2,1,0:T(8,128)S(1)}, u32[]{:S(2)}, u32[]{:S(2)}) collective-permute-start(f32[5,8,16]{2,1,0:T(8,128)S(1)} %fusion.29), channel_id=1, source_target_pairs={{0,16},{16,0},{1,17},{17,1},{2,18},{18,2},{3,19},{19,3},{4,20},{20... | collective-permute-start | bytes 7688 | tf_op jit(solution)/shard_map/ppermute | solution.py:17
  7.8 1.8 %copy-start.10 = (s32[2]{0:T(128)S(1)}, s32[2]{0:T(128)}, u32[]{:S(2)}) copy-start(s32[2]{0:T(128)} %param.14) | copy-start | bytes 28
  7.9 19.5 %collective-permute-start.1 = (f32[5,1,16,256]{3,2,1,0:T(8,128)S(1)}, f32[5,1,16,256]{3,2,1,0:T(8,128)S(1)}, u32[]{:S(2)}, u32[]{:S(2)}) collective-permute-start(f32[5,1,16,256]{3,2,1,0:T(8,128)S(1)} %get-tuple-element.84), channel_id=1, source_target_pairs={{0,4},{4,8},{8,12},{12,0},{1,5},{5,9},{9,13},{13,1},{2,6},{6,10},{... | collective-permute-start | bytes 245768 | tf_op jit(solution)/shard_map/ppermute | solution.py:27
  7.9 19.4 %collective-permute-start.2 = (f32[5,1,16,256]{3,2,1,0:T(8,128)S(1)}, f32[5,1,16,256]{3,2,1,0:T(8,128)S(1)}, u32[]{:S(2)}, u32[]{:S(2)}) collective-permute-start(f32[5,1,16,256]{3,2,1,0:T(8,128)S(1)} %get-tuple-element.85), channel_id=1, source_target_pairs={{4,0},{8,4},{12,8},{0,12},{5,1},{9,5},{13,9},{1,13},{6,2},{10,6},{... | collective-permute-start | bytes 245768 | tf_op jit(solution)/shard_map/ppermute | solution.py:29
  12.0 0.7 copy-start.8
  21.7 0.7 copy-start.9
  28.0 5.4 %copy-start.7 = (f32[5]{0:T(128)S(1)}, f32[5]{0:T(128)}, u32[]{:S(2)}) copy-start(f32[5]{0:T(128)} %constant.89.clone) | copy-start | bytes 64
  28.0 5.4 %collective-permute-start.4 = (f32[5,10,1,256]{3,2,1,0:T(1,128)S(1)}, f32[5,10,1,256]{3,2,1,0:T(1,128)S(1)}, u32[]{:S(2)}, u32[]{:S(2)}) collective-permute-start(f32[5,10,1,256]{3,2,1,0:T(1,128)S(1)} %pad_maximum_fusion.50), channel_id=1, source_target_pairs={{1,0},{2,1},{3,2},{0,3},{5,4},{6,5},{7,6},{4,7},{9,8},{10,9},{11,1... | collective-permute-start | bytes 153608 | tf_op jit(solution)/shard_map/ppermute | solution.py:29
  33.6 6.3 %collective-permute-start.3 = (f32[5,10,1,256]{3,2,1,0:T(1,128)S(1)}, f32[5,10,1,256]{3,2,1,0:T(1,128)S(1)}, u32[]{:S(2)}, u32[]{:S(2)}) collective-permute-start(f32[5,10,1,256]{3,2,1,0:T(1,128)S(1)} %get-tuple-element.61), channel_id=1, source_target_pairs={{0,1},{1,2},{2,3},{3,0},{4,5},{5,6},{6,7},{7,4},{8,9},{9,10},{10,1... | collective-permute-start | bytes 153608 | tf_op jit(solution)/shard_map/ppermute | solution.py:27
  40.8 1.1 %copy-start.4 = (f32[5,8,16,256]{3,2,1,0:T(8,128)S(1)}, f32[5,8,16,256]{3,2,1,0:T(8,128)}, u32[]{:S(2)}) copy-start(f32[5,8,16,256]{3,2,1,0:T(8,128)} %constant_dynamic-update-slice_fusion.4) | copy-start | bytes 1966084
  42.7 1.1 %copy-start.2 = (f32[5,8,16,256]{3,2,1,0:T(8,128)S(1)}, f32[5,8,16,256]{3,2,1,0:T(8,128)}, u32[]{:S(2)}) copy-start(f32[5,8,16,256]{3,2,1,0:T(8,128)} %constant_dynamic-update-slice_fusion.19) | copy-start | bytes 1966084
  42.8 3.8 %collective-permute-start.5 = (f32[5,8,16]{2,1,0:T(8,128)S(1)}, f32[5,8,16]{2,1,0:T(8,128)S(1)}, u32[]{:S(2)}, u32[]{:S(2)}) collective-permute-start(f32[5,8,16]{2,1,0:T(8,128)S(1)} %fusion.28), channel_id=1, source_target_pairs={{0,16},{16,0},{1,17},{17,1},{2,18},{18,2},{3,19},{19,3},{4,20},{20... | collective-permute-start | bytes 7688 | tf_op jit(solution)/shard_map/ppermute | solution.py:17
  44.6 12.8 %collective-permute-start.6 = (f32[5,1,16,256]{3,2,1,0:T(8,128)S(1)}, f32[5,1,16,256]{3,2,1,0:T(8,128)S(1)}, u32[]{:S(2)}, u32[]{:S(2)}) collective-permute-start(f32[5,1,16,256]{3,2,1,0:T(8,128)S(1)} %get-tuple-element.78), channel_id=1, source_target_pairs={{0,4},{4,8},{8,12},{12,0},{1,5},{5,9},{9,13},{13,1},{2,6},{6,10},{... | collective-permute-start | bytes 245768 | tf_op jit(solution)/shard_map/ppermute | solution.py:27
  44.7 12.7 %collective-permute-start.7 = (f32[5,1,16,256]{3,2,1,0:T(8,128)S(1)}, f32[5,1,16,256]{3,2,1,0:T(8,128)S(1)}, u32[]{:S(2)}, u32[]{:S(2)}) collective-permute-start(f32[5,1,16,256]{3,2,1,0:T(8,128)S(1)} %get-tuple-element.79), channel_id=1, source_target_pairs={{4,0},{8,4},{12,8},{0,12},{5,1},{9,5},{13,9},{1,13},{6,2},{10,6},{... | collective-permute-start | bytes 245768 | tf_op jit(solution)/shard_map/ppermute | solution.py:29
  57.6 4.2 %collective-permute-start.9 = (f32[5,10,1,256]{3,2,1,0:T(1,128)S(1)}, f32[5,10,1,256]{3,2,1,0:T(1,128)S(1)}, u32[]{:S(2)}, u32[]{:S(2)}) collective-permute-start(f32[5,10,1,256]{3,2,1,0:T(1,128)S(1)} %pad_maximum_fusion.45), channel_id=1, source_target_pairs={{1,0},{2,1},{3,2},{0,3},{5,4},{6,5},{7,6},{4,7},{9,8},{10,9},{11,1... | collective-permute-start | bytes 153608 | tf_op jit(solution)/shard_map/ppermute | solution.py:29
  61.9 6.0 %collective-permute-start.8 = (f32[5,10,1,256]{3,2,1,0:T(1,128)S(1)}, f32[5,10,1,256]{3,2,1,0:T(1,128)S(1)}, u32[]{:S(2)}, u32[]{:S(2)}) collective-permute-start(f32[5,10,1,256]{3,2,1,0:T(1,128)S(1)} %get-tuple-element.32), channel_id=1, source_target_pairs={{0,1},{1,2},{2,3},{3,0},{4,5},{5,6},{6,7},{7,4},{8,9},{9,10},{10,1... | collective-permute-start | bytes 153608 | tf_op jit(solution)/shard_map/ppermute | solution.py:27
where the time goes:
time: 70.9 us; the launch traced here: 70.5 us
  other arithmetic  17.2 us (24%)
  waiting for transfers between devices  15 us (21%)
  starting transfers between devices  13.3 us (19%)
  local copies, waits for them, and re-layouts  10.6 us (15%)
  blocking collectives  10.5 us (15%)
  between operations  3.8 us (5%)
    ppermute x4, waiting for transfers between devices, extended(): lax.ppermute(tail, axis, [(i, (i + 1) % count) for i in range(count)])  11.3 us
    all_gather x2, blocking collectives, interface(): whole_cycle = lax.all_gather(partner, 'circ', axis=1, tiled=True)  10.5 us
    ppermute x4, starting transfers between devices, extended(): lax.ppermute(head, axis, [((i + 1) % count, i) for i in range(count)])  9.19 us
    unnamed x34, local copies, waits for them, and re-layouts  6.64 us
    select_n x2, other arithmetic, advance(): jnp.where(row_index == 0, jnp.broadcast_to(inlet, ghost_layer.shape), gho...  5.09 us
    ppermute x2, starting transfers between devices, from_partner(): return lax.ppermute(block, axis, route)  3.63 us
    ppermute x4, waiting for transfers between devices, extended(): lax.ppermute(head, axis, [((i + 1) % count, i) for i in range(count)])  3.53 us
    unnamed x39, other arithmetic  2.33 us
  transfers between devices with their start and end apart: 10, of which 5 were waited for; matrix products, arithmetic and copies ran while one was open for 22% of the time, Pallas kernels for 0%

commit v1 on v0

v1 whole, which is shorter than its diff:
```python
import functools

import jax
import jax.numpy as jnp
from jax import lax
from jax.experimental import pallas as pl
from jax.experimental.pallas import tpu as pltpu
from jax.sharding import PartitionSpec as P

GAMMA = 1.4
STEP = 0.04
INLET = (1.0, 0.5, 0.0, 0.0, 2.625)
LANES = 128
ROWS = 24


def vmem():
    return pl.BlockSpec(memory_space=pltpu.VMEM)


def smem():
    return pl.BlockSpec(memory_space=pltpu.SMEM)


def call(kernel, shapes, args, specs=None, scratch=(), aliases=None, cost=None):
    return pl.pallas_call(
        kernel,
        out_shape=[jax.ShapeDtypeStruct(s, jnp.float32) for s in shapes],
        in_specs=specs or [vmem()] * len(args),
        out_specs=[vmem()] * len(shapes),
        scratch_shapes=list(scratch),
        input_output_aliases=aliases or {},
        cost_estimate=cost,
    )(*args)


class Cell:
    def __init__(self, u):
        self.u = u
        rho, m0, m1, m2, en = u
        self.inv = 1.0 / rho
        kin = 0.5 * (m0 * m0 + m1 * m1 + m2 * m2) * self.inv
        self.p = (GAMMA - 1.0) * (en - kin)
        self.sound = jnp.sqrt(GAMMA * self.p * self.inv)

    def flux(self, d):
        m = self.u[1:4]
        vel = m[d] * self.inv
        f = [m[d], m[0] * vel, m[1] * vel, m[2] * vel, (self.u[4] + self.p) * vel]
        f[1 + d] = f[1 + d] + self.p
        return f, jnp.abs(vel) + self.sound


def face(ul, fl, sl, ur, fr, sr):
    top = jnp.maximum(sl, sr)
    return [a + b - top * (y - x) for x, a, y, b in zip(ul, fl, ur, fr)]


def updated(u, force, *spans):
    src = [None, u[0] * force[0], u[0] * force[1], u[0] * force[2]]
    src.append(u[1] * force[0] + u[2] * force[1] + u[3] * force[2])
    out = []
    for k in range(5):
        div = spans[0][0][k] - spans[0][1][k]
        for hi, lo in spans[1:]:
            div = div + (hi[k] - lo[k])
        new = u[k] - (0.5 * STEP) * div
        out.append(new if src[k] is None else new + STEP * src[k])
    return out


def conserved(rho, v, p):
    m = [rho * x for x in v]
    en = p / (GAMMA - 1.0) + 0.5 * rho * (v[0] * v[0] + v[1] * v[1] + v[2] * v[2])
    return [rho] + m + [en]


def inlet_flux():
    rho, m0, m1, m2, en = INLET
    p = (GAMMA - 1.0) * (en - 0.5 * (m0 * m0 + m1 * m1 + m2 * m2) / rho)
    vel = m0 / rho
    f = [m0, m0 * vel + p, m1 * vel, m2 * vel, (en + p) * vel]
    return f, abs(vel) + (GAMMA * p / rho) ** 0.5


def axial_faces(cell, slide, rotor):
    u = cell.u
    f, s = cell.flux(0)
    shape = u[0].shape
    lane = lax.broadcasted_iota(jnp.int32, shape, 1)
    last = shape[1] - 1
    first_lane = lane == 0
    last_lane = lane == last
    inf, ins = inlet_flux()

    def back(x, v):
        return jnp.where(first_lane, v, pltpu.roll(x, 1, 1))

    pu = [back(x, v) for x, v in zip(u, INLET)]
    pf = [pu[1]] + [back(x, v) for x, v in zip(f[1:], inf[1:])]
    lo = face(pu, pf, back(s, ins), u, f, s)
    stator_first = jnp.logical_and(first_lane, jnp.logical_not(rotor))
    lo = [jnp.where(stator_first, h, x) for h, x in zip(slide, lo)]
    hi = [
        jnp.where(last_lane, jnp.where(rotor, h, 2.0 * g), pltpu.roll(x, last, 1))
        for h, g, x in zip(slide, f, lo)
    ]
    return hi, lo


def wall_face(f, s, m, sign):
    zero = jnp.zeros_like(s)
    return [zero, zero, zero, 2.0 * (f[3] + sign * s * m), zero]


def place():
    row = lax.axis_index("row")
    circ = lax.axis_index("circ")
    span = lax.axis_index("span")
    return row, lax.rem(circ, 2) == 0, lax.rem(span, 2) == 0, span


def first_kernel(C, T, rho_ref, v_ref, p_ref, f_ref, u_ref, sa_ref, sb_ref, pa_ref, pb_ref):
    _, even_c, even_s, _ = place()
    for c in range(C):
        u = conserved(rho_ref[c], [v_ref[k, c] for k in range(3)], p_ref[c])
        for k in range(5):
            u_ref[k, c] = u[k]

    def row(k, s):
        ref = u_ref.at[k] if k < 5 else f_ref.at[k - 5]
        return ref[:, s, :]

    def send(slot, k, low, high):
        a, b = row(k, low), row(k, high)
        sa_ref[slot] = jnp.where(even_s, b, a)
        sb_ref[slot] = jnp.where(even_s, a, b)

    for k in range(5):
        send(k, k, 0, T - 1)
        send(5 + k, k, 1, T - 2)
    for k in range(3):
        send(10 + k, 5 + k, 0, T - 1)
    near = jnp.where(even_c, C - 1, 0)
    far = jnp.where(even_c, C - 2, 1)
    for ref, n, m in ((pa_ref, near, far), (pb_ref, C - 1 - near, C - 1 - far)):
        for k in range(5):
            ref[k] = u_ref[k, n]
            ref[5 + k] = u_ref[k, m]
        for k in range(3):
            ref[10 + k] = f_ref[k, n]


def thin_kernel(C, T, u_ref, f_ref, ha_ref, hb_ref, m1_ref, m2_ref, t_ref):
    row, even_c, even_s, _ = place()
    rotor = row == 0
    width = u_ref.shape[3]
    half = pl.ds(pl.multiple_of(jnp.where(rotor, width - LANES, 0), LANES), LANES)
    end = jnp.where(rotor, LANES - 1, 0)
    second = jnp.where(rotor, LANES - 2, 1)
    lane = lax.broadcasted_iota(jnp.int32, (C * T, LANES), 1)
    t = jnp.zeros((C * T, LANES), jnp.float32)

    def put(x, j, e):
        return pltpu.roll(x, lax.rem(j - e + LANES, LANES), 1)

    for k in range(5):
        x = u_ref[k, :, :, half].reshape(C * T, LANES)
        t = jnp.where(lane == k, put(x, k, end), t)
        t = jnp.where(lane == 5 + k, put(x, 5 + k, second), t)
    for k in range(3):
        t = jnp.where(lane == 10 + k, put(f_ref[k, :, :, half].reshape(C * T, LANES), 10 + k, end), t)
    t_ref[...] = t
    small = lax.broadcasted_iota(jnp.int32, (C, LANES), 1)
    for start, is_low in ((0, True), (T - 1, False)):
        where_a = even_s if not is_low else jnp.logical_not(even_s)
        rows = pl.ds(start, C, stride=T)
        x = t_ref[rows, :]
        for k in range(5):
            h = jnp.where(where_a, ha_ref[k, :, half], hb_ref[k, :, half])
            x = jnp.where(small == 13 + k, put(h, 13 + k, end), x)
        t_ref[rows, :] = x
    planes = t_ref[...].T[:ROWS]
    m1_ref[0:ROWS, :] = planes
    m2_ref[0:ROWS, :] = planes
    m2_ref[ROWS : 2 * ROWS, :] = jnp.zeros((ROWS, LANES), jnp.float32)

    def corner(ref, base, c):
        for k in range(5):
            for side in range(2):
                where_a = even_s if side == 1 else jnp.logical_not(even_s)
                x = jnp.where(where_a, ha_ref[k, pl.ds(c, 1), :], hb_ref[k, pl.ds(c, 1), :])
                for part in range(width // LANES):
                    r = base + 16 * part + 2 * k + side
                    ref[r : r + 1, :] = x[:, part * LANES : (part + 1) * LANES]
        for part in range(width // LANES):
            r = base + 16 * part
            ref[r + 10 : r + 16, :] = jnp.zeros((6, LANES), jnp.float32)

    near = jnp.where(even_c, C - 1, 0)
    corner(m1_ref, ROWS, near)
    corner(m2_ref, 2 * ROWS, C - 1 - near)


def fill_kernel(m1_ref, m2_ref, out_ref):
    out_ref[...] = m2_ref[...]
    out_ref[ROWS : 2 * ROWS, :] = m1_ref[0:ROWS, :]


def ring_kernel(m2_ref, got_ref, ring_ref):
    _, even, _, _ = place()
    mate = m2_ref[ROWS : 2 * ROWS, :]
    next_ = got_ref[0:ROWS, :]
    ring_ref[0] = m2_ref[0:ROWS, :]
    ring_ref[1] = jnp.where(even, mate, next_)
    ring_ref[2] = got_ref[ROWS : 2 * ROWS, :]
    ring_ref[3] = jnp.where(even, next_, mate)


def final_kernel(
    C, T, nc, ns,
    off_ref, wt_ref, u_ref, f_ref, ha_ref, hb_ref, pa_ref, pb_ref, m1_ref, m2_ref, own_ref, par_ref,
    out_ref, pf_ref,
    own_s, par_s, ht_s, ext_s, one_s, far_s, edge_s, rows_s,
):
    row, even_c, even_s, span = place()
    rotor = row == 0
    hub = span == 0
    casing = span == ns - 1
    width = u_ref.shape[3]
    periods = own_s.shape[0] // (nc * ROWS)
    depth = nc * periods
    sg = jnp.where(rotor, 1, -1)
    sgf = jnp.where(rotor, 1.0, -1.0)
    cycle = nc * C

    for copy in range(periods):
        own_s[copy * nc * ROWS : (copy + 1) * nc * ROWS, :] = own_ref[...]
        par_s[copy * nc * ROWS : (copy + 1) * nc * ROWS, :] = par_ref[...]
    shape = (depth, LANES)
    lane = lax.broadcasted_iota(jnp.int32, shape, 1)
    in_span = lax.rem(lane, T)

    def get(ref, j):
        return ref[pl.ds(j, depth, stride=ROWS), :]

    def ahead(x, k):
        if k == 0:
            return x
        a = pltpu.roll(x, (LANES - T * k) % LANES, 1)
        b = pltpu.roll(a, depth - 1, 0)
        return jnp.where(lane < LANES - T * k, a, b)

    def behind(x):
        a = pltpu.roll(x, T, 1)
        b = pltpu.roll(a, 1, 0)
        return jnp.where(lane >= T, a, b)

    def turned(x, cells):
        q = lax.div(cells, C)
        r = lax.rem(cells, C)
        y = pltpu.roll(x, lax.rem(depth - q, depth), 0)
        a = pltpu.roll(y, lax.rem(LANES - T * r, LANES), 1)
        b = pltpu.roll(a, depth - 1, 0)
        return jnp.where(lane < LANES - T * r, a, b)

    def taps(t):
        w = [jnp.full((1, LANES), wt_ref[t, k], jnp.float32) for k in range(4)]
        total = w[0] + w[1] + w[2] + w[3]
        return [x / total for x in w]

    def ghosts(xs, t, sign):
        w = taps(t)
        start = lax.rem(sign * off_ref[t] - 1 + 2 * cycle, cycle)
        out = []
        for x in xs:
            x = turned(x, start)
            g = w[0] * x
            for k in range(1, 4):
                g = g + w[k] * ahead(x, k)
            out.append(g)
        return out

    def slide(cell, ghost, sign):
        f, s = cell.flux(0)
        g = Cell(ghost)
        fg, s_g = g.flux(0)
        top = jnp.maximum(s, s_g) * sign
        return [a + b - top * (y - x) for x, a, y, b in zip(cell.u, f, ghost, fg)]

    def ring_step(ref, cell, h, sign):
        inner = Cell([get(ref, 5 + k) for k in range(5)])
        fi, si = inner.flux(0)
        f, s = cell.flux(0)
        top = jnp.maximum(s, si) * sign
        h1 = [a + b - top * (x - y) for x, a, y, b in zip(cell.u, f, inner.u, fi)]
        ax_hi = [sign * x for x in h]
        ax_lo = [sign * x for x in h1]
        f, s = cell.flux(1)
        lo = face([behind(x) for x in cell.u], [behind(x) for x in f], behind(s), cell.u, f, s)
        hi = [ahead(x, 1) for x in lo]
        f, s = cell.flux(2)
        edge = Cell([get(ref, 13 + k) for k in range(5)])
        fe, se = edge.flux(2)
        first = in_span == 0
        last = in_span == T - 1

        def prev(x, e):
            return jnp.where(first, e, pltpu.roll(x, 1, 1))

        slo = face([prev(x, e) for x, e in zip(cell.u, edge.u)], [prev(x, e) for x, e in zip(f, fe)], prev(s, se), cell.u, f, s)
        wall = wall_face(f, s, cell.u[3], -1.0)
        slo = [jnp.where(jnp.logical_and(first, hub), a, b) for a, b in zip(wall, slo)]
        top_face = face(cell.u, f, s, edge.u, fe, se)
        wall = wall_face(f, s, cell.u[3], 1.0)
        top_face = [jnp.where(casing, a, b) for a, b in zip(wall, top_face)]
        shi = [jnp.where(last, a, pltpu.roll(b, LANES - 1, 1)) for a, b in zip(top_face, slo)]
        force = [get(ref, 10 + k) for k in range(3)]
        return updated(cell.u, force, (ax_hi, ax_lo), (hi, lo), (shi, slo))

    own = Cell([get(own_s, k) for k in range(5)])
    par = Cell([get(par_s, k) for k in range(5)])
    g_own = ghosts(par.u, 0, sg)
    g_par = ghosts(own.u, 0, -sg)
    h_own = slide(own, g_own, sgf)
    h_par = slide(par, g_par, -sgf)
    g_edge = ghosts([get(par_s, 13 + k) for k in range(5)], 0, sg)
    h_edge = slide(Cell([get(own_s, 13 + k) for k in range(5)]), g_edge, sgf)
    own_new = ring_step(own_s, own, h_own, sgf)
    par_new = ring_step(par_s, par, h_par, -sgf)
    h_next = slide(Cell(own_new), ghosts(par_new, 1, sg), sgf)

    def eight(x):
        if depth == 8:
            return x
        return jnp.concatenate([x[0:7], x[depth - 1 : depth]], 0)

    tile = [eight(x) for x in h_own + h_edge + h_next]
    tile.append(jnp.zeros((8, LANES), jnp.float32))
    ht_s[...] = jnp.concatenate(tile, 0).T
    for t, h in ((0, h_own), (1, h_next)):
        for k in range(5):
            x = 0.5 * h[k][0:1, :]
            for c in range(C):
                pf_ref[t, k, c : c + 1, :] = x[:, c * T : (c + 1) * T]

    def left(slot, rows=slice(None)):
        return jnp.where(even_c, pb_ref[slot, rows, :], pa_ref[slot, rows, :])

    def right(slot, rows=slice(None)):
        return jnp.where(even_c, pa_ref[slot, rows, :], pb_ref[slot, rows, :])

    def low(slot):
        return jnp.where(even_s, hb_ref[slot], ha_ref[slot])

    def high(slot):
        return jnp.where(even_s, ha_ref[slot], hb_ref[slot])

    def corner(ref, base, k, side):
        parts = [ref[pl.ds(base + 16 * q + 2 * k + side, 1), :] for q in range(width // LANES)]
        return jnp.concatenate(parts, 1)

    def corners(k, side):
        a = corner(m1_ref, ROWS, k, side)
        b = corner(m2_ref, 2 * ROWS, k, side)
        return jnp.where(even_c, b, a), jnp.where(even_c, a, b)

    eight_rows = lax.broadcasted_iota(jnp.int32, (C, width), 0)

    def extend(mid, lf, rt):
        shape = (C, width)
        tail = jnp.where(eight_rows == 0, jnp.broadcast_to(rt, shape), jnp.broadcast_to(lf, shape))
        return jnp.concatenate([mid, tail], 0)

    def own_row(k, s):
        mid = u_ref[k, :, s, :]
        return extend(mid, left(k, pl.ds(s, 1)), right(k, pl.ds(s, 1)))

    for side in range(2):
        halo = low if side == 0 else high
        inner = Cell([own_row(k, 0 if side == 0 else T - 1) for k in range(5)])
        lf_rt = [corners(k, side) for k in range(5)]
        cell = Cell([extend(halo(k), *lf_rt[k]) for k in range(5)])
        outer = Cell([halo(5 + k) for k in range(5)])
        f, s = cell.flux(2)
        fi, si = inner.flux(2)
        fo, so = outer.flux(2)
        cut = lambda xs: [x[:C] for x in xs]
        if side == 0:
            near = face(cell.u, f, s, inner.u, fi, si)
            hi2, lo2 = near, face(outer.u, fo, so, cut(cell.u), cut(f), s[:C])
            wall = wall_face(fi, si, inner.u[3], -1.0)
            at_wall = hub
        else:
            near = face(inner.u, fi, si, cell.u, f, s)
            hi2, lo2 = face(cut(cell.u), cut(f), s[:C], outer.u, fo, so), near
            wall = wall_face(fi, si, inner.u[3], 1.0)
            at_wall = casing
        for k in range(5):
            edge_s[side, k] = jnp.where(at_wall, wall[k], near[k])
        f, s = cell.flux(1)
        back = lambda x: pltpu.roll(x, 1, 0)
        lo1 = face([back(x) for x in cell.u], [back(x) for x in f], back(s), cell.u, f, s)
        hi1 = [pltpu.roll(x, 2 * C - 1, 0) for x in lo1]
        mid = Cell(cut(cell.u))
        first = 0 if side == 0 else T - 1
        strip = ht_s[pl.ds(first, C, stride=T), :]
        hs = [strip[:, 40 + 8 * k : 41 + 8 * k] for k in range(5)]
        hi0, lo0 = axial_faces(mid, hs, rotor)
        force = [halo(10 + k) for k in range(3)]
        new = updated(mid.u, force, (hi0, lo0), (cut(hi1), cut(lo1)), (cut(hi2), cut(lo2)))
        for k in range(5):
            rows_s[side, k] = new[k]

    column = (T, width)
    srow = lax.broadcasted_iota(jnp.int32, column, 0)

    def column_update(cell, circ_lo, circ_hi, slide_h, edge_row, force):
        hi0, lo0 = axial_faces(cell, slide_h, rotor)
        f, s = cell.flux(2)
        back = lambda x: pltpu.roll(x, 1, 0)
        lo2 = face([back(x) for x in cell.u], [back(x) for x in f], back(s), cell.u, f, s)
        low_row = [edge_s[0, k, edge_row : edge_row + 1, :] for k in range(5)]
        top_row = [edge_s[1, k, edge_row : edge_row + 1, :] for k in range(5)]
        lo2 = [jnp.where(srow == 0, jnp.broadcast_to(e, column), x) for e, x in zip(low_row, lo2)]
        hi2 = [
            jnp.where(srow == T - 1, jnp.broadcast_to(e, column), pltpu.roll(x, T - 1, 0))
            for e, x in zip(top_row, lo2)
        ]
        return updated(cell.u, force, (hi0, lo0), (circ_hi, circ_lo), (hi2, lo2))

    def sweep(load, lo, hi, slide_of, force_of, store):
        prev = Cell(load(lo - 1))
        pf, ps = prev.flux(1)
        cell = Cell(load(lo))
        cf, cs = cell.flux(1)
        h_lo = face(prev.u, pf, ps, cell.u, cf, cs)
        for c in range(lo, hi):
            nxt = Cell(load(c + 1))
            nf, ns_ = nxt.flux(1)
            h_hi = face(cell.u, cf, cs, nxt.u, nf, ns_)
            edge_row = c if c >= 0 else 2 * C - 1
            store(c, column_update(cell, h_lo, h_hi, slide_of(c), edge_row, force_of(c)))
            cell, cf, cs, h_lo = nxt, nf, ns_, h_hi

    def load0(c):
        if c < 0:
            return [left(k + (5 if c == -2 else 0)) for k in range(5)]
        if c >= C:
            return [right(k + (5 if c == C + 1 else 0)) for k in range(5)]
        return [u_ref[k, c] for k in range(5)]

    def force0(c):
        if c < 0:
            return [left(10 + k) for k in range(3)]
        if c >= C:
            return [right(10 + k) for k in range(3)]
        return [f_ref[k, c] for k in range(3)]

    def slide0(c):
        sector = 0 if 0 <= c < C else (1 if c >= C else 7)
        r = (c % C) * T
        return [ht_s[r : r + T, 8 * k + sector : 8 * k + sector + 1] for k in range(5)]

    def store0(c, u):
        for k in range(5):
            one_s[k, c + 1] = u[k]

    sweep(load0, -1, C + 1, slide0, force0, store0)

    for side in range(2):
        s = 0 if side == 0 else T - 1
        inner = Cell([one_s[k, 1 : C + 1, s, :] for k in range(5)])
        outer = Cell([rows_s[side, k] for k in range(5)])
        fi, si = inner.flux(2)
        fo, so = outer.flux(2)
        if side == 0:
            near = face(outer.u, fo, so, inner.u, fi, si)
            wall, at_wall = wall_face(fi, si, inner.u[3], -1.0), hub
        else:
            near = face(inner.u, fi, si, outer.u, fo, so)
            wall, at_wall = wall_face(fi, si, inner.u[3], 1.0), casing
        for k in range(5):
            edge_s[side, k, 0:C, :] = jnp.where(at_wall, wall[k], near[k])

    def load1(c):
        return [one_s[k, c + 1] for k in range(5)]

    def slide1(c):
        return [ht_s[c * T : (c + 1) * T, 80 + 8 * k : 81 + 8 * k] for k in range(5)]

    def store1(c, u):
        for k in range(5):
            out_ref[k, c] = u[k]

    sweep(load1, 0, C, slide1, force0, store1)


def pairs(count, first, wrap):
    route = []
    for low in range(first, count, 2):
        high = low + 1
        if high < count or wrap:
            route += [(low, high % count), (high % count, low)]
    return route


def body(density, velocity, pressure, blade_force, offsets, weights):
    C, T, A = density.shape[1:]
    nc = lax.axis_size("circ")
    ns = lax.axis_size("span")
    area = C * T
    assert area == LANES and nc % 2 == 0 and A % LANES == 0 and C == 8
    rho, v, p, force = density[0], velocity[0], pressure[0], blade_force[0]

    u, sa, sb, pa, pb = call(
        functools.partial(first_kernel, C, T),
        [(5, C, T, A), (13, C, A), (13, C, A), (13, T, A), (13, T, A)],
        (rho, v, p, force),
    )
    ha = lax.ppermute(sa, "span", pairs(ns, 0, False))
    hb = lax.ppermute(sb, "span", pairs(ns, 1, False))
    pa = lax.ppermute(pa, "circ", pairs(nc, 0, True))
    pb = lax.ppermute(pb, "circ", pairs(nc, 1, True))

    thin = 2 * 16 * (A // LANES) // 2
    m1, m2 = call(
        functools.partial(thin_kernel, C, T),
        [(ROWS + thin, LANES), (2 * ROWS + thin, LANES)],
        (u, force, ha, hb),
        scratch=[pltpu.VMEM((area, LANES), jnp.float32)],
    )
    planes = m1[:ROWS]
    m1 = lax.ppermute(m1, "circ", pairs(nc, 0, True))
    if nc == 4:
        (m2,) = call(fill_kernel, [m2.shape], (m1, m2), aliases={1: 0})
        got = lax.ppermute(m2, "circ", pairs(nc, 1, True))
        (ring,) = call(ring_kernel, [(nc, ROWS, LANES)], (m2, got))
    else:
        got = lax.ppermute(m2, "circ", pairs(nc, 1, True))
        whole = lax.all_gather(planes, "circ")
        whole = jnp.concatenate([whole, whole], 0)
        ring = lax.dynamic_slice_in_dim(whole, lax.axis_index("circ"), nc, 0)
    partner = lax.ppermute(ring, "row", [(0, 1), (1, 0)])
    copies = max(1, 8 // nc)
    rows = nc * ROWS
    state, plane_flux = call(
        functools.partial(final_kernel, C, T, nc, ns),
        [(5, C, T, A), (2, 5, C, T)],
        (offsets, weights, u, force, ha, hb, pa, pb, m1, got, ring.reshape(rows, LANES), partner.reshape(rows, LANES)),
        specs=[smem(), smem()] + [vmem()] * 10,
        scratch=[
            pltpu.VMEM((copies * rows, LANES), jnp.float32),
            pltpu.VMEM((copies * rows, LANES), jnp.float32),
            pltpu.VMEM((LANES, LANES), jnp.float32),
            pltpu.VMEM((8, LANES), jnp.float32),
            pltpu.VMEM((5, C + 2, T, A), jnp.float32),
            pltpu.VMEM((8, LANES), jnp.float32),
            pltpu.VMEM((2, 5, 2 * C, A), jnp.float32),
            pltpu.VMEM((2, 5, C, A), jnp.float32),
        ],
    )
    return state[None], plane_flux[None]


def solution(mesh):
    placed = (
        P("row", "circ", "span", None),
        P("row", None, "circ", "span", None),
        P("row", "circ", "span", None),
        P("row", None, "circ", "span", None),
        P(),
        P(),
    )
    return jax.shard_map(
        body,
        mesh=mesh,
        in_specs=placed,
        out_specs=(P("row", None, "circ", "span", None), P("row", None, None, "circ", "span")),
        check_vma=False,
    )
```

time: 70.9 us -> 34.8 us (0.49)
  the two profiles are of different devices: /device:TPU:0 before, /device:TPU:16 now
where the time goes in v1:
time: 34.8 us; the launch traced here: 34.5 us
  Pallas kernels  13.6 us (39%)
  waiting for transfers between devices  9.85 us (28%)
  starting transfers between devices  7.93 us (23%)
  local copies, waits for them, and re-layouts  2.46 us (7%)
  between operations  0.67 us (2%)
    pallas_call x5, Pallas kernels, call(): pl.pallas_call(kernel, out_shape=[jax.ShapeDtypeStruct(s, jnp.float32) fo...  13.6 us
    ppermute x1, waiting for transfers between devices, body(): hb = lax.ppermute(sb, 'span', pairs(ns, 1, False))  3.2 us
    ppermute x1, waiting for transfers between devices, body(): partner = lax.ppermute(ring, 'row', [(0, 1), (1, 0)])  2.76 us
    ppermute x1, waiting for transfers between devices, body(): got = lax.ppermute(m2, 'circ', pairs(nc, 1, True))  2.47 us
    unnamed x14, local copies, waits for them, and re-layouts  2.46 us
    ppermute x1, starting transfers between devices, body(): hb = lax.ppermute(sb, 'span', pairs(ns, 1, False))  1.91 us
    ppermute x1, starting transfers between devices, body(): pb = lax.ppermute(pb, 'circ', pairs(nc, 1, True))  1.59 us
    ppermute x1, starting transfers between devices, body(): ha = lax.ppermute(sa, 'span', pairs(ns, 0, False))  1.58 us
  transfers between devices with their start and end apart: 7, of which 4 were waited for; matrix products, arithmetic and copies ran while one was open for 0% of the time, Pallas kernels for 15%

profile of v1, /device:TPU:16, one launch (start us, length us, event | category | flops | bytes accessed | tf_op | source)
XLA Modules:
  0.0 34.5 jit_solution(1339765126812727974)
XLA Ops:
  0.6 2.4 %shard_map.77 = (f32[5,8,16,256]{3,2,1,0:T(8,128)}, f32[13,8,256]{2,1,0:T(8,128)}, f32[13,8,256]{2,1,0:T(8,128)}, f32[13,16,256]{2,1,0:T(8,128)}, f32[13,16,256]{2,1,0:T(8,128)}) custom-call(f32[8,16,256]{2,1,0:T(8,128)} %bitcast.13, f32[3,8,16,256]{3,2,1,0:T(8,128)} %bitcast.11, f32[8,16,256]{2,1,0:T(8,128)} %bitcast.14, f32[3,8,16,256]{3,2,1,0:T(8,128)} %bitcast.8), custom_call_target="tpu_custom_call" | custom-call | tf_op jit(solution)/shard_map/pallas_call | solution.py:26
  3.0 1.6 %collective-permute-start = (f32[13,8,256]{2,1,0:T(8,128)}, f32[13,8,256]{2,1,0:T(8,128)S(1)}, u32[]{:S(2)}, u32[]{:S(2)}) collective-permute-start(f32[13,8,256]{2,1,0:T(8,128)} %get-tuple-element.12), channel_id=1, source_target_pairs={{0,1},{1,0},{2,3},{3,2},{4,5},{5,4},{6,7},{7,6},{8,9},{9,8},{10,11... | collective-permute-start | bytes 319496 | tf_op jit(solution)/shard_map/ppermute | solution.py:521
  4.6 1.9 %collective-permute-start.1 = (f32[13,8,256]{2,1,0:T(8,128)}, f32[13,8,256]{2,1,0:T(8,128)S(1)}, u32[]{:S(2)}, u32[]{:S(2)}) collective-permute-start(f32[13,8,256]{2,1,0:T(8,128)} %get-tuple-element.13), channel_id=1, source_target_pairs={{1,2},{2,1},{5,6},{6,5},{9,10},{10,9},{13,14},{14,13},{17,18},{18,... | collective-permute-start | bytes 319496 | tf_op jit(solution)/shard_map/ppermute | solution.py:522
  6.5 0.1 collective-permute-start.2
  6.6 1.6 %collective-permute-start.3 = (f32[13,16,256]{2,1,0:T(8,128)}, f32[13,16,256]{2,1,0:T(8,128)S(1)}, u32[]{:S(2)}, u32[]{:S(2)}) collective-permute-start(f32[13,16,256]{2,1,0:T(8,128)} %get-tuple-element.15), channel_id=1, source_target_pairs={{4,8},{8,4},{12,0},{0,12},{5,9},{9,5},{13,1},{1,13},{6,10},{10,6},... | collective-permute-start | bytes 638984 | tf_op jit(solution)/shard_map/ppermute | solution.py:524
  8.2 0.0 collective-permute-done.ha_ref
  8.2 0.0 copy-start
  8.2 3.2 %collective-permute-done.1.hb_ref = f32[13,8,256]{2,1,0:T(8,128)S(1)} collective-permute-done((f32[13,8,256]{2,1,0:T(8,128)}, f32[13,8,256]{2,1,0:T(8,128)S(1)}, u32[]{:S(2)}, u32[]{:S(2)}) %collective-permute-start.1) | collective-permute-done | bytes 106528 | tf_op jit(solution)/shard_map/ppermute | solution.py:522
  11.4 0.0 copy-done
  11.4 0.6 %copy-done.1 = f32[13,8,256]{2,1,0:T(8,128)} copy-done((f32[13,8,256]{2,1,0:T(8,128)}, f32[13,8,256]{2,1,0:T(8,128)S(1)}, u32[]{:S(2)}) %copy-start.1) | copy-done | bytes 106520
  12.0 2.3 %shard_map.78 = (f32[56,128]{1,0:T(8,128)}, f32[80,128]{1,0:T(8,128)}) custom-call(f32[5,8,16,256]{3,2,1,0:T(8,128)} %get-tuple-element.11.u_ref, f32[3,8,16,256]{3,2,1,0:T(8,128)} %bitcast.9, f32[13,8,256]{2,1,0:T(8,128)} %copy-done, f32[13,8,256]{2,1,0:T(8,128)} %copy-done.1), custom_call_target="tpu_custom_call" | custom-call | tf_op jit(solution)/shard_map/pallas_call | solution.py:26
  14.3 0.0 collective-permute-start.4
  14.3 1.4 %collective-permute-done.4.m1_ref = f32[56,128]{1,0:T(8,128)S(1)} collective-permute-done((f32[56,128]{1,0:T(8,128)}, f32[56,128]{1,0:T(8,128)S(1)}, u32[]{:S(2)}, u32[]{:S(2)}) %collective-permute-start.4) | collective-permute-done | bytes 28704 | tf_op jit(solution)/shard_map/ppermute | solution.py:534
  15.7 0.0 copy-start.5
  15.7 0.6 %copy-done.5 = f32[56,128]{1,0:T(8,128)} copy-done((f32[56,128]{1,0:T(8,128)}, f32[56,128]{1,0:T(8,128)S(1)}, u32[]{:S(2)}) %copy-start.5) | copy-done | bytes 28696
  16.3 1.4 %shard_map.79.m2_ref = f32[80,128]{1,0:T(8,128)} custom-call(f32[56,128]{1,0:T(8,128)} %copy-done.5, f32[80,128]{1,0:T(8,128)} %get-tuple-element.17.m2_ref), custom_call_target="tpu_custom_call", output_to_operand_aliasing={{}: (1, {})} | custom-call | tf_op jit(solution)/shard_map/pallas_call | solution.py:26
  17.7 1.3 %collective-permute-start.5 = (f32[80,128]{1,0:T(8,128)}, f32[80,128]{1,0:T(8,128)S(1)}, u32[]{:S(2)}, u32[]{:S(2)}) collective-permute-start(f32[80,128]{1,0:T(8,128)} %shard_map.79.m2_ref), channel_id=1, source_target_pairs={{4,8},{8,4},{12,0},{0,12},{5,9},{9,5},{13,1},{1,13},{6,10},{10,6},... | collective-permute-start | bytes 122888 | tf_op jit(solution)/shard_map/ppermute | solution.py:537
  19.0 2.5 %collective-permute-done.5.got_ref.m2_ref = f32[80,128]{1,0:T(8,128)S(1)} collective-permute-done((f32[80,128]{1,0:T(8,128)}, f32[80,128]{1,0:T(8,128)S(1)}, u32[]{:S(2)}, u32[]{:S(2)}) %collective-permute-start.5) | collective-permute-done | bytes 40992 | tf_op jit(solution)/shard_map/ppermute | solution.py:537
  21.4 0.0 copy-start.4
  21.4 0.6 %copy-done.4 = f32[80,128]{1,0:T(8,128)} copy-done((f32[80,128]{1,0:T(8,128)}, f32[80,128]{1,0:T(8,128)S(1)}, u32[]{:S(2)}) %copy-start.4) | copy-done | bytes 40984
  22.0 1.4 %shard_map.80 = f32[4,24,128]{2,1,0:T(8,128)} custom-call(f32[80,128]{1,0:T(8,128)} %shard_map.79.m2_ref, f32[80,128]{1,0:T(8,128)} %copy-done.4), custom_call_target="tpu_custom_call" | custom-call | tf_op jit(solution)/shard_map/pallas_call | solution.py:26
  23.5 1.5 %collective-permute-start.6 = (f32[4,24,128]{2,1,0:T(8,128)}, f32[4,24,128]{2,1,0:T(8,128)S(1)}, u32[]{:S(2)}, u32[]{:S(2)}) collective-permute-start(f32[4,24,128]{2,1,0:T(8,128)} %shard_map.80), channel_id=1, source_target_pairs={{0,16},{16,0},{1,17},{17,1},{2,18},{18,2},{3,19},{19,3},{4,20},{20... | collective-permute-start | bytes 147464 | tf_op jit(solution)/shard_map/ppermute | solution.py:544
  25.0 0.0 collective-permute-done.2.pa_ref
  25.0 0.0 copy-start.2
  25.0 0.0 collective-permute-done.3.pb_ref
  25.0 0.0 copy-start.3
  25.0 2.8 %collective-permute-done.6 = f32[4,24,128]{2,1,0:T(8,128)S(1)} collective-permute-done((f32[4,24,128]{2,1,0:T(8,128)}, f32[4,24,128]{2,1,0:T(8,128)S(1)}, u32[]{:S(2)}, u32[]{:S(2)}) %collective-permute-start.6) | collective-permute-done | bytes 49184 | tf_op jit(solution)/shard_map/ppermute | solution.py:544
  27.8 0.0 copy-start.6
  27.8 0.0 copy-done.2
  27.8 0.0 copy-done.3
  27.8 0.6 %copy-done.6 = f32[4,24,128]{2,1,0:T(8,128)} copy-done((f32[4,24,128]{2,1,0:T(8,128)}, f32[4,24,128]{2,1,0:T(8,128)S(1)}, u32[]{:S(2)}) %copy-start.6) | copy-done | bytes 49176
  28.4 6.1 %shard_map.81 = (f32[5,8,16,256]{3,2,1,0:T(8,128)}, f32[2,5,8,16]{3,2,1,0:T(8,128)}) custom-call(s32[2]{0:T(128)} %off_ref.1, f32[2,4]{1,0:T(2,128)} %wt_ref.1, f32[5,8,16,256]{3,2,1,0:T(8,128)} %get-tuple-element.11.u_ref, f32[3,8,16,256]{3,2,1,0:T(8,128)} %bitcast.10, f32[13,8,256]{2,1,0:T(8,128)} %copy-done, f32[13,8,256]{2,1,0:T(8,128)} %copy-done.1, ...), custom_call_target="tpu_custom_call" | custom-call | tf_op jit(solution)/shard_map/pallas_call | solution.py:26
  (1 shorter events, 0.0 us)
Async XLA Ops:
  3.0 5.2 %collective-permute-start = (f32[13,8,256]{2,1,0:T(8,128)}, f32[13,8,256]{2,1,0:T(8,128)S(1)}, u32[]{:S(2)}, u32[]{:S(2)}) collective-permute-start(f32[13,8,256]{2,1,0:T(8,128)} %get-tuple-element.12), channel_id=1, source_target_pairs={{0,1},{1,0},{2,3},{3,2},{4,5},{5,4},{6,7},{7,6},{8,9},{9,8},{10,11... | collective-permute-start | bytes 319496 | tf_op jit(solution)/shard_map/ppermute | solution.py:521
  4.6 6.8 %collective-permute-start.1 = (f32[13,8,256]{2,1,0:T(8,128)}, f32[13,8,256]{2,1,0:T(8,128)S(1)}, u32[]{:S(2)}, u32[]{:S(2)}) collective-permute-start(f32[13,8,256]{2,1,0:T(8,128)} %get-tuple-element.13), channel_id=1, source_target_pairs={{1,2},{2,1},{5,6},{6,5},{9,10},{10,9},{13,14},{14,13},{17,18},{18,... | collective-permute-start | bytes 319496 | tf_op jit(solution)/shard_map/ppermute | solution.py:522
  6.5 18.5 %collective-permute-start.2 = (f32[13,16,256]{2,1,0:T(8,128)}, f32[13,16,256]{2,1,0:T(8,128)S(1)}, u32[]{:S(2)}, u32[]{:S(2)}) collective-permute-start(f32[13,16,256]{2,1,0:T(8,128)} %get-tuple-element.14), channel_id=1, source_target_pairs={{0,4},{4,0},{8,12},{12,8},{1,5},{5,1},{9,13},{13,9},{2,6},{6,2},{1... | collective-permute-start | bytes 638984 | tf_op jit(solution)/shard_map/ppermute | solution.py:523
  6.6 18.4 %collective-permute-start.3 = (f32[13,16,256]{2,1,0:T(8,128)}, f32[13,16,256]{2,1,0:T(8,128)S(1)}, u32[]{:S(2)}, u32[]{:S(2)}) collective-permute-start(f32[13,16,256]{2,1,0:T(8,128)} %get-tuple-element.15), channel_id=1, source_target_pairs={{4,8},{8,4},{12,0},{0,12},{5,9},{9,5},{13,1},{1,13},{6,10},{10,6},... | collective-permute-start | bytes 638984 | tf_op jit(solution)/shard_map/ppermute | solution.py:524
  8.2 3.2 %copy-start = (f32[13,8,256]{2,1,0:T(8,128)}, f32[13,8,256]{2,1,0:T(8,128)S(1)}, u32[]{:S(2)}) copy-start(f32[13,8,256]{2,1,0:T(8,128)S(1)} %collective-permute-done.ha_ref) | copy-start | bytes 319492
  11.4 0.6 %copy-start.1 = (f32[13,8,256]{2,1,0:T(8,128)}, f32[13,8,256]{2,1,0:T(8,128)S(1)}, u32[]{:S(2)}) copy-start(f32[13,8,256]{2,1,0:T(8,128)S(1)} %collective-permute-done.1.hb_ref) | copy-start | bytes 319492
  14.3 1.4 %collective-permute-start.4 = (f32[56,128]{1,0:T(8,128)}, f32[56,128]{1,0:T(8,128)S(1)}, u32[]{:S(2)}, u32[]{:S(2)}) collective-permute-start(f32[56,128]{1,0:T(8,128)} %get-tuple-element.16), channel_id=1, source_target_pairs={{0,4},{4,0},{8,12},{12,8},{1,5},{5,1},{9,13},{13,9},{2,6},{6,2},{1... | collective-permute-start | bytes 86024 | tf_op jit(solution)/shard_map/ppermute | solution.py:534
  15.7 0.6 %copy-start.5 = (f32[56,128]{1,0:T(8,128)}, f32[56,128]{1,0:T(8,128)S(1)}, u32[]{:S(2)}) copy-start(f32[56,128]{1,0:T(8,128)S(1)} %collective-permute-done.4.m1_ref) | copy-start | bytes 86020
  17.7 3.7 %collective-permute-start.5 = (f32[80,128]{1,0:T(8,128)}, f32[80,128]{1,0:T(8,128)S(1)}, u32[]{:S(2)}, u32[]{:S(2)}) collective-permute-start(f32[80,128]{1,0:T(8,128)} %shard_map.79.m2_ref), channel_id=1, source_target_pairs={{4,8},{8,4},{12,0},{0,12},{5,9},{9,5},{13,1},{1,13},{6,10},{10,6},... | collective-permute-start | bytes 122888 | tf_op jit(solution)/shard_map/ppermute | solution.py:537
  21.4 0.6 %copy-start.4 = (f32[80,128]{1,0:T(8,128)}, f32[80,128]{1,0:T(8,128)S(1)}, u32[]{:S(2)}) copy-start(f32[80,128]{1,0:T(8,128)S(1)} %collective-permute-done.5.got_ref.m2_ref) | copy-start | bytes 122884
  23.5 4.3 %collective-permute-start.6 = (f32[4,24,128]{2,1,0:T(8,128)}, f32[4,24,128]{2,1,0:T(8,128)S(1)}, u32[]{:S(2)}, u32[]{:S(2)}) collective-permute-start(f32[4,24,128]{2,1,0:T(8,128)} %shard_map.80), channel_id=1, source_target_pairs={{0,16},{16,0},{1,17},{17,1},{2,18},{18,2},{3,19},{19,3},{4,20},{20... | collective-permute-start | bytes 147464 | tf_op jit(solution)/shard_map/ppermute | solution.py:544
  25.0 2.8 %copy-start.2 = (f32[13,16,256]{2,1,0:T(8,128)}, f32[13,16,256]{2,1,0:T(8,128)S(1)}, u32[]{:S(2)}) copy-start(f32[13,16,256]{2,1,0:T(8,128)S(1)} %collective-permute-done.2.pa_ref) | copy-start | bytes 638980
  25.0 2.8 %copy-start.3 = (f32[13,16,256]{2,1,0:T(8,128)}, f32[13,16,256]{2,1,0:T(8,128)S(1)}, u32[]{:S(2)}) copy-start(f32[13,16,256]{2,1,0:T(8,128)S(1)} %collective-permute-done.3.pb_ref) | copy-start | bytes 638980
  27.8 0.6 %copy-start.6 = (f32[4,24,128]{2,1,0:T(8,128)}, f32[4,24,128]{2,1,0:T(8,128)S(1)}, u32[]{:S(2)}) copy-start(f32[4,24,128]{2,1,0:T(8,128)S(1)} %collective-permute-done.6) | copy-start | bytes 147460

commit v2 on v1

--- a/solution.py
+++ b/solution.py
@@ -22,15 +22,20 @@
     return pl.BlockSpec(memory_space=pltpu.SMEM)
 
 
-def call(kernel, shapes, args, specs=None, scratch=(), aliases=None, cost=None):
+def hbm():
+    return pl.BlockSpec(memory_space=pltpu.HBM)
+
+
+def call(kernel, shapes, args, specs=None, scratch=(), aliases=None, cost=None, limit=6):
     return pl.pallas_call(
         kernel,
-        out_shape=[jax.ShapeDtypeStruct(s, jnp.float32) for s in shapes],
+        out_shape=[jax.ShapeDtypeStruct(s.shape, s.dtype) if hasattr(s, "dtype") else jax.ShapeDtypeStruct(s, jnp.float32) for s in shapes],
         in_specs=specs or [vmem()] * len(args),
         out_specs=[vmem()] * len(shapes),
         scratch_shapes=list(scratch),
         input_output_aliases=aliases or {},
         cost_estimate=cost,
+        compiler_params=pltpu.CompilerParams(vmem_limit_bytes=limit << 20),
     )(*args)
 
 
@@ -120,8 +125,23 @@
     return row, lax.rem(circ, 2) == 0, lax.rem(span, 2) == 0, span
 
 
-def first_kernel(C, T, rho_ref, v_ref, p_ref, f_ref, u_ref, sa_ref, sb_ref, pa_ref, pb_ref):
+def first_kernel(
+    C, T,
+    rho_hbm, v_hbm, p_hbm, f_hbm, off_hbm, wt_hbm,
+    u_ref, f_ref, off_ref, wt_ref, sa_ref, sb_ref, pa_ref, pb_ref,
+    rho_ref, v_ref, p_ref, sem,
+):
+    copies = [
+        pltpu.make_async_copy(src, dst, sem.at[i])
+        for i, (src, dst) in enumerate(
+            [(rho_hbm, rho_ref), (v_hbm, v_ref), (p_hbm, p_ref), (f_hbm, f_ref), (off_hbm, off_ref), (wt_hbm, wt_ref)]
+        )
+    ]
+    for copy in copies:
+        copy.start()
     _, even_c, even_s, _ = place()
+    for copy in copies:
+        copy.wait()
     for c in range(C):
         u = conserved(rho_ref[c], [v_ref[k, c] for k in range(3)], p_ref[c])
         for k in range(5):
@@ -513,10 +533,17 @@
     assert area == LANES and nc % 2 == 0 and A % LANES == 0 and C == 8
     rho, v, p, force = density[0], velocity[0], pressure[0], blade_force[0]
 
-    u, sa, sb, pa, pb = call(
+    u, force, off, wt, sa, sb, pa, pb = call(
         functools.partial(first_kernel, C, T),
-        [(5, C, T, A), (13, C, A), (13, C, A), (13, T, A), (13, T, A)],
-        (rho, v, p, force),
+        [(5, C, T, A), (3, C, T, A), offsets, weights, (13, C, A), (13, C, A), (13, T, A), (13, T, A)],
+        [pltpu.with_memory_space_constraint(x, pltpu.HBM) for x in (rho, v, p, force, offsets, weights)],
+        specs=[hbm()] * 6,
+        scratch=[
+            pltpu.VMEM((C, T, A), jnp.float32),
+            pltpu.VMEM((3, C, T, A), jnp.float32),
+            pltpu.VMEM((C, T, A), jnp.float32),
+            pltpu.SemaphoreType.DMA((6,)),
+        ],
     )
     ha = lax.ppermute(sa, "span", pairs(ns, 0, False))
     hb = lax.ppermute(sb, "span", pairs(ns, 1, False))
@@ -547,8 +574,9 @@
     state, plane_flux = call(
         functools.partial(final_kernel, C, T, nc, ns),
         [(5, C, T, A), (2, 5, C, T)],
-        (offsets, weights, u, force, ha, hb, pa, pb, m1, got, ring.reshape(rows, LANES), partner.reshape(rows, LANES)),
+        (off, wt, u, force, ha, hb, pa, pb, m1, got, ring.reshape(rows, LANES), partner.reshape(rows, LANES)),
         specs=[smem(), smem()] + [vmem()] * 10,
+        limit=16,
         scratch=[
             pltpu.VMEM((copies * rows, LANES), jnp.float32),
             pltpu.VMEM((copies * rows, LANES), jnp.float32),

time: 34.8 us -> 25 us (0.72)
  Pallas kernels: 13.6 us -> 7.11 us
  local copies, waits for them, and re-layouts: 2.46 us -> 0 us
  waiting for transfers between devices: 9.85 us -> 9.02 us
    pallas_call x5, Pallas kernels: 13.6 us -> 7.11 us  [call(): pl.pallas_call(kernel, out_shape=[jax.ShapeDtypeStruct(s.shape, s.dtype)...]
    unnamed x14 -> x0, local copies, waits for them, and re-layouts: 2.46 us -> none
  transfers between devices with their start and end apart: 7 -> 7, of which waited for: 4 -> 4; matrix products, arithmetic and copies ran while one was open for 0% -> 0% of each run, Pallas kernels for 15% -> 1%
where the time goes in v2:
time: 25 us; the launch traced here: 24.8 us
  waiting for transfers between devices  9.02 us (36%)
  starting transfers between devices  8.04 us (32%)
  Pallas kernels  7.11 us (28%)
  between operations  0.67 us (3%)
    pallas_call x5, Pallas kernels, call(): pl.pallas_call(kernel, out_shape=[jax.ShapeDtypeStruct(s.shape, s.dtype)...  7.11 us
    ppermute x1, waiting for transfers between devices, body(): hb = lax.ppermute(sb, 'span', pairs(ns, 1, False))  2.99 us
    ppermute x1, waiting for transfers between devices, body(): partner = lax.ppermute(ring, 'row', [(0, 1), (1, 0)])  2.56 us
    ppermute x1, waiting for transfers between devices, body(): got = lax.ppermute(m2, 'circ', pairs(nc, 1, True))  2.26 us
    ppermute x1, starting transfers between devices, body(): hb = lax.ppermute(sb, 'span', pairs(ns, 1, False))  1.91 us
    ppermute x1, starting transfers between devices, body(): ha = lax.ppermute(sa, 'span', pairs(ns, 0, False))  1.64 us
    ppermute x1, starting transfers between devices, body(): pb = lax.ppermute(pb, 'circ', pairs(nc, 1, True))  1.59 us
    ppermute x1, starting transfers between devices, body(): partner = lax.ppermute(ring, 'row', [(0, 1), (1, 0)])  1.52 us
  transfers between devices with their start and end apart: 7, of which 4 were waited for; matrix products, arithmetic and copies ran while one was open for 0% of the time, Pallas kernels for 1%

profile of v2, /device:TPU:16, one launch (start us, length us, event | category | flops | bytes accessed | tf_op | source)
XLA Modules:
  0.0 24.8 jit_solution(9695507290799137388)
XLA Ops:
  0.6 1.4 %shard_map.77 = (f32[5,8,16,256]{3,2,1,0:T(8,128)S(1)}, f32[3,8,16,256]{3,2,1,0:T(8,128)S(1)}, s32[2]{0:T(128)S(1)}, f32[2,4]{1,0:T(2,128)S(1)}, f32[13,8,256]{2...) custom-call(f32[8,16,256]{2,1,0:T(8,128)} %bitcast.12, ...), custom_call_target="tpu_custom_call" | custom-call | tf_op jit(solution)/shard_map/pallas_call | solution.py:30
  2.1 1.6 %collective-permute-start = (f32[13,8,256]{2,1,0:T(8,128)S(1)}, f32[13,8,256]{2,1,0:T(8,128)S(1)}, u32[]{:S(2)}, u32[]{:S(2)}) collective-permute-start(f32[13,8,256]{2,1,0:T(8,128)S(1)} %get-tuple-element.18), channel_id=1, source_target_pairs={{0,1},{1,0},{2,3},{3,2},{4,5},{5,4},{6,7},{7,6},{8,9},{9,8},{10,11... | collective-permute-start | bytes 319496 | tf_op jit(solution)/shard_map/ppermute | solution.py:548
  3.7 1.9 %collective-permute-start.1 = (f32[13,8,256]{2,1,0:T(8,128)S(1)}, f32[13,8,256]{2,1,0:T(8,128)S(1)}, u32[]{:S(2)}, u32[]{:S(2)}) collective-permute-start(f32[13,8,256]{2,1,0:T(8,128)S(1)} %get-tuple-element.19), channel_id=1, source_target_pairs={{1,2},{2,1},{5,6},{6,5},{9,10},{10,9},{13,14},{14,13},{17,18},{18,... | collective-permute-start | bytes 319496 | tf_op jit(solution)/shard_map/ppermute | solution.py:549
  5.6 0.1 collective-permute-start.2
  5.7 1.6 %collective-permute-start.3 = (f32[13,16,256]{2,1,0:T(8,128)S(1)}, f32[13,16,256]{2,1,0:T(8,128)S(1)}, u32[]{:S(2)}, u32[]{:S(2)}) collective-permute-start(f32[13,16,256]{2,1,0:T(8,128)S(1)} %get-tuple-element.21), channel_id=1, source_target_pairs={{4,8},{8,4},{12,0},{0,12},{5,9},{9,5},{13,1},{1,13},{6,10},{10,6},... | collective-permute-start | bytes 638984 | tf_op jit(solution)/shard_map/ppermute | solution.py:551
  7.3 0.0 collective-permute-done.ha_ref
  7.3 3.0 %collective-permute-done.1.hb_ref = f32[13,8,256]{2,1,0:T(8,128)S(1)} collective-permute-done((f32[13,8,256]{2,1,0:T(8,128)S(1)}, f32[13,8,256]{2,1,0:T(8,128)S(1)}, u32[]{:S(2)}, u32[]{:S(2)}) %collective-permute-start.1) | collective-permute-done | bytes 106528 | tf_op jit(solution)/shard_map/ppermute | solution.py:549
  10.3 0.4 %shard_map.78 = (f32[56,128]{1,0:T(8,128)S(1)}, f32[80,128]{1,0:T(8,128)S(1)}) custom-call(f32[5,8,16,256]{3,2,1,0:T(8,128)S(1)} %get-tuple-element.16.u_ref, f32[3,8,16,256]{3,2,1,0:T(8,128)S(1)} %get-tuple-element.17.f_ref, f32[13,8,256]{2,1,0:T(8,128)S(1)} %collective-permute-done.ha_ref, f32[13,8,256]{2,1,0:T(8,128)S(1)} %collective-permute-done.1.hb_ref), custom_call_target="tpu_custom_call" | custom-call | tf_op jit(solution)/shard_map/pallas_call | solution.py:30
  10.7 0.0 collective-permute-start.4
  10.7 1.2 %collective-permute-done.4.m1_ref = f32[56,128]{1,0:T(8,128)S(1)} collective-permute-done((f32[56,128]{1,0:T(8,128)S(1)}, f32[56,128]{1,0:T(8,128)S(1)}, u32[]{:S(2)}, u32[]{:S(2)}) %collective-permute-start.4) | collective-permute-done | bytes 28704 | tf_op jit(solution)/shard_map/ppermute | solution.py:561
  11.9 1.3 %collective-permute-start.5 = (f32[80,128]{1,0:T(8,128)S(1)}, f32[80,128]{1,0:T(8,128)S(1)}, u32[]{:S(2)}, u32[]{:S(2)}) collective-permute-start(f32[80,128]{1,0:T(8,128)S(1)} %shard_map.79.m2_ref), channel_id=1, source_target_pairs={{4,8},{8,4},{12,0},{0,12},{5,9},{9,5},{13,1},{1,13},{6,10},{10,6},... | collective-permute-start | bytes 122888 | tf_op jit(solution)/shard_map/ppermute | solution.py:564
  13.2 2.3 %collective-permute-done.5.got_ref.m2_ref = f32[80,128]{1,0:T(8,128)S(1)} collective-permute-done((f32[80,128]{1,0:T(8,128)S(1)}, f32[80,128]{1,0:T(8,128)S(1)}, u32[]{:S(2)}, u32[]{:S(2)}) %collective-permute-start.5) | collective-permute-done | bytes 40992 | tf_op jit(solution)/shard_map/ppermute | solution.py:564
  15.4 1.5 %collective-permute-start.6 = (f32[4,24,128]{2,1,0:T(8,128)S(1)}, f32[4,24,128]{2,1,0:T(8,128)S(1)}, u32[]{:S(2)}, u32[]{:S(2)}) collective-permute-start(f32[4,24,128]{2,1,0:T(8,128)S(1)} %shard_map.80), channel_id=1, source_target_pairs={{0,16},{16,0},{1,17},{17,1},{2,18},{18,2},{3,19},{19,3},{4,20},{20... | collective-permute-start | bytes 147464 | tf_op jit(solution)/shard_map/ppermute | solution.py:571
  17.0 0.0 collective-permute-done.2.pa_ref
  17.0 0.0 collective-permute-done.3.pb_ref
  17.0 2.6 %collective-permute-done.6 = f32[4,24,128]{2,1,0:T(8,128)S(1)} collective-permute-done((f32[4,24,128]{2,1,0:T(8,128)S(1)}, f32[4,24,128]{2,1,0:T(8,128)S(1)}, u32[]{:S(2)}, u32[]{:S(2)}) %collective-permute-start.6) | collective-permute-done | bytes 49184 | tf_op jit(solution)/shard_map/ppermute | solution.py:571
  19.5 5.3 %shard_map.81 = (f32[5,8,16,256]{3,2,1,0:T(8,128)}, f32[2,5,8,16]{3,2,1,0:T(8,128)}) custom-call(s32[2]{0:T(128)S(1)} %get-tuple-element.14.off_ref, f32[2,4]{1,0:T(2,128)S(1)} %get-tuple-element.15.wt_ref, f32[5,8,16,256]{3,2,1,0:T(8,128)S(1)} %get-tuple-element.16.u_ref, f32[3,8,16,256]{3,2,1,0:T(8,128)S(1)} %get-tuple-element.17.f_ref, ...), custom_call_target="tpu_custom_call" | custom-call | tf_op jit(solution)/shard_map/pallas_call | solution.py:30
  (2 shorter events, 0.0 us)
Async XLA Ops:
  2.1 5.2 %collective-permute-start = (f32[13,8,256]{2,1,0:T(8,128)S(1)}, f32[13,8,256]{2,1,0:T(8,128)S(1)}, u32[]{:S(2)}, u32[]{:S(2)}) collective-permute-start(f32[13,8,256]{2,1,0:T(8,128)S(1)} %get-tuple-element.18), channel_id=1, source_target_pairs={{0,1},{1,0},{2,3},{3,2},{4,5},{5,4},{6,7},{7,6},{8,9},{9,8},{10,11... | collective-permute-start | bytes 319496 | tf_op jit(solution)/shard_map/ppermute | solution.py:548
  3.7 6.6 %collective-permute-start.1 = (f32[13,8,256]{2,1,0:T(8,128)S(1)}, f32[13,8,256]{2,1,0:T(8,128)S(1)}, u32[]{:S(2)}, u32[]{:S(2)}) collective-permute-start(f32[13,8,256]{2,1,0:T(8,128)S(1)} %get-tuple-element.19), channel_id=1, source_target_pairs={{1,2},{2,1},{5,6},{6,5},{9,10},{10,9},{13,14},{14,13},{17,18},{18,... | collective-permute-start | bytes 319496 | tf_op jit(solution)/shard_map/ppermute | solution.py:549
  5.6 11.3 %collective-permute-start.2 = (f32[13,16,256]{2,1,0:T(8,128)S(1)}, f32[13,16,256]{2,1,0:T(8,128)S(1)}, u32[]{:S(2)}, u32[]{:S(2)}) collective-permute-start(f32[13,16,256]{2,1,0:T(8,128)S(1)} %get-tuple-element.20), channel_id=1, source_target_pairs={{0,4},{4,0},{8,12},{12,8},{1,5},{5,1},{9,13},{13,9},{2,6},{6,2},{1... | collective-permute-start | bytes 638984 | tf_op jit(solution)/shard_map/ppermute | solution.py:550
  5.7 11.3 %collective-permute-start.3 = (f32[13,16,256]{2,1,0:T(8,128)S(1)}, f32[13,16,256]{2,1,0:T(8,128)S(1)}, u32[]{:S(2)}, u32[]{:S(2)}) collective-permute-start(f32[13,16,256]{2,1,0:T(8,128)S(1)} %get-tuple-element.21), channel_id=1, source_target_pairs={{4,8},{8,4},{12,0},{0,12},{5,9},{9,5},{13,1},{1,13},{6,10},{10,6},... | collective-permute-start | bytes 638984 | tf_op jit(solution)/shard_map/ppermute | solution.py:551
  10.7 1.2 %collective-permute-start.4 = (f32[56,128]{1,0:T(8,128)S(1)}, f32[56,128]{1,0:T(8,128)S(1)}, u32[]{:S(2)}, u32[]{:S(2)}) collective-permute-start(f32[56,128]{1,0:T(8,128)S(1)} %get-tuple-element.22), channel_id=1, source_target_pairs={{0,4},{4,0},{8,12},{12,8},{1,5},{5,1},{9,13},{13,9},{2,6},{6,2},{1... | collective-permute-start | bytes 86024 | tf_op jit(solution)/shard_map/ppermute | solution.py:561
  11.9 3.5 %collective-permute-start.5 = (f32[80,128]{1,0:T(8,128)S(1)}, f32[80,128]{1,0:T(8,128)S(1)}, u32[]{:S(2)}, u32[]{:S(2)}) collective-permute-start(f32[80,128]{1,0:T(8,128)S(1)} %shard_map.79.m2_ref), channel_id=1, source_target_pairs={{4,8},{8,4},{12,0},{0,12},{5,9},{9,5},{13,1},{1,13},{6,10},{10,6},... | collective-permute-start | bytes 122888 | tf_op jit(solution)/shard_map/ppermute | solution.py:564
  15.4 4.1 %collective-permute-start.6 = (f32[4,24,128]{2,1,0:T(8,128)S(1)}, f32[4,24,128]{2,1,0:T(8,128)S(1)}, u32[]{:S(2)}, u32[]{:S(2)}) collective-permute-start(f32[4,24,128]{2,1,0:T(8,128)S(1)} %shard_map.80), channel_id=1, source_target_pairs={{0,16},{16,0},{1,17},{17,1},{2,18},{18,2},{3,19},{19,3},{4,20},{20... | collective-permute-start | bytes 147464 | tf_op jit(solution)/shard_map/ppermute | solution.py:571

commit v3 on v2

--- a/solution.py
+++ b/solution.py
@@ -26,12 +26,12 @@
     return pl.BlockSpec(memory_space=pltpu.HBM)
 
 
-def call(kernel, shapes, args, specs=None, scratch=(), aliases=None, cost=None, limit=6):
+def call(kernel, shapes, args, specs=None, scratch=(), aliases=None, cost=None, limit=6, outs=None):
     return pl.pallas_call(
         kernel,
         out_shape=[jax.ShapeDtypeStruct(s.shape, s.dtype) if hasattr(s, "dtype") else jax.ShapeDtypeStruct(s, jnp.float32) for s in shapes],
         in_specs=specs or [vmem()] * len(args),
-        out_specs=[vmem()] * len(shapes),
+        out_specs=outs or [vmem()] * len(shapes),
         scratch_shapes=list(scratch),
         input_output_aliases=aliases or {},
         cost_estimate=cost,
@@ -227,7 +227,7 @@
     out_ref[ROWS : 2 * ROWS, :] = m1_ref[0:ROWS, :]
 
 
-def ring_kernel(m2_ref, got_ref, ring_ref):
+def ring_kernel(m2_ref, got_ref, after_ref, ring_ref):
     _, even, _, _ = place()
     mate = m2_ref[ROWS : 2 * ROWS, :]
     next_ = got_ref[0:ROWS, :]
@@ -237,17 +237,266 @@
     ring_ref[3] = jnp.where(even, next_, mate)
 
 
-def final_kernel(
+class Halo:
+    def __init__(self, C, ha, hb, pa, pb):
+        _, self.even_c, self.even_s, _ = place()
+        self.C, self.ha, self.hb, self.pa, self.pb = C, ha, hb, pa, pb
+
+    def left(self, slot, rows=slice(None)):
+        return jnp.where(self.even_c, self.pb[slot, rows, :], self.pa[slot, rows, :])
+
+    def right(self, slot, rows=slice(None)):
+        return jnp.where(self.even_c, self.pa[slot, rows, :], self.pb[slot, rows, :])
+
+    def beyond(self, side, slot):
+        where_a = self.even_s if side == 1 else jnp.logical_not(self.even_s)
+        return jnp.where(where_a, self.ha[slot], self.hb[slot])
+
+
+def edge_faces(side, outer, inner, at_wall):
+    fo, so = outer.flux(2)
+    fi, si = inner.flux(2)
+    if side == 0:
+        near = face(outer.u, fo, so, inner.u, fi, si)
+        wall = wall_face(fi, si, inner.u[3], -1.0)
+    else:
+        near = face(inner.u, fi, si, outer.u, fo, so)
+        wall = wall_face(fi, si, inner.u[3], 1.0)
+    return [jnp.where(at_wall, w, x) for w, x in zip(wall, near)], near
+
+
+def column_update(cell, circ_lo, circ_hi, axial, low_row, top_row, force):
+    column = cell.u[0].shape
+    T = column[0]
+    srow = lax.broadcasted_iota(jnp.int32, column, 0)
+    f, s = cell.flux(2)
+    back = lambda x: pltpu.roll(x, 1, 0)
+    lo2 = face([back(x) for x in cell.u], [back(x) for x in f], back(s), cell.u, f, s)
+    lo2 = [jnp.where(srow == 0, jnp.broadcast_to(e, column), x) for e, x in zip(low_row, lo2)]
+    hi2 = [
+        jnp.where(srow == T - 1, jnp.broadcast_to(e, column), pltpu.roll(x, T - 1, 0))
+        for e, x in zip(top_row, lo2)
+    ]
+    return updated(cell.u, force, axial, (circ_hi, circ_lo), (hi2, lo2))
+
+
+def sweep(load, lo, hi, axial_of, edges_of, force_of, store):
+    prev = Cell(load(lo - 1))
+    pf, ps = prev.flux(1)
+    cell = Cell(load(lo))
+    cf, cs = cell.flux(1)
+    h_lo = face(prev.u, pf, ps, cell.u, cf, cs)
+    for c in range(lo, hi):
+        nxt = Cell(load(c + 1))
+        nf, ns_ = nxt.flux(1)
+        h_hi = face(cell.u, cf, cs, nxt.u, nf, ns_)
+        store(c, column_update(cell, h_lo, h_hi, axial_of(c, cell), *edges_of(c), force_of(c)))
+        cell, cf, cs, h_lo = nxt, nf, ns_, h_hi
+
+
+def walls(ns):
+    span = lax.axis_index("span")
+    return span == 0, span == ns - 1
+
+
+def bulk_kernel(C, T, ns, u_ref, f_ref, ha_ref, hb_ref, after_ref, one_ref, edge_s):
+    rotor = lax.axis_index("row") == 0
+    halo = Halo(C, ha_ref, hb_ref, None, None)
+    for side, wall in enumerate(walls(ns)):
+        inner = Cell([u_ref[k, :, 0 if side == 0 else T - 1, :] for k in range(5)])
+        outer = Cell([halo.beyond(side, k) for k in range(5)])
+        edge, _ = edge_faces(side, outer, inner, wall)
+        for k in range(5):
+            edge_s[side, k] = edge[k]
+
+    def axial(c, cell):
+        return axial_faces(cell, [0.0] * 5, rotor)
+
+    def edges(c):
+        return [[edge_s[side, k, c : c + 1, :] for k in range(5)] for side in range(2)]
+
+    def store(c, u):
+        for k in range(5):
+            one_ref[k, c] = u[k]
+
+    sweep(lambda c: [u_ref[k, c] for k in range(5)], 1, C - 1, axial, edges, lambda c: [f_ref[k, c] for k in range(3)], store)
+
+
+def half_faces(cell, beside, rotor, near, slide=None):
+    f, s = cell.flux(0)
+    lane = lax.broadcasted_iota(jnp.int32, s.shape, 1)
+    first = lane == 0
+    last = lane == LANES - 1
+    inf, ins = inlet_flux()
+
+    def back(x, v):
+        return jnp.where(first, v, pltpu.roll(x, 1, 1))
+
+    pu = [back(x, v) for x, v in zip(cell.u, INLET)]
+    pf = [pu[1]] + [back(x, v) for x, v in zip(f[1:], inf[1:])]
+    lo = face(pu, pf, back(s, ins), cell.u, f, s)
+    fb, sb = beside.flux(0)
+    sign = jnp.where(rotor, 1.0, -1.0) * (-1.0 if near else 1.0)
+    top = jnp.maximum(s, sb) * sign
+    mid = [a + b - top * (y - x) for x, a, y, b in zip(cell.u, f, beside.u, fb)]
+    if near:
+        lo = [jnp.where(first, jnp.where(rotor, m, h), x) for m, h, x in zip(mid, slide, lo)]
+        hi = [jnp.where(last, jnp.where(rotor, h, m), pltpu.roll(x, LANES - 1, 1)) for m, h, x in zip(mid, slide, lo)]
+    else:
+        lo = [jnp.where(jnp.logical_and(first, jnp.logical_not(rotor)), m, x) for m, x in zip(mid, lo)]
+        hi = [
+            jnp.where(last, jnp.where(rotor, m, 2.0 * g), pltpu.roll(x, LANES - 1, 1))
+            for m, g, x in zip(mid, f, lo)
+        ]
+    return hi, lo
+
+
+def halves(width, rotor):
+    near = pl.multiple_of(jnp.where(rotor, width - LANES, 0), LANES)
+    return near, pl.multiple_of(width - LANES - near, LANES)
+
+
+def far_kernel(
+    C, T, ns,
+    u_ref, f_ref, ha_ref, hb_ref, pa_ref, pb_ref, m1_ref, m2_ref, one_ref, after_ref,
+    near_ref, rows_ref, beside_ref, far_ref,
+    edge_s, col_s, row_s, fedge_s,
+):
+    rotor = lax.axis_index("row") == 0
+    width = u_ref.shape[3]
+    near, far = halves(width, rotor)
+    halo = Halo(C, ha_ref, hb_ref, pa_ref, pb_ref)
+
+    def corner(ref, base, k, side):
+        parts = [ref[pl.ds(base + 16 * q + 2 * k + side, 1), :] for q in range(width // LANES)]
+        return jnp.concatenate(parts, 1)
+
+    def corners(k, side):
+        a = corner(m1_ref, ROWS, k, side)
+        b = corner(m2_ref, 2 * ROWS, k, side)
+        return jnp.where(halo.even_c, b, a), jnp.where(halo.even_c, a, b)
+
+    top_rows = lax.broadcasted_iota(jnp.int32, (C, width), 0)
+
+    def extend(mid, lf, rt):
+        shape = (C, width)
+        tail = jnp.where(top_rows == 0, jnp.broadcast_to(rt, shape), jnp.broadcast_to(lf, shape))
+        return jnp.concatenate([mid, tail], 0)
+
+    cut = lambda xs: [x[:C] for x in xs]
+    for side, wall in enumerate(walls(ns)):
+        s0 = 0 if side == 0 else T - 1
+        row = pl.ds(s0, 1)
+        inner = Cell([extend(u_ref[k, :, s0, :], halo.left(k, row), halo.right(k, row)) for k in range(5)])
+        cell = Cell([extend(halo.beyond(side, k), *corners(k, side)) for k in range(5)])
+        outer = Cell([halo.beyond(side, 5 + k) for k in range(5)])
+        edge, adjoining = edge_faces(side, cell, inner, wall)
+        for k in range(5):
+            edge_s[side, k] = edge[k]
+        f, s = cell.flux(2)
+        fo, so = outer.flux(2)
+        if side == 0:
+            span = cut(adjoining), face(outer.u, fo, so, cut(cell.u), cut(f), s[:C])
+        else:
+            span = face(cut(cell.u), cut(f), s[:C], outer.u, fo, so), cut(adjoining)
+        f, s = cell.flux(1)
+        back = lambda x: pltpu.roll(x, 1, 0)
+        lo1 = face([back(x) for x in cell.u], [back(x) for x in f], back(s), cell.u, f, s)
+        hi1 = [pltpu.roll(x, 2 * C - 1, 0) for x in lo1]
+        mid = Cell(cut(cell.u))
+        axial = axial_faces(mid, [0.0] * 5, rotor)
+        force = [halo.beyond(side, 10 + k) for k in range(3)]
+        new = updated(mid.u, force, axial, (cut(hi1), cut(lo1)), span)
+        for k in range(5):
+            row_s[side, k] = new[k]
+            rows_ref[side, k] = row_s[side, k, :, pl.ds(near, LANES)]
+
+    def load(c):
+        if c < 0:
+            return [halo.left(k + (5 if c == -2 else 0)) for k in range(5)]
+        if c >= C:
+            return [halo.right(k + (5 if c == C + 1 else 0)) for k in range(5)]
+        return [u_ref[k, c] for k in range(5)]
+
+    def edges(c):
+        r = c if c >= 0 else 2 * C - 1
+        return [[edge_s[side, k, r : r + 1, :] for k in range(5)] for side in range(2)]
+
+    def force_of(c):
+        if 0 <= c < C:
+            return [f_ref[k, c] for k in range(3)]
+        return [(halo.left if c < 0 else halo.right)(10 + k) for k in range(3)]
+
+    slots = {-1: 0, 0: 1, C - 1: 2, C: 3}
+
+    def store(c, u):
+        for k in range(5):
+            col_s[k, slots[c]] = u[k]
+
+    axial = lambda c, cell: axial_faces(cell, [0.0] * 5, rotor)
+    sweep(load, -1, 1, axial, edges, force_of, store)
+    sweep(load, C - 1, C + 1, axial, edges, force_of, store)
+
+    def half(k, c, start):
+        lanes = pl.ds(start, LANES)
+        if c in slots:
+            return col_s[k, slots[c], :, lanes]
+        return one_ref[k, c, :, lanes]
+
+    def across(k, s0):
+        lanes = pl.ds(far, LANES)
+        mid = one_ref[k, :, s0, lanes]
+        c = lax.broadcasted_iota(jnp.int32, mid.shape, 0)
+        ends = [jnp.broadcast_to(col_s[k, slots[e], s0 : s0 + 1, lanes], mid.shape) for e in (0, C - 1)]
+        return jnp.where(c == 0, ends[0], jnp.where(c == C - 1, ends[1], mid))
+
+    for k in range(5):
+        for c in range(-1, C + 1):
+            near_ref[k, c + 1] = half(k, c, near)
+
+    for side, wall in enumerate(walls(ns)):
+        s0 = 0 if side == 0 else T - 1
+        inner = Cell([across(k, s0) for k in range(5)])
+        outer = Cell([row_s[side, k, :, pl.ds(far, LANES)] for k in range(5)])
+        edge, _ = edge_faces(side, outer, inner, wall)
+        for k in range(5):
+            fedge_s[side, k] = edge[k]
+
+    down = jnp.where(rotor, LANES - 1, 1)
+    up = jnp.where(rotor, 1, LANES - 1)
+
+    def far_axial(c, cell):
+        for k in range(5):
+            beside_ref[k, c] = pltpu.roll(cell.u[k], up, 1)
+        beside = Cell([pltpu.roll(near_ref[k, c + 1], down, 1) for k in range(5)])
+        return half_faces(cell, beside, rotor, False)
+
+    def far_edges(c):
+        return [[fedge_s[side, k, c : c + 1, :] for k in range(5)] for side in range(2)]
+
+    def far_store(c, u):
+        for k in range(5):
+            far_ref[k, c] = u[k]
+
+    sweep(
+        lambda c: [half(k, c, far) for k in range(5)], 0, C, far_axial, far_edges,
+        lambda c: [f_ref[k, c, :, pl.ds(far, LANES)] for k in range(3)], far_store,
+    )
+
+
+def last_kernel(
     C, T, nc, ns,
-    off_ref, wt_ref, u_ref, f_ref, ha_ref, hb_ref, pa_ref, pb_ref, m1_ref, m2_ref, own_ref, par_ref,
-    out_ref, pf_ref,
-    own_s, par_s, ht_s, ext_s, one_s, far_s, edge_s, rows_s,
+    off_ref, wt_ref, f_ref, own_ref, par_ref, near_ref, rows_ref, beside_ref, far_ref,
+    out_hbm, pf_hbm,
+    own_s, par_s, ht_s, one_s, edge_s, new_s, pf_ref, sem,
 ):
-    row, even_c, even_s, span = place()
+    row = lax.axis_index("row")
     rotor = row == 0
-    hub = span == 0
-    casing = span == ns - 1
-    width = u_ref.shape[3]
+    hub, casing = walls(ns)
+    width = f_ref.shape[3]
+    near, far = halves(width, rotor)
+    far_copy = pltpu.make_async_copy(far_ref, out_hbm.at[:, :, :, pl.ds(far, LANES)], sem.at[C])
+    far_copy.start()
     periods = own_s.shape[0] // (nc * ROWS)
     depth = nc * periods
     sg = jnp.where(rotor, 1, -1)
@@ -364,156 +613,58 @@
             for c in range(C):
                 pf_ref[t, k, c : c + 1, :] = x[:, c * T : (c + 1) * T]
 
-    def left(slot, rows=slice(None)):
-        return jnp.where(even_c, pb_ref[slot, rows, :], pa_ref[slot, rows, :])
-
-    def right(slot, rows=slice(None)):
-        return jnp.where(even_c, pa_ref[slot, rows, :], pb_ref[slot, rows, :])
-
-    def low(slot):
-        return jnp.where(even_s, hb_ref[slot], ha_ref[slot])
-
-    def high(slot):
-        return jnp.where(even_s, ha_ref[slot], hb_ref[slot])
-
-    def corner(ref, base, k, side):
-        parts = [ref[pl.ds(base + 16 * q + 2 * k + side, 1), :] for q in range(width // LANES)]
-        return jnp.concatenate(parts, 1)
-
-    def corners(k, side):
-        a = corner(m1_ref, ROWS, k, side)
-        b = corner(m2_ref, 2 * ROWS, k, side)
-        return jnp.where(even_c, b, a), jnp.where(even_c, a, b)
-
-    eight_rows = lax.broadcasted_iota(jnp.int32, (C, width), 0)
-
-    def extend(mid, lf, rt):
-        shape = (C, width)
-        tail = jnp.where(eight_rows == 0, jnp.broadcast_to(rt, shape), jnp.broadcast_to(lf, shape))
-        return jnp.concatenate([mid, tail], 0)
-
-    def own_row(k, s):
-        mid = u_ref[k, :, s, :]
-        return extend(mid, left(k, pl.ds(s, 1)), right(k, pl.ds(s, 1)))
-
-    for side in range(2):
-        halo = low if side == 0 else high
-        inner = Cell([own_row(k, 0 if side == 0 else T - 1) for k in range(5)])
-        lf_rt = [corners(k, side) for k in range(5)]
-        cell = Cell([extend(halo(k), *lf_rt[k]) for k in range(5)])
-        outer = Cell([halo(5 + k) for k in range(5)])
-        f, s = cell.flux(2)
-        fi, si = inner.flux(2)
-        fo, so = outer.flux(2)
-        cut = lambda xs: [x[:C] for x in xs]
-        if side == 0:
-            near = face(cell.u, f, s, inner.u, fi, si)
-            hi2, lo2 = near, face(outer.u, fo, so, cut(cell.u), cut(f), s[:C])
-            wall = wall_face(fi, si, inner.u[3], -1.0)
-            at_wall = hub
-        else:
-            near = face(inner.u, fi, si, cell.u, f, s)
-            hi2, lo2 = face(cut(cell.u), cut(f), s[:C], outer.u, fo, so), near
-            wall = wall_face(fi, si, inner.u[3], 1.0)
-            at_wall = casing
-        for k in range(5):
-            edge_s[side, k] = jnp.where(at_wall, wall[k], near[k])
-        f, s = cell.flux(1)
-        back = lambda x: pltpu.roll(x, 1, 0)
-        lo1 = face([back(x) for x in cell.u], [back(x) for x in f], back(s), cell.u, f, s)
-        hi1 = [pltpu.roll(x, 2 * C - 1, 0) for x in lo1]
-        mid = Cell(cut(cell.u))
-        first = 0 if side == 0 else T - 1
-        strip = ht_s[pl.ds(first, C, stride=T), :]
-        hs = [strip[:, 40 + 8 * k : 41 + 8 * k] for k in range(5)]
-        hi0, lo0 = axial_faces(mid, hs, rotor)
-        force = [halo(10 + k) for k in range(3)]
-        new = updated(mid.u, force, (hi0, lo0), (cut(hi1), cut(lo1)), (cut(hi2), cut(lo2)))
-        for k in range(5):
-            rows_s[side, k] = new[k]
-
-    column = (T, width)
-    srow = lax.broadcasted_iota(jnp.int32, column, 0)
-
-    def column_update(cell, circ_lo, circ_hi, slide_h, edge_row, force):
-        hi0, lo0 = axial_faces(cell, slide_h, rotor)
-        f, s = cell.flux(2)
-        back = lambda x: pltpu.roll(x, 1, 0)
-        lo2 = face([back(x) for x in cell.u], [back(x) for x in f], back(s), cell.u, f, s)
-        low_row = [edge_s[0, k, edge_row : edge_row + 1, :] for k in range(5)]
-        top_row = [edge_s[1, k, edge_row : edge_row + 1, :] for k in range(5)]
-        lo2 = [jnp.where(srow == 0, jnp.broadcast_to(e, column), x) for e, x in zip(low_row, lo2)]
-        hi2 = [
-            jnp.where(srow == T - 1, jnp.broadcast_to(e, column), pltpu.roll(x, T - 1, 0))
-            for e, x in zip(top_row, lo2)
-        ]
-        return updated(cell.u, force, (hi0, lo0), (circ_hi, circ_lo), (hi2, lo2))
-
-    def sweep(load, lo, hi, slide_of, force_of, store):
-        prev = Cell(load(lo - 1))
-        pf, ps = prev.flux(1)
-        cell = Cell(load(lo))
-        cf, cs = cell.flux(1)
-        h_lo = face(prev.u, pf, ps, cell.u, cf, cs)
-        for c in range(lo, hi):
-            nxt = Cell(load(c + 1))
-            nf, ns_ = nxt.flux(1)
-            h_hi = face(cell.u, cf, cs, nxt.u, nf, ns_)
-            edge_row = c if c >= 0 else 2 * C - 1
-            store(c, column_update(cell, h_lo, h_hi, slide_of(c), edge_row, force_of(c)))
-            cell, cf, cs, h_lo = nxt, nf, ns_, h_hi
-
-    def load0(c):
-        if c < 0:
-            return [left(k + (5 if c == -2 else 0)) for k in range(5)]
-        if c >= C:
-            return [right(k + (5 if c == C + 1 else 0)) for k in range(5)]
-        return [u_ref[k, c] for k in range(5)]
-
-    def force0(c):
-        if c < 0:
-            return [left(10 + k) for k in range(3)]
-        if c >= C:
-            return [right(10 + k) for k in range(3)]
-        return [f_ref[k, c] for k in range(3)]
-
-    def slide0(c):
+    pf_copy = pltpu.make_async_copy(pf_ref, pf_hbm, sem.at[C + 1])
+    pf_copy.start()
+
+    lane = lax.broadcasted_iota(jnp.int32, (T, LANES), 1)
+    end = lane == jnp.where(rotor, LANES - 1, 0)
+    weight = (0.5 * STEP) * sgf
+
+    def at_end(x, column):
+        return pltpu.roll(x, jnp.where(rotor, LANES - 1 - column, (LANES - column) % LANES), 1)
+
+    for c in range(-1, C + 1):
         sector = 0 if 0 <= c < C else (1 if c >= C else 7)
         r = (c % C) * T
-        return [ht_s[r : r + T, 8 * k + sector : 8 * k + sector + 1] for k in range(5)]
-
-    def store0(c, u):
-        for k in range(5):
-            one_s[k, c + 1] = u[k]
-
-    sweep(load0, -1, C + 1, slide0, force0, store0)
-
-    for side in range(2):
-        s = 0 if side == 0 else T - 1
-        inner = Cell([one_s[k, 1 : C + 1, s, :] for k in range(5)])
-        outer = Cell([rows_s[side, k] for k in range(5)])
-        fi, si = inner.flux(2)
-        fo, so = outer.flux(2)
-        if side == 0:
-            near = face(outer.u, fo, so, inner.u, fi, si)
-            wall, at_wall = wall_face(fi, si, inner.u[3], -1.0), hub
-        else:
-            near = face(inner.u, fi, si, outer.u, fo, so)
-            wall, at_wall = wall_face(fi, si, inner.u[3], 1.0), casing
-        for k in range(5):
-            edge_s[side, k, 0:C, :] = jnp.where(at_wall, wall[k], near[k])
-
-    def load1(c):
-        return [one_s[k, c + 1] for k in range(5)]
-
-    def slide1(c):
-        return [ht_s[c * T : (c + 1) * T, 80 + 8 * k : 81 + 8 * k] for k in range(5)]
-
-    def store1(c, u):
-        for k in range(5):
-            out_ref[k, c] = u[k]
-
-    sweep(load1, 0, C, slide1, force0, store1)
+        for k in range(5):
+            h = at_end(ht_s[r : r + T, :], 8 * k + sector)
+            one_s[k, c + 1] = near_ref[k, c + 1] - jnp.where(end, weight * h, 0.0)
+    for side, wall in enumerate((hub, casing)):
+        s0 = 0 if side == 0 else T - 1
+        strip = ht_s[pl.ds(s0, C, stride=T), :]
+        inner = Cell([one_s[k, 1 : C + 1, s0, :] for k in range(5)])
+        outer = Cell([
+            rows_ref[side, k] - jnp.where(end[:C], weight * at_end(strip, 40 + 8 * k), 0.0)
+            for k in range(5)
+        ])
+        edge, _ = edge_faces(side, outer, inner, wall)
+        for k in range(5):
+            edge_s[side, k] = edge[k]
+
+    def axial(c, cell):
+        beside = Cell([beside_ref[k, c] for k in range(5)])
+        h = [at_end(ht_s[c * T : (c + 1) * T, :], 80 + 8 * k) for k in range(5)]
+        return half_faces(cell, beside, rotor, True, h)
+
+    def edges(c):
+        return [[edge_s[side, k, c : c + 1, :] for k in range(5)] for side in range(2)]
+
+    def out_copy(c):
+        return pltpu.make_async_copy(new_s.at[:, c], out_hbm.at[:, c, :, pl.ds(near, LANES)], sem.at[c])
+
+    def store(c, u):
+        for k in range(5):
+            new_s[k, c] = u[k]
+        out_copy(c).start()
+
+    sweep(
+        lambda c: [one_s[k, c + 1] for k in range(5)], 0, C, axial, edges,
+        lambda c: [f_ref[k, c, :, pl.ds(near, LANES)] for k in range(3)], store,
+    )
+    far_copy.wait()
+    pf_copy.wait()
+    for c in range(C):
+        out_copy(c).wait()
 
 
 def pairs(count, first, wrap):
@@ -530,7 +681,7 @@
     nc = lax.axis_size("circ")
     ns = lax.axis_size("span")
     area = C * T
-    assert area == LANES and nc % 2 == 0 and A % LANES == 0 and C == 8
+    assert area == LANES and nc % 2 == 0 and A == 2 * LANES and C == 8
     rho, v, p, force = density[0], velocity[0], pressure[0], blade_force[0]
 
     u, force, off, wt, sa, sb, pa, pb = call(
@@ -559,10 +710,19 @@
     )
     planes = m1[:ROWS]
     m1 = lax.ppermute(m1, "circ", pairs(nc, 0, True))
+    f32 = jnp.float32
     if nc == 4:
         (m2,) = call(fill_kernel, [m2.shape], (m1, m2), aliases={1: 0})
+    (one,) = call(
+        functools.partial(bulk_kernel, C, T, ns),
+        [(5, C, T, A)],
+        (u, force, ha, hb, m2),
+        scratch=[pltpu.VMEM((2, 5, C, A), f32)],
+        cost=pl.CostEstimate(flops=10_000_000, bytes_accessed=4_000_000, transcendentals=0),
+    )
+    if nc == 4:
         got = lax.ppermute(m2, "circ", pairs(nc, 1, True))
-        (ring,) = call(ring_kernel, [(nc, ROWS, LANES)], (m2, got))
+        (ring,) = call(ring_kernel, [(nc, ROWS, LANES)], (m2, got, one))
     else:
         got = lax.ppermute(m2, "circ", pairs(nc, 1, True))
         whole = lax.all_gather(planes, "circ")
@@ -571,22 +731,35 @@
     partner = lax.ppermute(ring, "row", [(0, 1), (1, 0)])
     copies = max(1, 8 // nc)
     rows = nc * ROWS
+    near, halo_rows, beside, far = call(
+        functools.partial(far_kernel, C, T, ns),
+        [(5, C + 2, T, LANES), (2, 5, C, LANES), (5, C, T, LANES), (5, C, T, LANES)],
+        (u, force, ha, hb, pa, pb, m1, got, one, ring),
+        scratch=[
+            pltpu.VMEM((2, 5, 2 * C, A), f32),
+            pltpu.VMEM((5, 4, T, A), f32),
+            pltpu.VMEM((2, 5, C, A), f32),
+            pltpu.VMEM((2, 5, C, LANES), f32),
+        ],
+        cost=pl.CostEstimate(flops=10_000_000, bytes_accessed=4_000_000, transcendentals=0),
+    )
     state, plane_flux = call(
-        functools.partial(final_kernel, C, T, nc, ns),
+        functools.partial(last_kernel, C, T, nc, ns),
         [(5, C, T, A), (2, 5, C, T)],
-        (off, wt, u, force, ha, hb, pa, pb, m1, got, ring.reshape(rows, LANES), partner.reshape(rows, LANES)),
-        specs=[smem(), smem()] + [vmem()] * 10,
+        (off, wt, force, ring.reshape(rows, LANES), partner.reshape(rows, LANES), near, halo_rows, beside, far),
+        specs=[smem(), smem()] + [vmem()] * 7,
+        outs=[hbm(), hbm()],
+        scratch=[
+            pltpu.VMEM((copies * rows, LANES), f32),
+            pltpu.VMEM((copies * rows, LANES), f32),
+            pltpu.VMEM((LANES, LANES), f32),
+            pltpu.VMEM((5, C + 2, T, LANES), f32),
+            pltpu.VMEM((2, 5, C, LANES), f32),
+            pltpu.VMEM((5, C, T, LANES), f32),
+            pltpu.VMEM((2, 5, C, T), f32),
+            pltpu.SemaphoreType.DMA((C + 2,)),
+        ],
         limit=16,
-        scratch=[
-            pltpu.VMEM((copies * rows, LANES), jnp.float32),
-            pltpu.VMEM((copies * rows, LANES), jnp.float32),
-            pltpu.VMEM((LANES, LANES), jnp.float32),
-            pltpu.VMEM((8, LANES), jnp.float32),
-            pltpu.VMEM((5, C + 2, T, A), jnp.float32),
-            pltpu.VMEM((8, LANES), jnp.float32),
-            pltpu.VMEM((2, 5, 2 * C, A), jnp.float32),
-            pltpu.VMEM((2, 5, C, A), jnp.float32),
-        ],
     )
     return state[None], plane_flux[None]
 

time: 25 us -> 23 us (0.920)
  waiting for transfers between devices: 9.02 us -> 5.85 us
  Pallas kernels: 7.11 us -> 8.26 us
    ppermute x1, waiting for transfers between devices: 2.56 us -> 0.55 us  [body(): partner = lax.ppermute(ring, 'row', [(0, 1), (1, 0)])]
    ppermute x1, waiting for transfers between devices: 2.26 us -> 1.11 us  [body(): got = lax.ppermute(m2, 'circ', pairs(nc, 1, True))]
    pallas_call x5 -> x7, Pallas kernels: 7.11 us -> 8.26 us  [call(): pl.pallas_call(kernel, out_shape=[jax.ShapeDtypeStruct(s.shape, s.dtype)...]
  transfers between devices with their start and end apart: 7 -> 7, of which waited for: 4 -> 4; matrix products, arithmetic and copies ran while one was open for 0% -> 0% of each run, Pallas kernels for 1% -> 15%
where the time goes in v3:
time: 23 us; the launch traced here: 22.8 us
  Pallas kernels  8.26 us (36%)
  starting transfers between devices  8.04 us (35%)
  waiting for transfers between devices  5.85 us (25%)
  between operations  0.68 us (3%)
    pallas_call x7, Pallas kernels, call(): pl.pallas_call(kernel, out_shape=[jax.ShapeDtypeStruct(s.shape, s.dtype)...  8.26 us
    ppermute x1, waiting for transfers between devices, body(): hb = lax.ppermute(sb, 'span', pairs(ns, 1, False))  2.99 us
    ppermute x1, starting transfers between devices, body(): hb = lax.ppermute(sb, 'span', pairs(ns, 1, False))  1.91 us
    ppermute x1, starting transfers between devices, body(): ha = lax.ppermute(sa, 'span', pairs(ns, 0, False))  1.64 us
    ppermute x1, starting transfers between devices, body(): pb = lax.ppermute(pb, 'circ', pairs(nc, 1, True))  1.59 us
    ppermute x1, starting transfers between devices, body(): partner = lax.ppermute(ring, 'row', [(0, 1), (1, 0)])  1.52 us
    ppermute x1, starting transfers between devices, body(): got = lax.ppermute(m2, 'circ', pairs(nc, 1, True))  1.26 us
    ppermute x1, waiting for transfers between devices, body(): m1 = lax.ppermute(m1, 'circ', pairs(nc, 0, True))  1.19 us
  transfers between devices with their start and end apart: 7, of which 4 were waited for; matrix products, arithmetic and copies ran while one was open for 0% of the time, Pallas kernels for 15%

profile of v3, /device:TPU:16, one launch (start us, length us, event | category | flops | bytes accessed | tf_op | source)
XLA Modules:
  0.0 22.8 jit_solution(9188800958967210648)
XLA Ops:
  0.6 1.4 %shard_map.77 = (f32[5,8,16,256]{3,2,1,0:T(8,128)S(1)}, f32[3,8,16,256]{3,2,1,0:T(8,128)S(1)}, s32[2]{0:T(128)S(1)}, f32[2,4]{1,0:T(2,128)S(1)}, f32[13,8,256]{2...) custom-call(f32[8,16,256]{2,1,0:T(8,128)} %bitcast.12, ...), custom_call_target="tpu_custom_call" | custom-call | tf_op jit(solution)/shard_map/pallas_call | solution.py:30
  2.1 1.6 %collective-permute-start = (f32[13,8,256]{2,1,0:T(8,128)S(1)}, f32[13,8,256]{2,1,0:T(8,128)S(1)}, u32[]{:S(2)}, u32[]{:S(2)}) collective-permute-start(f32[13,8,256]{2,1,0:T(8,128)S(1)} %get-tuple-element.22), channel_id=1, source_target_pairs={{0,1},{1,0},{2,3},{3,2},{4,5},{5,4},{6,7},{7,6},{8,9},{9,8},{10,11... | collective-permute-start | bytes 319496 | tf_op jit(solution)/shard_map/ppermute | solution.py:699
  3.7 1.9 %collective-permute-start.1 = (f32[13,8,256]{2,1,0:T(8,128)S(1)}, f32[13,8,256]{2,1,0:T(8,128)S(1)}, u32[]{:S(2)}, u32[]{:S(2)}) collective-permute-start(f32[13,8,256]{2,1,0:T(8,128)S(1)} %get-tuple-element.23), channel_id=1, source_target_pairs={{1,2},{2,1},{5,6},{6,5},{9,10},{10,9},{13,14},{14,13},{17,18},{18,... | collective-permute-start | bytes 319496 | tf_op jit(solution)/shard_map/ppermute | solution.py:700
  5.6 0.1 collective-permute-start.5
  5.7 1.6 %collective-permute-start.6 = (f32[13,16,256]{2,1,0:T(8,128)S(1)}, f32[13,16,256]{2,1,0:T(8,128)S(1)}, u32[]{:S(2)}, u32[]{:S(2)}) collective-permute-start(f32[13,16,256]{2,1,0:T(8,128)S(1)} %get-tuple-element.27), channel_id=1, source_target_pairs={{4,8},{8,4},{12,0},{0,12},{5,9},{9,5},{13,1},{1,13},{6,10},{10,6},... | collective-permute-start | bytes 638984 | tf_op jit(solution)/shard_map/ppermute | solution.py:702
  7.3 0.0 collective-permute-done.ha_ref
  7.3 3.0 %collective-permute-done.1.hb_ref = f32[13,8,256]{2,1,0:T(8,128)S(1)} collective-permute-done((f32[13,8,256]{2,1,0:T(8,128)S(1)}, f32[13,8,256]{2,1,0:T(8,128)S(1)}, u32[]{:S(2)}, u32[]{:S(2)}) %collective-permute-start.1) | collective-permute-done | bytes 106528 | tf_op jit(solution)/shard_map/ppermute | solution.py:700
  10.3 0.4 %shard_map.78 = (f32[56,128]{1,0:T(8,128)S(1)}, f32[80,128]{1,0:T(8,128)S(1)}) custom-call(f32[5,8,16,256]{3,2,1,0:T(8,128)S(1)} %get-tuple-element.21.u_ref, f32[3,8,16,256]{3,2,1,0:T(8,128)S(1)} %get-tuple-element.20.f_ref, f32[13,8,256]{2,1,0:T(8,128)S(1)} %collective-permute-done.ha_ref, f32[13,8,256]{2,1,0:T(8,128)S(1)} %collective-permute-done.1.hb_ref), custom_call_target="tpu_custom_call" | custom-call | tf_op jit(solution)/shard_map/pallas_call | solution.py:30
  10.7 0.0 collective-permute-start.2
  10.7 1.2 %collective-permute-done.2.m1_ref = f32[56,128]{1,0:T(8,128)S(1)} collective-permute-done((f32[56,128]{1,0:T(8,128)S(1)}, f32[56,128]{1,0:T(8,128)S(1)}, u32[]{:S(2)}, u32[]{:S(2)}) %collective-permute-start.2) | collective-permute-done | bytes 28704 | tf_op jit(solution)/shard_map/ppermute | solution.py:712
  11.9 1.3 %collective-permute-start.3 = (f32[80,128]{1,0:T(8,128)S(1)}, f32[80,128]{1,0:T(8,128)S(1)}, u32[]{:S(2)}, u32[]{:S(2)}) collective-permute-start(f32[80,128]{1,0:T(8,128)S(1)} %shard_map.79.after_ref.m2_ref), channel_id=1, source_target_pairs={{4,8},{8,4},{12,0},{0,12},{5,9},{9,5},{13,1},{1,13},{6,10},{10,6},... | collective-permute-start | bytes 122888 | tf_op jit(solution)/shard_map/ppermute | solution.py:724
  13.2 1.1 %shard_map.80.after_ref.one_ref = f32[5,8,16,256]{3,2,1,0:T(8,128)S(1)} custom-call(f32[5,8,16,256]{3,2,1,0:T(8,128)S(1)} %get-tuple-element.21.u_ref, f32[3,8,16,256]{3,2,1,0:T(8,128)S(1)} %get-tuple-element.20.f_ref, f32[13,8,256]{2,1,0:T(8,128)S(1)} %collective-permute-done.ha_ref, f32[13,8,256]{2,1,0:T(8,128)S(1)} %collective-permute-done.1.hb_ref, ...), custom_call_target="tpu_custom_call" | custom-call | flops 10000000 | bytes 4000000 | tf_op jit(solution)/shard_map/pallas_call | solution.py:30
  14.3 1.1 %collective-permute-done.3.got_ref.m2_ref = f32[80,128]{1,0:T(8,128)S(1)} collective-permute-done((f32[80,128]{1,0:T(8,128)S(1)}, f32[80,128]{1,0:T(8,128)S(1)}, u32[]{:S(2)}, u32[]{:S(2)}) %collective-permute-start.3) | collective-permute-done | bytes 40992 | tf_op jit(solution)/shard_map/ppermute | solution.py:724
  15.4 1.5 %collective-permute-start.4 = (f32[4,24,128]{2,1,0:T(8,128)S(1)}, f32[4,24,128]{2,1,0:T(8,128)S(1)}, u32[]{:S(2)}, u32[]{:S(2)}) collective-permute-start(f32[4,24,128]{2,1,0:T(8,128)S(1)} %shard_map.81.after_ref), channel_id=1, source_target_pairs={{0,16},{16,0},{1,17},{17,1},{2,18},{18,2},{3,19},{19,3},{4,20},{20... | collective-permute-start | bytes 147464 | tf_op jit(solution)/shard_map/ppermute | solution.py:731
  17.0 0.0 collective-permute-done.5.pa_ref
  17.0 0.0 collective-permute-done.6.pb_ref
  17.0 2.0 %shard_map.82 = (f32[5,10,16,128]{3,2,1,0:T(8,128)S(1)}, f32[2,5,8,128]{3,2,1,0:T(8,128)S(1)}, f32[5,8,16,128]{3,2,1,0:T(8,128)S(1)}, f32[5,8,16,128]{3,2,1,0:T(8,128)S(1)}) custom-call(f32[5,8,16,256]{3,2,1,0:T(8,128)S(1)} %get-tuple-element.21.u_ref, f32[3,8,16,256]{3,2,1,0:T(8,128)S(1)} %get-tuple-element.20.f_ref, ...), custom_call_target="tpu_custom_call" | custom-call | flops 10000000 | bytes 4000000 | tf_op jit(solution)/shard_map/pallas_call | solution.py:30
  19.0 0.5 %collective-permute-done.4 = f32[4,24,128]{2,1,0:T(8,128)S(1)} collective-permute-done((f32[4,24,128]{2,1,0:T(8,128)S(1)}, f32[4,24,128]{2,1,0:T(8,128)S(1)}, u32[]{:S(2)}, u32[]{:S(2)}) %collective-permute-start.4) | collective-permute-done | bytes 49184 | tf_op jit(solution)/shard_map/ppermute | solution.py:731
  19.5 3.3 %shard_map.83 = (f32[5,8,16,256]{3,2,1,0:T(8,128)}, f32[2,5,8,16]{3,2,1,0:T(8,128)}) custom-call(s32[2]{0:T(128)S(1)} %get-tuple-element.18.off_ref, f32[2,4]{1,0:T(2,128)S(1)} %get-tuple-element.19.wt_ref, f32[3,8,16,256]{3,2,1,0:T(8,128)S(1)} %get-tuple-element.20.f_ref, f32[96,128]{1,0:T(8,128)S(1)} %bitcast.8, f32[96,128]{1,0:T(8,128)S(1)} %bitcast.9, ...), custom_call_target="tpu_custom_call" | custom-call | tf_op jit(solution)/shard_map/pallas_call | solution.py:30
  (2 shorter events, 0.0 us)
Async XLA Ops:
  2.1 5.2 %collective-permute-start = (f32[13,8,256]{2,1,0:T(8,128)S(1)}, f32[13,8,256]{2,1,0:T(8,128)S(1)}, u32[]{:S(2)}, u32[]{:S(2)}) collective-permute-start(f32[13,8,256]{2,1,0:T(8,128)S(1)} %get-tuple-element.22), channel_id=1, source_target_pairs={{0,1},{1,0},{2,3},{3,2},{4,5},{5,4},{6,7},{7,6},{8,9},{9,8},{10,11... | collective-permute-start | bytes 319496 | tf_op jit(solution)/shard_map/ppermute | solution.py:699
  3.7 6.6 %collective-permute-start.1 = (f32[13,8,256]{2,1,0:T(8,128)S(1)}, f32[13,8,256]{2,1,0:T(8,128)S(1)}, u32[]{:S(2)}, u32[]{:S(2)}) collective-permute-start(f32[13,8,256]{2,1,0:T(8,128)S(1)} %get-tuple-element.23), channel_id=1, source_target_pairs={{1,2},{2,1},{5,6},{6,5},{9,10},{10,9},{13,14},{14,13},{17,18},{18,... | collective-permute-start | bytes 319496 | tf_op jit(solution)/shard_map/ppermute | solution.py:700
  5.6 11.3 %collective-permute-start.5 = (f32[13,16,256]{2,1,0:T(8,128)S(1)}, f32[13,16,256]{2,1,0:T(8,128)S(1)}, u32[]{:S(2)}, u32[]{:S(2)}) collective-permute-start(f32[13,16,256]{2,1,0:T(8,128)S(1)} %get-tuple-element.26), channel_id=1, source_target_pairs={{0,4},{4,0},{8,12},{12,8},{1,5},{5,1},{9,13},{13,9},{2,6},{6,2},{1... | collective-permute-start | bytes 638984 | tf_op jit(solution)/shard_map/ppermute | solution.py:701
  5.7 11.3 %collective-permute-start.6 = (f32[13,16,256]{2,1,0:T(8,128)S(1)}, f32[13,16,256]{2,1,0:T(8,128)S(1)}, u32[]{:S(2)}, u32[]{:S(2)}) collective-permute-start(f32[13,16,256]{2,1,0:T(8,128)S(1)} %get-tuple-element.27), channel_id=1, source_target_pairs={{4,8},{8,4},{12,0},{0,12},{5,9},{9,5},{13,1},{1,13},{6,10},{10,6},... | collective-permute-start | bytes 638984 | tf_op jit(solution)/shard_map/ppermute | solution.py:702
  10.7 1.2 %collective-permute-start.2 = (f32[56,128]{1,0:T(8,128)S(1)}, f32[56,128]{1,0:T(8,128)S(1)}, u32[]{:S(2)}, u32[]{:S(2)}) collective-permute-start(f32[56,128]{1,0:T(8,128)S(1)} %get-tuple-element.24), channel_id=1, source_target_pairs={{0,4},{4,0},{8,12},{12,8},{1,5},{5,1},{9,13},{13,9},{2,6},{6,2},{1... | collective-permute-start | bytes 86024 | tf_op jit(solution)/shard_map/ppermute | solution.py:712
  11.9 3.5 %collective-permute-start.3 = (f32[80,128]{1,0:T(8,128)S(1)}, f32[80,128]{1,0:T(8,128)S(1)}, u32[]{:S(2)}, u32[]{:S(2)}) collective-permute-start(f32[80,128]{1,0:T(8,128)S(1)} %shard_map.79.after_ref.m2_ref), channel_id=1, source_target_pairs={{4,8},{8,4},{12,0},{0,12},{5,9},{9,5},{13,1},{1,13},{6,10},{10,6},... | collective-permute-start | bytes 122888 | tf_op jit(solution)/shard_map/ppermute | solution.py:724
  15.4 4.1 %collective-permute-start.4 = (f32[4,24,128]{2,1,0:T(8,128)S(1)}, f32[4,24,128]{2,1,0:T(8,128)S(1)}, u32[]{:S(2)}, u32[]{:S(2)}) collective-permute-start(f32[4,24,128]{2,1,0:T(8,128)S(1)} %shard_map.81.after_ref), channel_id=1, source_target_pairs={{0,16},{16,0},{1,17},{17,1},{2,18},{18,2},{3,19},{19,3},{4,20},{20... | collective-permute-start | bytes 147464 | tf_op jit(solution)/shard_map/ppermute | solution.py:731

commit v4 on v3

--- a/solution.py
+++ b/solution.py
@@ -16,10 +16,6 @@
 
 def vmem():
     return pl.BlockSpec(memory_space=pltpu.VMEM)
-
-
-def smem():
-    return pl.BlockSpec(memory_space=pltpu.SMEM)
 
 
 def hbm():
@@ -356,16 +352,116 @@
     return near, pl.multiple_of(width - LANES - near, LANES)
 
 
+class Ring:
+    def __init__(self, C, T, nc, ns, off_ref, wt_ref):
+        self.C, self.T, self.nc = C, T, nc
+        self.off, self.wt = off_ref, wt_ref
+        self.periods = max(1, 8 // nc)
+        self.depth = nc * self.periods
+        self.cycle = nc * C
+        self.hub, self.casing = walls(ns)
+        self.lane = lax.broadcasted_iota(jnp.int32, (self.depth, LANES), 1)
+
+    def unpack(self, scratch, message):
+        rows = self.nc * ROWS
+        for copy in range(self.periods):
+            scratch[copy * rows : (copy + 1) * rows, :] = message[...]
+
+    def get(self, ref, j):
+        return ref[pl.ds(j, self.depth, stride=ROWS), :]
+
+    def ahead(self, x, k):
+        if k == 0:
+            return x
+        a = pltpu.roll(x, (LANES - self.T * k) % LANES, 1)
+        b = pltpu.roll(a, self.depth - 1, 0)
+        return jnp.where(self.lane < LANES - self.T * k, a, b)
+
+    def behind(self, x):
+        a = pltpu.roll(x, self.T, 1)
+        b = pltpu.roll(a, 1, 0)
+        return jnp.where(self.lane >= self.T, a, b)
+
+    def turned(self, x, cells):
+        q = lax.div(cells, self.C)
+        r = lax.rem(cells, self.C)
+        y = pltpu.roll(x, lax.rem(self.depth - q, self.depth), 0)
+        a = pltpu.roll(y, lax.rem(LANES - self.T * r, LANES), 1)
+        b = pltpu.roll(a, self.depth - 1, 0)
+        return jnp.where(self.lane < LANES - self.T * r, a, b)
+
+    def ghosts(self, xs, t, sign):
+        w = [jnp.full((1, LANES), self.wt[t, k], jnp.float32) for k in range(4)]
+        total = w[0] + w[1] + w[2] + w[3]
+        w = [x / total for x in w]
+        start = lax.rem(sign * self.off[t] - 1 + 2 * self.cycle, self.cycle)
+        out = []
+        for x in xs:
+            x = self.turned(x, start)
+            g = w[0] * x
+            for k in range(1, 4):
+                g = g + w[k] * self.ahead(x, k)
+            out.append(g)
+        return out
+
+    def partial_step(self, ref, cell, sign):
+        inner = Cell([self.get(ref, 5 + k) for k in range(5)])
+        fi, si = inner.flux(0)
+        f, s = cell.flux(0)
+        top = jnp.maximum(s, si) * sign
+        h1 = [sign * (a + b - top * (x - y)) for x, a, y, b in zip(cell.u, f, inner.u, fi)]
+        zero = jnp.zeros_like(s)
+        f, s = cell.flux(1)
+        behind = self.behind
+        lo = face([behind(x) for x in cell.u], [behind(x) for x in f], behind(s), cell.u, f, s)
+        hi = [self.ahead(x, 1) for x in lo]
+        f, s = cell.flux(2)
+        edge = Cell([self.get(ref, 13 + k) for k in range(5)])
+        fe, se = edge.flux(2)
+        in_span = lax.rem(self.lane, self.T)
+        first = in_span == 0
+        last = in_span == self.T - 1
+
+        def prev(x, e):
+            return jnp.where(first, e, pltpu.roll(x, 1, 1))
+
+        slo = face([prev(x, e) for x, e in zip(cell.u, edge.u)], [prev(x, e) for x, e in zip(f, fe)], prev(s, se), cell.u, f, s)
+        wall = wall_face(f, s, cell.u[3], -1.0)
+        slo = [jnp.where(jnp.logical_and(first, self.hub), a, b) for a, b in zip(wall, slo)]
+        top_face = face(cell.u, f, s, edge.u, fe, se)
+        wall = wall_face(f, s, cell.u[3], 1.0)
+        top_face = [jnp.where(self.casing, a, b) for a, b in zip(wall, top_face)]
+        shi = [jnp.where(last, a, pltpu.roll(b, LANES - 1, 1)) for a, b in zip(top_face, slo)]
+        force = [self.get(ref, 10 + k) for k in range(3)]
+        return updated(cell.u, force, ([zero] * 5, h1), (hi, lo), (shi, slo))
+
+
+def slide(cell, ghost, sign):
+    f, s = cell.flux(0)
+    g = Cell(ghost)
+    fg, s_g = g.flux(0)
+    top = jnp.maximum(s, s_g) * sign
+    return [a + b - top * (y - x) for x, a, y, b in zip(cell.u, f, ghost, fg)]
+
+
+def scalar_copies(off_ref, wt_ref, off_s, wt_s, sem):
+    copies = [pltpu.make_async_copy(off_ref, off_s, sem.at[0]), pltpu.make_async_copy(wt_ref, wt_s, sem.at[1])]
+    for copy in copies:
+        copy.start()
+    return copies
+
+
 def far_kernel(
-    C, T, ns,
-    u_ref, f_ref, ha_ref, hb_ref, pa_ref, pb_ref, m1_ref, m2_ref, one_ref, after_ref,
-    near_ref, rows_ref, beside_ref, far_ref,
-    edge_s, col_s, row_s, fedge_s,
+    C, T, nc, ns,
+    off_ref, wt_ref, u_ref, f_ref, ha_ref, hb_ref, pa_ref, pb_ref, m1_ref, m2_ref, one_ref, own_ref,
+    near_ref, rows_ref, beside_ref, far_ref, pre_ref,
+    edge_s, col_s, row_s, fedge_s, own_s, off_s, wt_s, small_sem,
 ):
     rotor = lax.axis_index("row") == 0
     width = u_ref.shape[3]
     near, far = halves(width, rotor)
     halo = Halo(C, ha_ref, hb_ref, pa_ref, pb_ref)
+    scalars = scalar_copies(off_ref, wt_ref, off_s, wt_s, small_sem)
 
     def corner(ref, base, k, side):
         parts = [ref[pl.ds(base + 16 * q + 2 * k + side, 1), :] for q in range(width // LANES)]
@@ -482,122 +578,50 @@
         lambda c: [half(k, c, far) for k in range(5)], 0, C, far_axial, far_edges,
         lambda c: [f_ref[k, c, :, pl.ds(far, LANES)] for k in range(3)], far_store,
     )
+    for copy in scalars:
+        copy.wait()
+    ring = Ring(C, T, nc, ns, off_s, wt_s)
+    ring.unpack(own_s, own_ref)
+    own = Cell([ring.get(own_s, k) for k in range(5)])
+    part = ring.partial_step(own_s, own, jnp.where(rotor, 1.0, -1.0))
+    ghost = ring.ghosts(own.u, 0, jnp.where(rotor, -1, 1))
+    for k in range(5):
+        pre_ref[k] = part[k]
+        pre_ref[5 + k] = ghost[k]
 
 
 def last_kernel(
     C, T, nc, ns,
-    off_ref, wt_ref, f_ref, own_ref, par_ref, near_ref, rows_ref, beside_ref, far_ref,
+    off_ref, wt_ref, f_ref, own_ref, par_ref, near_ref, rows_ref, beside_ref, pre_ref, far_ref,
     out_hbm, pf_hbm,
-    own_s, par_s, ht_s, one_s, edge_s, new_s, pf_ref, sem,
+    own_s, par_s, ht_s, one_s, edge_s, new_s, pf_ref, off_s, wt_s, sem, small_sem,
 ):
     row = lax.axis_index("row")
     rotor = row == 0
     hub, casing = walls(ns)
     width = f_ref.shape[3]
     near, far = halves(width, rotor)
-    far_copy = pltpu.make_async_copy(far_ref, out_hbm.at[:, :, :, pl.ds(far, LANES)], sem.at[C])
-    far_copy.start()
-    periods = own_s.shape[0] // (nc * ROWS)
-    depth = nc * periods
+    scalars = scalar_copies(off_ref, wt_ref, off_s, wt_s, small_sem)
+    ring = Ring(C, T, nc, ns, off_s, wt_s)
+    get = ring.get
     sg = jnp.where(rotor, 1, -1)
     sgf = jnp.where(rotor, 1.0, -1.0)
-    cycle = nc * C
-
-    for copy in range(periods):
-        own_s[copy * nc * ROWS : (copy + 1) * nc * ROWS, :] = own_ref[...]
-        par_s[copy * nc * ROWS : (copy + 1) * nc * ROWS, :] = par_ref[...]
-    shape = (depth, LANES)
-    lane = lax.broadcasted_iota(jnp.int32, shape, 1)
-    in_span = lax.rem(lane, T)
-
-    def get(ref, j):
-        return ref[pl.ds(j, depth, stride=ROWS), :]
-
-    def ahead(x, k):
-        if k == 0:
-            return x
-        a = pltpu.roll(x, (LANES - T * k) % LANES, 1)
-        b = pltpu.roll(a, depth - 1, 0)
-        return jnp.where(lane < LANES - T * k, a, b)
-
-    def behind(x):
-        a = pltpu.roll(x, T, 1)
-        b = pltpu.roll(a, 1, 0)
-        return jnp.where(lane >= T, a, b)
-
-    def turned(x, cells):
-        q = lax.div(cells, C)
-        r = lax.rem(cells, C)
-        y = pltpu.roll(x, lax.rem(depth - q, depth), 0)
-        a = pltpu.roll(y, lax.rem(LANES - T * r, LANES), 1)
-        b = pltpu.roll(a, depth - 1, 0)
-        return jnp.where(lane < LANES - T * r, a, b)
-
-    def taps(t):
-        w = [jnp.full((1, LANES), wt_ref[t, k], jnp.float32) for k in range(4)]
-        total = w[0] + w[1] + w[2] + w[3]
-        return [x / total for x in w]
-
-    def ghosts(xs, t, sign):
-        w = taps(t)
-        start = lax.rem(sign * off_ref[t] - 1 + 2 * cycle, cycle)
-        out = []
-        for x in xs:
-            x = turned(x, start)
-            g = w[0] * x
-            for k in range(1, 4):
-                g = g + w[k] * ahead(x, k)
-            out.append(g)
-        return out
-
-    def slide(cell, ghost, sign):
-        f, s = cell.flux(0)
-        g = Cell(ghost)
-        fg, s_g = g.flux(0)
-        top = jnp.maximum(s, s_g) * sign
-        return [a + b - top * (y - x) for x, a, y, b in zip(cell.u, f, ghost, fg)]
-
-    def ring_step(ref, cell, h, sign):
-        inner = Cell([get(ref, 5 + k) for k in range(5)])
-        fi, si = inner.flux(0)
-        f, s = cell.flux(0)
-        top = jnp.maximum(s, si) * sign
-        h1 = [a + b - top * (x - y) for x, a, y, b in zip(cell.u, f, inner.u, fi)]
-        ax_hi = [sign * x for x in h]
-        ax_lo = [sign * x for x in h1]
-        f, s = cell.flux(1)
-        lo = face([behind(x) for x in cell.u], [behind(x) for x in f], behind(s), cell.u, f, s)
-        hi = [ahead(x, 1) for x in lo]
-        f, s = cell.flux(2)
-        edge = Cell([get(ref, 13 + k) for k in range(5)])
-        fe, se = edge.flux(2)
-        first = in_span == 0
-        last = in_span == T - 1
-
-        def prev(x, e):
-            return jnp.where(first, e, pltpu.roll(x, 1, 1))
-
-        slo = face([prev(x, e) for x, e in zip(cell.u, edge.u)], [prev(x, e) for x, e in zip(f, fe)], prev(s, se), cell.u, f, s)
-        wall = wall_face(f, s, cell.u[3], -1.0)
-        slo = [jnp.where(jnp.logical_and(first, hub), a, b) for a, b in zip(wall, slo)]
-        top_face = face(cell.u, f, s, edge.u, fe, se)
-        wall = wall_face(f, s, cell.u[3], 1.0)
-        top_face = [jnp.where(casing, a, b) for a, b in zip(wall, top_face)]
-        shi = [jnp.where(last, a, pltpu.roll(b, LANES - 1, 1)) for a, b in zip(top_face, slo)]
-        force = [get(ref, 10 + k) for k in range(3)]
-        return updated(cell.u, force, (ax_hi, ax_lo), (hi, lo), (shi, slo))
-
+    weight = (0.5 * STEP) * sgf
+    ring.unpack(own_s, own_ref)
+    ring.unpack(par_s, par_ref)
     own = Cell([get(own_s, k) for k in range(5)])
     par = Cell([get(par_s, k) for k in range(5)])
-    g_own = ghosts(par.u, 0, sg)
-    g_par = ghosts(own.u, 0, -sg)
-    h_own = slide(own, g_own, sgf)
-    h_par = slide(par, g_par, -sgf)
-    g_edge = ghosts([get(par_s, 13 + k) for k in range(5)], 0, sg)
+    h_par = slide(par, [pre_ref[5 + k] for k in range(5)], -sgf)
+    par_new = ring.partial_step(par_s, par, -sgf)
+    par_new = [x + weight * h for x, h in zip(par_new, h_par)]
+    for copy in scalars:
+        copy.wait()
+    h_own = slide(own, ring.ghosts(par.u, 0, sg), sgf)
+    g_edge = ring.ghosts([get(par_s, 13 + k) for k in range(5)], 0, sg)
     h_edge = slide(Cell([get(own_s, 13 + k) for k in range(5)]), g_edge, sgf)
-    own_new = ring_step(own_s, own, h_own, sgf)
-    par_new = ring_step(par_s, par, h_par, -sgf)
-    h_next = slide(Cell(own_new), ghosts(par_new, 1, sg), sgf)
+    own_new = [pre_ref[k] - weight * h_own[k] for k in range(5)]
+    h_next = slide(Cell(own_new), ring.ghosts(par_new, 1, sg), sgf)
+    depth = ring.depth
 
     def eight(x):
         if depth == 8:
@@ -613,12 +637,11 @@
             for c in range(C):
                 pf_ref[t, k, c : c + 1, :] = x[:, c * T : (c + 1) * T]
 
-    pf_copy = pltpu.make_async_copy(pf_ref, pf_hbm, sem.at[C + 1])
+    pf_copy = pltpu.make_async_copy(pf_ref, pf_hbm, small_sem.at[2])
     pf_copy.start()
 
     lane = lax.broadcasted_iota(jnp.int32, (T, LANES), 1)
     end = lane == jnp.where(rotor, LANES - 1, 0)
-    weight = (0.5 * STEP) * sgf
 
     def at_end(x, column):
         return pltpu.roll(x, jnp.where(rotor, LANES - 1 - column, (LANES - column) % LANES), 1)
@@ -649,22 +672,23 @@
     def edges(c):
         return [[edge_s[side, k, c : c + 1, :] for k in range(5)] for side in range(2)]
 
-    def out_copy(c):
-        return pltpu.make_async_copy(new_s.at[:, c], out_hbm.at[:, c, :, pl.ds(near, LANES)], sem.at[c])
+    def out_copy(k, c):
+        return pltpu.make_async_copy(new_s.at[k, c], out_hbm.at[k, c], sem.at[c, k])
 
     def store(c, u):
         for k in range(5):
-            new_s[k, c] = u[k]
-        out_copy(c).start()
+            new_s[k, c, :, pl.ds(near, LANES)] = u[k]
+            new_s[k, c, :, pl.ds(far, LANES)] = far_ref[k, c]
+            out_copy(k, c).start()
 
     sweep(
         lambda c: [one_s[k, c + 1] for k in range(5)], 0, C, axial, edges,
         lambda c: [f_ref[k, c, :, pl.ds(near, LANES)] for k in range(3)], store,
     )
-    far_copy.wait()
     pf_copy.wait()
     for c in range(C):
-        out_copy(c).wait()
+        for k in range(5):
+            out_copy(k, c).wait()
 
 
 def pairs(count, first, wrap):
@@ -731,23 +755,27 @@
     partner = lax.ppermute(ring, "row", [(0, 1), (1, 0)])
     copies = max(1, 8 // nc)
     rows = nc * ROWS
-    near, halo_rows, beside, far = call(
-        functools.partial(far_kernel, C, T, ns),
-        [(5, C + 2, T, LANES), (2, 5, C, LANES), (5, C, T, LANES), (5, C, T, LANES)],
-        (u, force, ha, hb, pa, pb, m1, got, one, ring),
+    ring = ring.reshape(rows, LANES)
+    near, halo_rows, beside, far, pre = call(
+        functools.partial(far_kernel, C, T, nc, ns),
+        [(5, C + 2, T, LANES), (2, 5, C, LANES), (5, C, T, LANES), (5, C, T, LANES), (10, copies * nc, LANES)],
+        (off, wt, u, force, ha, hb, pa, pb, m1, got, one, ring),
         scratch=[
             pltpu.VMEM((2, 5, 2 * C, A), f32),
             pltpu.VMEM((5, 4, T, A), f32),
             pltpu.VMEM((2, 5, C, A), f32),
             pltpu.VMEM((2, 5, C, LANES), f32),
+            pltpu.VMEM((copies * rows, LANES), f32),
+            pltpu.SMEM(offsets.shape, jnp.int32),
+            pltpu.SMEM(weights.shape, f32),
+            pltpu.SemaphoreType.DMA((2,)),
         ],
         cost=pl.CostEstimate(flops=10_000_000, bytes_accessed=4_000_000, transcendentals=0),
     )
     state, plane_flux = call(
         functools.partial(last_kernel, C, T, nc, ns),
         [(5, C, T, A), (2, 5, C, T)],
-        (off, wt, force, ring.reshape(rows, LANES), partner.reshape(rows, LANES), near, halo_rows, beside, far),
-        specs=[smem(), smem()] + [vmem()] * 7,
+        (off, wt, force, ring, partner.reshape(rows, LANES), near, halo_rows, beside, pre, far),
         outs=[hbm(), hbm()],
         scratch=[
             pltpu.VMEM((copies * rows, LANES), f32),
@@ -755,9 +783,12 @@
             pltpu.VMEM((LANES, LANES), f32),
             pltpu.VMEM((5, C + 2, T, LANES), f32),
             pltpu.VMEM((2, 5, C, LANES), f32),
-            pltpu.VMEM((5, C, T, LANES), f32),
+            pltpu.VMEM((5, C, T, A), f32),
             pltpu.VMEM((2, 5, C, T), f32),
-            pltpu.SemaphoreType.DMA((C + 2,)),
+            pltpu.SMEM(offsets.shape, jnp.int32),
+            pltpu.SMEM(weights.shape, f32),
+            pltpu.SemaphoreType.DMA((C, 5)),
+            pltpu.SemaphoreType.DMA((3,)),
         ],
         limit=16,
     )

time: 23 us -> 22.6 us (0.983)
  waiting for transfers between devices: 5.85 us -> 5.36 us
    ppermute x1, waiting for transfers between devices: 0.55 us -> 0.07 us  [body(): partner = lax.ppermute(ring, 'row', [(0, 1), (1, 0)])]
  transfers between devices with their start and end apart: 7 -> 7, of which waited for: 4 -> 4; matrix products, arithmetic and copies ran while one was open for 0% -> 0% of each run, Pallas kernels for 15% -> 18%
where the time goes in v4:
time: 22.6 us; the launch traced here: 22.4 us
  Pallas kernels  8.33 us (37%)
  starting transfers between devices  8.04 us (36%)
  waiting for transfers between devices  5.36 us (24%)
  between operations  0.69 us (3%)
    pallas_call x7, Pallas kernels, call(): pl.pallas_call(kernel, out_shape=[jax.ShapeDtypeStruct(s.shape, s.dtype)...  8.33 us
    ppermute x1, waiting for transfers between devices, body(): hb = lax.ppermute(sb, 'span', pairs(ns, 1, False))  2.99 us
    ppermute x1, starting transfers between devices, body(): hb = lax.ppermute(sb, 'span', pairs(ns, 1, False))  1.91 us
    ppermute x1, starting transfers between devices, body(): ha = lax.ppermute(sa, 'span', pairs(ns, 0, False))  1.64 us
    ppermute x1, starting transfers between devices, body(): pb = lax.ppermute(pb, 'circ', pairs(nc, 1, True))  1.59 us
    ppermute x1, starting transfers between devices, body(): partner = lax.ppermute(ring, 'row', [(0, 1), (1, 0)])  1.52 us
    ppermute x1, starting transfers between devices, body(): got = lax.ppermute(m2, 'circ', pairs(nc, 1, True))  1.26 us
    ppermute x1, waiting for transfers between devices, body(): m1 = lax.ppermute(m1, 'circ', pairs(nc, 0, True))  1.19 us
  transfers between devices with their start and end apart: 7, of which 4 were waited for; matrix products, arithmetic and copies ran while one was open for 0% of the time, Pallas kernels for 18%

profile of v4, /device:TPU:16, one launch (start us, length us, event | category | flops | bytes accessed | tf_op | source)
XLA Modules:
  0.0 22.4 jit_solution(18440546573954901938)
XLA Ops:
  0.6 1.4 %shard_map.77 = (f32[5,8,16,256]{3,2,1,0:T(8,128)S(1)}, f32[3,8,16,256]{3,2,1,0:T(8,128)S(1)}, s32[2]{0:T(128)S(1)}, f32[2,4]{1,0:T(2,128)S(1)}, f32[13,8,256]{2...) custom-call(f32[8,16,256]{2,1,0:T(8,128)} %bitcast.13, ...), custom_call_target="tpu_custom_call" | custom-call | tf_op jit(solution)/shard_map/pallas_call | solution.py:26
  2.1 1.6 %collective-permute-start = (f32[13,8,256]{2,1,0:T(8,128)S(1)}, f32[13,8,256]{2,1,0:T(8,128)S(1)}, u32[]{:S(2)}, u32[]{:S(2)}) collective-permute-start(f32[13,8,256]{2,1,0:T(8,128)S(1)} %get-tuple-element.23), channel_id=1, source_target_pairs={{0,1},{1,0},{2,3},{3,2},{4,5},{5,4},{6,7},{7,6},{8,9},{9,8},{10,11... | collective-permute-start | bytes 319496 | tf_op jit(solution)/shard_map/ppermute | solution.py:723
  3.7 1.9 %collective-permute-start.1 = (f32[13,8,256]{2,1,0:T(8,128)S(1)}, f32[13,8,256]{2,1,0:T(8,128)S(1)}, u32[]{:S(2)}, u32[]{:S(2)}) collective-permute-start(f32[13,8,256]{2,1,0:T(8,128)S(1)} %get-tuple-element.24), channel_id=1, source_target_pairs={{1,2},{2,1},{5,6},{6,5},{9,10},{10,9},{13,14},{14,13},{17,18},{18,... | collective-permute-start | bytes 319496 | tf_op jit(solution)/shard_map/ppermute | solution.py:724
  5.6 0.1 collective-permute-start.5
  5.7 1.6 %collective-permute-start.6 = (f32[13,16,256]{2,1,0:T(8,128)S(1)}, f32[13,16,256]{2,1,0:T(8,128)S(1)}, u32[]{:S(2)}, u32[]{:S(2)}) collective-permute-start(f32[13,16,256]{2,1,0:T(8,128)S(1)} %get-tuple-element.28), channel_id=1, source_target_pairs={{4,8},{8,4},{12,0},{0,12},{5,9},{9,5},{13,1},{1,13},{6,10},{10,6},... | collective-permute-start | bytes 638984 | tf_op jit(solution)/shard_map/ppermute | solution.py:726
  7.3 0.0 collective-permute-done.ha_ref
  7.3 3.0 %collective-permute-done.1.hb_ref = f32[13,8,256]{2,1,0:T(8,128)S(1)} collective-permute-done((f32[13,8,256]{2,1,0:T(8,128)S(1)}, f32[13,8,256]{2,1,0:T(8,128)S(1)}, u32[]{:S(2)}, u32[]{:S(2)}) %collective-permute-start.1) | collective-permute-done | bytes 106528 | tf_op jit(solution)/shard_map/ppermute | solution.py:724
  10.3 0.4 %shard_map.78 = (f32[56,128]{1,0:T(8,128)S(1)}, f32[80,128]{1,0:T(8,128)S(1)}) custom-call(f32[5,8,16,256]{3,2,1,0:T(8,128)S(1)} %get-tuple-element.22.u_ref, f32[3,8,16,256]{3,2,1,0:T(8,128)S(1)} %get-tuple-element.21.f_ref, f32[13,8,256]{2,1,0:T(8,128)S(1)} %collective-permute-done.ha_ref, f32[13,8,256]{2,1,0:T(8,128)S(1)} %collective-permute-done.1.hb_ref), custom_call_target="tpu_custom_call" | custom-call | tf_op jit(solution)/shard_map/pallas_call | solution.py:26
  10.7 0.0 collective-permute-start.2
  10.7 1.2 %collective-permute-done.2.m1_ref = f32[56,128]{1,0:T(8,128)S(1)} collective-permute-done((f32[56,128]{1,0:T(8,128)S(1)}, f32[56,128]{1,0:T(8,128)S(1)}, u32[]{:S(2)}, u32[]{:S(2)}) %collective-permute-start.2) | collective-permute-done | bytes 28704 | tf_op jit(solution)/shard_map/ppermute | solution.py:736
  11.9 1.3 %collective-permute-start.3 = (f32[80,128]{1,0:T(8,128)S(1)}, f32[80,128]{1,0:T(8,128)S(1)}, u32[]{:S(2)}, u32[]{:S(2)}) collective-permute-start(f32[80,128]{1,0:T(8,128)S(1)} %shard_map.79.after_ref.m2_ref), channel_id=1, source_target_pairs={{4,8},{8,4},{12,0},{0,12},{5,9},{9,5},{13,1},{1,13},{6,10},{10,6},... | collective-permute-start | bytes 122888 | tf_op jit(solution)/shard_map/ppermute | solution.py:748
  13.2 1.1 %shard_map.80.after_ref.one_ref = f32[5,8,16,256]{3,2,1,0:T(8,128)S(1)} custom-call(f32[5,8,16,256]{3,2,1,0:T(8,128)S(1)} %get-tuple-element.22.u_ref, f32[3,8,16,256]{3,2,1,0:T(8,128)S(1)} %get-tuple-element.21.f_ref, f32[13,8,256]{2,1,0:T(8,128)S(1)} %collective-permute-done.ha_ref, f32[13,8,256]{2,1,0:T(8,128)S(1)} %collective-permute-done.1.hb_ref, ...), custom_call_target="tpu_custom_call" | custom-call | flops 10000000 | bytes 4000000 | tf_op jit(solution)/shard_map/pallas_call | solution.py:26
  14.3 1.1 %collective-permute-done.3.got_ref.m2_ref = f32[80,128]{1,0:T(8,128)S(1)} collective-permute-done((f32[80,128]{1,0:T(8,128)S(1)}, f32[80,128]{1,0:T(8,128)S(1)}, u32[]{:S(2)}, u32[]{:S(2)}) %collective-permute-start.3) | collective-permute-done | bytes 40992 | tf_op jit(solution)/shard_map/ppermute | solution.py:748
  15.4 1.5 %collective-permute-start.4 = (f32[4,24,128]{2,1,0:T(8,128)S(1)}, f32[4,24,128]{2,1,0:T(8,128)S(1)}, u32[]{:S(2)}, u32[]{:S(2)}) collective-permute-start(f32[4,24,128]{2,1,0:T(8,128)S(1)} %shard_map.81), channel_id=1, source_target_pairs={{0,16},{16,0},{1,17},{17,1},{2,18},{18,2},{3,19},{19,3},{4,20},{20... | collective-permute-start | bytes 147464 | tf_op jit(solution)/shard_map/ppermute | solution.py:755
  17.0 0.0 collective-permute-done.5.pa_ref
  17.0 0.0 collective-permute-done.6.pb_ref
  17.0 2.5 %shard_map.82 = (f32[5,10,16,128]{3,2,1,0:T(8,128)S(1)}, f32[2,5,8,128]{3,2,1,0:T(8,128)S(1)}, f32[5,8,16,128]{3,2,1,0:T(8,128)S(1)}, f32[5,8,16,128]{3,2,1,0:T(8,128)S(1)}, f32[10,8,128]{2,1,0:T(8,128)S(1)}) custom-call(s32[2]{0:T(128)S(1)} %get-tuple-element.19.off_ref, f32[2,4]{1,0:T(2,128)S(1)} %get-tuple-element.20.wt_ref, ...), custom_call_target="tpu_custom_call" | custom-call | flops 10000000 | bytes 4000000 | tf_op jit(solution)/shard_map/pallas_call | solution.py:26
  19.5 0.1 collective-permute-done.4
  19.5 2.9 %shard_map.83 = (f32[5,8,16,256]{3,2,1,0:T(8,128)}, f32[2,5,8,16]{3,2,1,0:T(8,128)}) custom-call(s32[2]{0:T(128)S(1)} %get-tuple-element.19.off_ref, f32[2,4]{1,0:T(2,128)S(1)} %get-tuple-element.20.wt_ref, f32[3,8,16,256]{3,2,1,0:T(8,128)S(1)} %get-tuple-element.21.f_ref, f32[96,128]{1,0:T(8,128)S(1)} %bitcast.9, f32[96,128]{1,0:T(8,128)S(1)} %bitcast.10, ...), custom_call_target="tpu_custom_call" | custom-call | tf_op jit(solution)/shard_map/pallas_call | solution.py:26
  (2 shorter events, 0.0 us)
Async XLA Ops:
  2.1 5.2 %collective-permute-start = (f32[13,8,256]{2,1,0:T(8,128)S(1)}, f32[13,8,256]{2,1,0:T(8,128)S(1)}, u32[]{:S(2)}, u32[]{:S(2)}) collective-permute-start(f32[13,8,256]{2,1,0:T(8,128)S(1)} %get-tuple-element.23), channel_id=1, source_target_pairs={{0,1},{1,0},{2,3},{3,2},{4,5},{5,4},{6,7},{7,6},{8,9},{9,8},{10,11... | collective-permute-start | bytes 319496 | tf_op jit(solution)/shard_map/ppermute | solution.py:723
  3.7 6.6 %collective-permute-start.1 = (f32[13,8,256]{2,1,0:T(8,128)S(1)}, f32[13,8,256]{2,1,0:T(8,128)S(1)}, u32[]{:S(2)}, u32[]{:S(2)}) collective-permute-start(f32[13,8,256]{2,1,0:T(8,128)S(1)} %get-tuple-element.24), channel_id=1, source_target_pairs={{1,2},{2,1},{5,6},{6,5},{9,10},{10,9},{13,14},{14,13},{17,18},{18,... | collective-permute-start | bytes 319496 | tf_op jit(solution)/shard_map/ppermute | solution.py:724
  5.6 11.3 %collective-permute-start.5 = (f32[13,16,256]{2,1,0:T(8,128)S(1)}, f32[13,16,256]{2,1,0:T(8,128)S(1)}, u32[]{:S(2)}, u32[]{:S(2)}) collective-permute-start(f32[13,16,256]{2,1,0:T(8,128)S(1)} %get-tuple-element.27), channel_id=1, source_target_pairs={{0,4},{4,0},{8,12},{12,8},{1,5},{5,1},{9,13},{13,9},{2,6},{6,2},{1... | collective-permute-start | bytes 638984 | tf_op jit(solution)/shard_map/ppermute | solution.py:725
  5.7 11.3 %collective-permute-start.6 = (f32[13,16,256]{2,1,0:T(8,128)S(1)}, f32[13,16,256]{2,1,0:T(8,128)S(1)}, u32[]{:S(2)}, u32[]{:S(2)}) collective-permute-start(f32[13,16,256]{2,1,0:T(8,128)S(1)} %get-tuple-element.28), channel_id=1, source_target_pairs={{4,8},{8,4},{12,0},{0,12},{5,9},{9,5},{13,1},{1,13},{6,10},{10,6},... | collective-permute-start | bytes 638984 | tf_op jit(solution)/shard_map/ppermute | solution.py:726
  10.7 1.2 %collective-permute-start.2 = (f32[56,128]{1,0:T(8,128)S(1)}, f32[56,128]{1,0:T(8,128)S(1)}, u32[]{:S(2)}, u32[]{:S(2)}) collective-permute-start(f32[56,128]{1,0:T(8,128)S(1)} %get-tuple-element.25), channel_id=1, source_target_pairs={{0,4},{4,0},{8,12},{12,8},{1,5},{5,1},{9,13},{13,9},{2,6},{6,2},{1... | collective-permute-start | bytes 86024 | tf_op jit(solution)/shard_map/ppermute | solution.py:736
  11.9 3.5 %collective-permute-start.3 = (f32[80,128]{1,0:T(8,128)S(1)}, f32[80,128]{1,0:T(8,128)S(1)}, u32[]{:S(2)}, u32[]{:S(2)}) collective-permute-start(f32[80,128]{1,0:T(8,128)S(1)} %shard_map.79.after_ref.m2_ref), channel_id=1, source_target_pairs={{4,8},{8,4},{12,0},{0,12},{5,9},{9,5},{13,1},{1,13},{6,10},{10,6},... | collective-permute-start | bytes 122888 | tf_op jit(solution)/shard_map/ppermute | solution.py:748
  15.4 4.1 %collective-permute-start.4 = (f32[4,24,128]{2,1,0:T(8,128)S(1)}, f32[4,24,128]{2,1,0:T(8,128)S(1)}, u32[]{:S(2)}, u32[]{:S(2)}) collective-permute-start(f32[4,24,128]{2,1,0:T(8,128)S(1)} %shard_map.81), channel_id=1, source_target_pairs={{0,16},{16,0},{1,17},{17,1},{2,18},{18,2},{3,19},{19,3},{4,20},{20... | collective-permute-start | bytes 147464 | tf_op jit(solution)/shard_map/ppermute | solution.py:755

commit v5 on v4

--- a/solution.py
+++ b/solution.py
@@ -118,7 +118,7 @@
     row = lax.axis_index("row")
     circ = lax.axis_index("circ")
     span = lax.axis_index("span")
-    return row, lax.rem(circ, 2) == 0, lax.rem(span, 2) == 0, span
+    return row, lax.rem(circ, 2) == 0, row == 0, span
 
 
 def first_kernel(
@@ -169,6 +169,7 @@
 
 def thin_kernel(C, T, u_ref, f_ref, ha_ref, hb_ref, m1_ref, m2_ref, t_ref):
     row, even_c, even_s, _ = place()
+    even_s = jnp.logical_not(even_s)
     rotor = row == 0
     width = u_ref.shape[3]
     half = pl.ds(pl.multiple_of(jnp.where(rotor, width - LANES, 0), LANES), LANES)
@@ -235,7 +236,8 @@
 
 class Halo:
     def __init__(self, C, ha, hb, pa, pb):
-        _, self.even_c, self.even_s, _ = place()
+        _, self.even_c, even_s, _ = place()
+        self.even_s = jnp.logical_not(even_s)
         self.C, self.ha, self.hb, self.pa, self.pb = C, ha, hb, pa, pb
 
     def left(self, slot, rows=slice(None)):
@@ -700,6 +702,12 @@
     return route
 
 
+def snake(count, turn):
+    order = [span for span in range(count)] + [2 * count - 1 - span for span in range(count)]
+    n = len(order)
+    return [(order[i], order[(i + turn) % n]) for i in range(n)]
+
+
 def body(density, velocity, pressure, blade_force, offsets, weights):
     C, T, A = density.shape[1:]
     nc = lax.axis_size("circ")
@@ -720,8 +728,8 @@
             pltpu.SemaphoreType.DMA((6,)),
         ],
     )
-    ha = lax.ppermute(sa, "span", pairs(ns, 0, False))
-    hb = lax.ppermute(sb, "span", pairs(ns, 1, False))
+    ha = lax.ppermute(sa, ("row", "span"), snake(ns, 1))
+    hb = lax.ppermute(sb, ("row", "span"), snake(ns, -1))
     pa = lax.ppermute(pa, "circ", pairs(nc, 0, True))
     pb = lax.ppermute(pb, "circ", pairs(nc, 1, True))
 

time: 22.6 us -> 22.1 us (0.978)
  the two profiles are of different devices: /device:TPU:16 before, /device:TPU:0 now
where the time goes in v5:
time: 22.1 us; the launch traced here: 22 us
  Pallas kernels  8.43 us (38%)
  starting transfers between devices  6.76 us (31%)
  waiting for transfers between devices  6.13 us (28%)
  between operations  0.67 us (3%)
    pallas_call x7, Pallas kernels, call(): pl.pallas_call(kernel, out_shape=[jax.ShapeDtypeStruct(s.shape, s.dtype)...  8.43 us
    ppermute x1, starting transfers between devices, body(): ha = lax.ppermute(sa, ('row', 'span'), snake(ns, 1))  3.1 us
    ppermute x1, starting transfers between devices, body(): pb = lax.ppermute(pb, 'circ', pairs(nc, 1, True))  2.04 us
    ppermute x1, waiting for transfers between devices, body(): hb = lax.ppermute(sb, ('row', 'span'), snake(ns, -1))  1.79 us
    ppermute x1, starting transfers between devices, body(): got = lax.ppermute(m2, 'circ', pairs(nc, 1, True))  1.26 us
    ppermute x1, waiting for transfers between devices, body(): m1 = lax.ppermute(m1, 'circ', pairs(nc, 0, True))  1.19 us
    ppermute x1, waiting for transfers between devices, body(): partner = lax.ppermute(ring, 'row', [(0, 1), (1, 0)])  1.18 us
    ppermute x1, waiting for transfers between devices, body(): got = lax.ppermute(m2, 'circ', pairs(nc, 1, True))  1.1 us
  transfers between devices with their start and end apart: 7, of which 5 were waited for; matrix products, arithmetic and copies ran while one was open for 0% of the time, Pallas kernels for 19%

profile of v5, /device:TPU:0, one launch (start us, length us, event | category | flops | bytes accessed | tf_op | source)
XLA Modules:
  0.0 22.0 jit_solution(1051032313318426878)
XLA Ops:
  0.6 1.4 %shard_map.77 = (f32[5,8,16,256]{3,2,1,0:T(8,128)S(1)}, f32[3,8,16,256]{3,2,1,0:T(8,128)S(1)}, s32[2]{0:T(128)S(1)}, f32[2,4]{1,0:T(2,128)S(1)}, f32[13,8,256]{2...) custom-call(f32[8,16,256]{2,1,0:T(8,128)} %bitcast.13, ...), custom_call_target="tpu_custom_call" | custom-call | tf_op jit(solution)/shard_map/pallas_call | solution.py:26
  2.1 3.1 %collective-permute-start = (f32[13,8,256]{2,1,0:T(8,128)S(1)}, f32[13,8,256]{2,1,0:T(8,128)S(1)}, u32[]{:S(2)}, u32[]{:S(2)}) collective-permute-start(f32[13,8,256]{2,1,0:T(8,128)S(1)} %get-tuple-element.23), channel_id=1, source_target_pairs={{0,1},{1,2},{2,3},{3,19},{19,18},{18,17},{17,16},{16,0},{4,5},{5,6... | collective-permute-start | bytes 319496 | tf_op jit(solution)/shard_map/ppermute | solution.py:731
  5.2 0.0 collective-permute-start.1
  5.2 0.0 collective-permute-start.5
  5.2 2.0 %collective-permute-start.6 = (f32[13,16,256]{2,1,0:T(8,128)S(1)}, f32[13,16,256]{2,1,0:T(8,128)S(1)}, u32[]{:S(2)}, u32[]{:S(2)}) collective-permute-start(f32[13,16,256]{2,1,0:T(8,128)S(1)} %get-tuple-element.28), channel_id=1, source_target_pairs={{4,8},{8,4},{12,0},{0,12},{5,9},{9,5},{13,1},{1,13},{6,10},{10,6},... | collective-permute-start | bytes 638984 | tf_op jit(solution)/shard_map/ppermute | solution.py:734
  7.2 0.9 %collective-permute-done.ha_ref = f32[13,8,256]{2,1,0:T(8,128)S(1)} collective-permute-done((f32[13,8,256]{2,1,0:T(8,128)S(1)}, f32[13,8,256]{2,1,0:T(8,128)S(1)}, u32[]{:S(2)}, u32[]{:S(2)}) %collective-permute-start) | collective-permute-done | bytes 106528 | tf_op jit(solution)/shard_map/ppermute | solution.py:731
  8.1 1.8 %collective-permute-done.1.hb_ref = f32[13,8,256]{2,1,0:T(8,128)S(1)} collective-permute-done((f32[13,8,256]{2,1,0:T(8,128)S(1)}, f32[13,8,256]{2,1,0:T(8,128)S(1)}, u32[]{:S(2)}, u32[]{:S(2)}) %collective-permute-start.1) | collective-permute-done | bytes 106528 | tf_op jit(solution)/shard_map/ppermute | solution.py:732
  9.9 0.4 %shard_map.78 = (f32[56,128]{1,0:T(8,128)S(1)}, f32[80,128]{1,0:T(8,128)S(1)}) custom-call(f32[5,8,16,256]{3,2,1,0:T(8,128)S(1)} %get-tuple-element.22.u_ref, f32[3,8,16,256]{3,2,1,0:T(8,128)S(1)} %get-tuple-element.21.f_ref, f32[13,8,256]{2,1,0:T(8,128)S(1)} %collective-permute-done.ha_ref, f32[13,8,256]{2,1,0:T(8,128)S(1)} %collective-permute-done.1.hb_ref), custom_call_target="tpu_custom_call" | custom-call | tf_op jit(solution)/shard_map/pallas_call | solution.py:26
  10.3 0.0 collective-permute-start.2
  10.3 1.2 %collective-permute-done.2.m1_ref = f32[56,128]{1,0:T(8,128)S(1)} collective-permute-done((f32[56,128]{1,0:T(8,128)S(1)}, f32[56,128]{1,0:T(8,128)S(1)}, u32[]{:S(2)}, u32[]{:S(2)}) %collective-permute-start.2) | collective-permute-done | bytes 28704 | tf_op jit(solution)/shard_map/ppermute | solution.py:744
  11.5 1.3 %collective-permute-start.3 = (f32[80,128]{1,0:T(8,128)S(1)}, f32[80,128]{1,0:T(8,128)S(1)}, u32[]{:S(2)}, u32[]{:S(2)}) collective-permute-start(f32[80,128]{1,0:T(8,128)S(1)} %shard_map.79.after_ref.m2_ref), channel_id=1, source_target_pairs={{4,8},{8,4},{12,0},{0,12},{5,9},{9,5},{13,1},{1,13},{6,10},{10,6},... | collective-permute-start | bytes 122888 | tf_op jit(solution)/shard_map/ppermute | solution.py:756
  12.8 1.1 %shard_map.80.after_ref.one_ref = f32[5,8,16,256]{3,2,1,0:T(8,128)S(1)} custom-call(f32[5,8,16,256]{3,2,1,0:T(8,128)S(1)} %get-tuple-element.22.u_ref, f32[3,8,16,256]{3,2,1,0:T(8,128)S(1)} %get-tuple-element.21.f_ref, f32[13,8,256]{2,1,0:T(8,128)S(1)} %collective-permute-done.ha_ref, f32[13,8,256]{2,1,0:T(8,128)S(1)} %collective-permute-done.1.hb_ref, ...), custom_call_target="tpu_custom_call" | custom-call | flops 10000000 | bytes 4000000 | tf_op jit(solution)/shard_map/pallas_call | solution.py:26
  13.9 1.1 %collective-permute-done.3.got_ref.m2_ref = f32[80,128]{1,0:T(8,128)S(1)} collective-permute-done((f32[80,128]{1,0:T(8,128)S(1)}, f32[80,128]{1,0:T(8,128)S(1)}, u32[]{:S(2)}, u32[]{:S(2)}) %collective-permute-start.3) | collective-permute-done | bytes 40992 | tf_op jit(solution)/shard_map/ppermute | solution.py:756
  15.0 0.3 %collective-permute-start.4 = (f32[4,24,128]{2,1,0:T(8,128)S(1)}, f32[4,24,128]{2,1,0:T(8,128)S(1)}, u32[]{:S(2)}, u32[]{:S(2)}) collective-permute-start(f32[4,24,128]{2,1,0:T(8,128)S(1)} %shard_map.81), channel_id=1, source_target_pairs={{0,16},{16,0},{1,17},{17,1},{2,18},{18,2},{3,19},{19,3},{4,20},{20... | collective-permute-start | bytes 147464 | tf_op jit(solution)/shard_map/ppermute | solution.py:763
  15.3 0.0 collective-permute-done.5.pa_ref
  15.3 0.0 collective-permute-done.6.pb_ref
  15.3 2.6 %shard_map.82 = (f32[5,10,16,128]{3,2,1,0:T(8,128)S(1)}, f32[2,5,8,128]{3,2,1,0:T(8,128)S(1)}, f32[5,8,16,128]{3,2,1,0:T(8,128)S(1)}, f32[5,8,16,128]{3,2,1,0:T(8,128)S(1)}, f32[10,8,128]{2,1,0:T(8,128)S(1)}) custom-call(s32[2]{0:T(128)S(1)} %get-tuple-element.19.off_ref, f32[2,4]{1,0:T(2,128)S(1)} %get-tuple-element.20.wt_ref, ...), custom_call_target="tpu_custom_call" | custom-call | flops 10000000 | bytes 4000000 | tf_op jit(solution)/shard_map/pallas_call | solution.py:26
  17.9 1.2 %collective-permute-done.4 = f32[4,24,128]{2,1,0:T(8,128)S(1)} collective-permute-done((f32[4,24,128]{2,1,0:T(8,128)S(1)}, f32[4,24,128]{2,1,0:T(8,128)S(1)}, u32[]{:S(2)}, u32[]{:S(2)}) %collective-permute-start.4) | collective-permute-done | bytes 49184 | tf_op jit(solution)/shard_map/ppermute | solution.py:763
  19.1 2.9 %shard_map.83 = (f32[5,8,16,256]{3,2,1,0:T(8,128)}, f32[2,5,8,16]{3,2,1,0:T(8,128)}) custom-call(s32[2]{0:T(128)S(1)} %get-tuple-element.19.off_ref, f32[2,4]{1,0:T(2,128)S(1)} %get-tuple-element.20.wt_ref, f32[3,8,16,256]{3,2,1,0:T(8,128)S(1)} %get-tuple-element.21.f_ref, f32[96,128]{1,0:T(8,128)S(1)} %bitcast.9, f32[96,128]{1,0:T(8,128)S(1)} %bitcast.10, ...), custom_call_target="tpu_custom_call" | custom-call | tf_op jit(solution)/shard_map/pallas_call | solution.py:26
  (2 shorter events, 0.0 us)
Async XLA Ops:
  2.1 6.0 %collective-permute-start = (f32[13,8,256]{2,1,0:T(8,128)S(1)}, f32[13,8,256]{2,1,0:T(8,128)S(1)}, u32[]{:S(2)}, u32[]{:S(2)}) collective-permute-start(f32[13,8,256]{2,1,0:T(8,128)S(1)} %get-tuple-element.23), channel_id=1, source_target_pairs={{0,1},{1,2},{2,3},{3,19},{19,18},{18,17},{17,16},{16,0},{4,5},{5,6... | collective-permute-start | bytes 319496 | tf_op jit(solution)/shard_map/ppermute | solution.py:731
  5.2 4.7 %collective-permute-start.1 = (f32[13,8,256]{2,1,0:T(8,128)S(1)}, f32[13,8,256]{2,1,0:T(8,128)S(1)}, u32[]{:S(2)}, u32[]{:S(2)}) collective-permute-start(f32[13,8,256]{2,1,0:T(8,128)S(1)} %get-tuple-element.24), channel_id=1, source_target_pairs={{0,16},{1,0},{2,1},{3,2},{19,3},{18,19},{17,18},{16,17},{4,20},{5,... | collective-permute-start | bytes 319496 | tf_op jit(solution)/shard_map/ppermute | solution.py:732
  5.2 10.1 %collective-permute-start.5 = (f32[13,16,256]{2,1,0:T(8,128)S(1)}, f32[13,16,256]{2,1,0:T(8,128)S(1)}, u32[]{:S(2)}, u32[]{:S(2)}) collective-permute-start(f32[13,16,256]{2,1,0:T(8,128)S(1)} %get-tuple-element.27), channel_id=1, source_target_pairs={{0,4},{4,0},{8,12},{12,8},{1,5},{5,1},{9,13},{13,9},{2,6},{6,2},{1... | collective-permute-start | bytes 638984 | tf_op jit(solution)/shard_map/ppermute | solution.py:733
  5.2 10.1 %collective-permute-start.6 = (f32[13,16,256]{2,1,0:T(8,128)S(1)}, f32[13,16,256]{2,1,0:T(8,128)S(1)}, u32[]{:S(2)}, u32[]{:S(2)}) collective-permute-start(f32[13,16,256]{2,1,0:T(8,128)S(1)} %get-tuple-element.28), channel_id=1, source_target_pairs={{4,8},{8,4},{12,0},{0,12},{5,9},{9,5},{13,1},{1,13},{6,10},{10,6},... | collective-permute-start | bytes 638984 | tf_op jit(solution)/shard_map/ppermute | solution.py:734
  10.3 1.2 %collective-permute-start.2 = (f32[56,128]{1,0:T(8,128)S(1)}, f32[56,128]{1,0:T(8,128)S(1)}, u32[]{:S(2)}, u32[]{:S(2)}) collective-permute-start(f32[56,128]{1,0:T(8,128)S(1)} %get-tuple-element.25), channel_id=1, source_target_pairs={{0,4},{4,0},{8,12},{12,8},{1,5},{5,1},{9,13},{13,9},{2,6},{6,2},{1... | collective-permute-start | bytes 86024 | tf_op jit(solution)/shard_map/ppermute | solution.py:744
  11.5 3.5 %collective-permute-start.3 = (f32[80,128]{1,0:T(8,128)S(1)}, f32[80,128]{1,0:T(8,128)S(1)}, u32[]{:S(2)}, u32[]{:S(2)}) collective-permute-start(f32[80,128]{1,0:T(8,128)S(1)} %shard_map.79.after_ref.m2_ref), channel_id=1, source_target_pairs={{4,8},{8,4},{12,0},{0,12},{5,9},{9,5},{13,1},{1,13},{6,10},{10,6},... | collective-permute-start | bytes 122888 | tf_op jit(solution)/shard_map/ppermute | solution.py:756
  15.0 4.1 %collective-permute-start.4 = (f32[4,24,128]{2,1,0:T(8,128)S(1)}, f32[4,24,128]{2,1,0:T(8,128)S(1)}, u32[]{:S(2)}, u32[]{:S(2)}) collective-permute-start(f32[4,24,128]{2,1,0:T(8,128)S(1)} %shard_map.81), channel_id=1, source_target_pairs={{0,16},{16,0},{1,17},{17,1},{2,18},{18,2},{3,19},{19,3},{4,20},{20... | collective-permute-start | bytes 147464 | tf_op jit(solution)/shard_map/ppermute | solution.py:763

commit v6 on v5

--- a/solution.py
+++ b/solution.py
@@ -124,7 +124,7 @@
 def first_kernel(
     C, T,
     rho_hbm, v_hbm, p_hbm, f_hbm, off_hbm, wt_hbm,
-    u_ref, f_ref, off_ref, wt_ref, sa_ref, sb_ref, pa_ref, pb_ref,
+    u_ref, f_ref, off_ref, wt_ref, ta_ref, tb_ref, sa_ref, sb_ref, pa_ref, pb_ref,
     rho_ref, v_ref, p_ref, sem,
 ):
     copies = [
@@ -143,6 +143,35 @@
         for k in range(5):
             u_ref[k, c] = u[k]
 
+    rotor = lax.axis_index("row") == 0
+    width = u_ref.shape[3]
+    half = pl.ds(pl.multiple_of(jnp.where(rotor, width - LANES, 0), LANES), LANES)
+    end = jnp.where(rotor, LANES - 1, 0)
+    small = lax.broadcasted_iota(jnp.int32, (C, LANES), 1)
+
+    def pick(ref, rows, low, high):
+        ref[0][rows, :] = jnp.where(even_s, high, low)
+        ref[1][rows, :] = jnp.where(even_s, low, high)
+
+    thin = ta_ref, tb_ref
+    tiles = []
+    for s in (0, T - 1):
+        tile = jnp.zeros((C, LANES), jnp.float32)
+        for k in range(5):
+            x = pltpu.roll(u_ref[k, :, s, half], lax.rem(13 + k - end + LANES, LANES), 1)
+            tile = jnp.where(small == 13 + k, x, tile)
+        tiles.append(tile)
+    pick(thin, slice(0, C), *tiles)
+    for part in range(width // LANES):
+        lanes = slice(part * LANES, (part + 1) * LANES)
+        base = C + 16 * part
+        for k in range(5):
+            for e, c in enumerate((0, C - 1)):
+                r = base + 2 * k + e
+                pick(thin, slice(r, r + 1), u_ref[k, c, 0:1, lanes], u_ref[k, c, T - 1 : T, lanes])
+        zero = jnp.zeros((6, LANES), jnp.float32)
+        pick(thin, slice(base + 10, base + 16), zero, zero)
+
     def row(k, s):
         ref = u_ref.at[k] if k < 5 else f_ref.at[k - 5]
         return ref[:, s, :]
@@ -192,11 +221,9 @@
     for start, is_low in ((0, True), (T - 1, False)):
         where_a = even_s if not is_low else jnp.logical_not(even_s)
         rows = pl.ds(start, C, stride=T)
-        x = t_ref[rows, :]
-        for k in range(5):
-            h = jnp.where(where_a, ha_ref[k, :, half], hb_ref[k, :, half])
-            x = jnp.where(small == 13 + k, put(h, 13 + k, end), x)
-        t_ref[rows, :] = x
+        x = jnp.where(where_a, ha_ref[0:C, :], hb_ref[0:C, :])
+        edge_lane = jnp.logical_and(small >= 13, small < 18)
+        t_ref[rows, :] = jnp.where(edge_lane, x, t_ref[rows, :])
     planes = t_ref[...].T[:ROWS]
     m1_ref[0:ROWS, :] = planes
     m2_ref[0:ROWS, :] = planes
@@ -206,10 +233,10 @@
         for k in range(5):
             for side in range(2):
                 where_a = even_s if side == 1 else jnp.logical_not(even_s)
-                x = jnp.where(where_a, ha_ref[k, pl.ds(c, 1), :], hb_ref[k, pl.ds(c, 1), :])
                 for part in range(width // LANES):
                     r = base + 16 * part + 2 * k + side
-                    ref[r : r + 1, :] = x[:, part * LANES : (part + 1) * LANES]
+                    q = pl.ds(C + 16 * part + 2 * k + jnp.where(c == 0, 0, 1), 1)
+                    ref[r : r + 1, :] = jnp.where(where_a, ha_ref[q, :], hb_ref[q, :])
         for part in range(width // LANES):
             r = base + 16 * part
             ref[r + 10 : r + 16, :] = jnp.zeros((6, LANES), jnp.float32)
@@ -297,21 +324,14 @@
     return span == 0, span == ns - 1
 
 
-def bulk_kernel(C, T, ns, u_ref, f_ref, ha_ref, hb_ref, after_ref, one_ref, edge_s):
+def bulk_kernel(C, u_ref, f_ref, after_ref, one_ref):
     rotor = lax.axis_index("row") == 0
-    halo = Halo(C, ha_ref, hb_ref, None, None)
-    for side, wall in enumerate(walls(ns)):
-        inner = Cell([u_ref[k, :, 0 if side == 0 else T - 1, :] for k in range(5)])
-        outer = Cell([halo.beyond(side, k) for k in range(5)])
-        edge, _ = edge_faces(side, outer, inner, wall)
-        for k in range(5):
-            edge_s[side, k] = edge[k]
 
     def axial(c, cell):
         return axial_faces(cell, [0.0] * 5, rotor)
 
     def edges(c):
-        return [[edge_s[side, k, c : c + 1, :] for k in range(5)] for side in range(2)]
+        return [[jnp.zeros((1, u_ref.shape[3]), jnp.float32)] * 5] * 2
 
     def store(c, u):
         for k in range(5):
@@ -535,15 +555,21 @@
     sweep(load, -1, 1, axial, edges, force_of, store)
     sweep(load, C - 1, C + 1, axial, edges, force_of, store)
 
+    span_row = lax.broadcasted_iota(jnp.int32, (T, LANES), 0)
+
     def half(k, c, start):
         lanes = pl.ds(start, LANES)
         if c in slots:
             return col_s[k, slots[c], :, lanes]
-        return one_ref[k, c, :, lanes]
+        low_face = jnp.broadcast_to(edge_s[0, k, c : c + 1, lanes], (T, LANES))
+        top_face = jnp.broadcast_to(edge_s[1, k, c : c + 1, lanes], (T, LANES))
+        gain = jnp.where(span_row == 0, low_face, jnp.where(span_row == T - 1, -top_face, 0.0))
+        return one_ref[k, c, :, lanes] + (0.5 * STEP) * gain
 
     def across(k, s0):
         lanes = pl.ds(far, LANES)
-        mid = one_ref[k, :, s0, lanes]
+        gain = edge_s[0, k, 0:C, lanes] if s0 == 0 else -edge_s[1, k, 0:C, lanes]
+        mid = one_ref[k, :, s0, lanes] + (0.5 * STEP) * gain
         c = lax.broadcasted_iota(jnp.int32, mid.shape, 0)
         ends = [jnp.broadcast_to(col_s[k, slots[e], s0 : s0 + 1, lanes], mid.shape) for e in (0, C - 1)]
         return jnp.where(c == 0, ends[0], jnp.where(c == C - 1, ends[1], mid))
@@ -716,9 +742,10 @@
     assert area == LANES and nc % 2 == 0 and A == 2 * LANES and C == 8
     rho, v, p, force = density[0], velocity[0], pressure[0], blade_force[0]
 
-    u, force, off, wt, sa, sb, pa, pb = call(
+    thin = 16 * (A // LANES)
+    u, force, off, wt, ta, tb, sa, sb, pa, pb = call(
         functools.partial(first_kernel, C, T),
-        [(5, C, T, A), (3, C, T, A), offsets, weights, (13, C, A), (13, C, A), (13, T, A), (13, T, A)],
+        [(5, C, T, A), (3, C, T, A), offsets, weights, (C + thin, LANES), (C + thin, LANES), (13, C, A), (13, C, A), (13, T, A), (13, T, A)],
         [pltpu.with_memory_space_constraint(x, pltpu.HBM) for x in (rho, v, p, force, offsets, weights)],
         specs=[hbm()] * 6,
         scratch=[
@@ -728,16 +755,17 @@
             pltpu.SemaphoreType.DMA((6,)),
         ],
     )
+    ta = lax.ppermute(ta, ("row", "span"), snake(ns, 1))
+    tb = lax.ppermute(tb, ("row", "span"), snake(ns, -1))
     ha = lax.ppermute(sa, ("row", "span"), snake(ns, 1))
     hb = lax.ppermute(sb, ("row", "span"), snake(ns, -1))
     pa = lax.ppermute(pa, "circ", pairs(nc, 0, True))
     pb = lax.ppermute(pb, "circ", pairs(nc, 1, True))
 
-    thin = 2 * 16 * (A // LANES) // 2
     m1, m2 = call(
         functools.partial(thin_kernel, C, T),
         [(ROWS + thin, LANES), (2 * ROWS + thin, LANES)],
-        (u, force, ha, hb),
+        (u, force, ta, tb),
         scratch=[pltpu.VMEM((area, LANES), jnp.float32)],
     )
     planes = m1[:ROWS]
@@ -746,10 +774,9 @@
     if nc == 4:
         (m2,) = call(fill_kernel, [m2.shape], (m1, m2), aliases={1: 0})
     (one,) = call(
-        functools.partial(bulk_kernel, C, T, ns),
+        functools.partial(bulk_kernel, C),
         [(5, C, T, A)],
-        (u, force, ha, hb, m2),
-        scratch=[pltpu.VMEM((2, 5, C, A), f32)],
+        (u, force, m2),
         cost=pl.CostEstimate(flops=10_000_000, bytes_accessed=4_000_000, transcendentals=0),
     )
     if nc == 4:

time: 22.1 us -> 24.2 us (1.095)
  waiting for transfers between devices: 6.13 us -> 7.25 us
  starting transfers between devices: 6.76 us -> 7.83 us
    ppermute x0 -> x2, waiting for transfers between devices: none -> 3.33 us  [the longest x1 1.76 us: body(): ta = lax.ppermute(ta, ('row', 'span'), snake(ns, 1))]
    ppermute x0 -> x2, starting transfers between devices: none -> 2.03 us  [the longest x1 1.58 us: body(): ta = lax.ppermute(ta, ('row', 'span'), snake(ns, 1))]
    ppermute x1, waiting for transfers between devices: 1.1 us -> 2.83 us  [body(): got = lax.ppermute(m2, 'circ', pairs(nc, 1, True))]
    ppermute x1, waiting for transfers between devices: 1.79 us -> 0.25 us  [body(): hb = lax.ppermute(sb, ('row', 'span'), snake(ns, -1))]
    ppermute x1, starting transfers between devices: 3.1 us -> 1.63 us  [body(): ha = lax.ppermute(sa, ('row', 'span'), snake(ns, 1))]
    ppermute x1, waiting for transfers between devices: 1.19 us -> 0.01 us  [body(): m1 = lax.ppermute(m1, 'circ', pairs(nc, 0, True))]
    ppermute x1, starting transfers between devices: 1.26 us -> 0.09 us  [body(): got = lax.ppermute(m2, 'circ', pairs(nc, 1, True))]
    ppermute x1, waiting for transfers between devices: 0.86 us -> 0.01 us  [body(): ha = lax.ppermute(sa, ('row', 'span'), snake(ns, 1))]
  transfers between devices with their start and end apart: 7 -> 9, of which waited for: 5 -> 5; matrix products, arithmetic and copies ran while one was open for 0% -> 0% of each run, Pallas kernels for 19% -> 16%
where the time goes in v6:
time: 24.2 us; the launch traced here: 24 us
  Pallas kernels  8.28 us (34%)
  starting transfers between devices  7.83 us (32%)
  waiting for transfers between devices  7.25 us (30%)
  between operations  0.68 us (3%)
    pallas_call x7, Pallas kernels, call(): pl.pallas_call(kernel, out_shape=[jax.ShapeDtypeStruct(s.shape, s.dtype)...  8.28 us
    ppermute x1, waiting for transfers between devices, body(): got = lax.ppermute(m2, 'circ', pairs(nc, 1, True))  2.83 us
    ppermute x1, starting transfers between devices, body(): pb = lax.ppermute(pb, 'circ', pairs(nc, 1, True))  2.59 us
    ppermute x1, waiting for transfers between devices, body(): ta = lax.ppermute(ta, ('row', 'span'), snake(ns, 1))  1.76 us
    ppermute x1, starting transfers between devices, body(): ha = lax.ppermute(sa, ('row', 'span'), snake(ns, 1))  1.63 us
    ppermute x1, starting transfers between devices, body(): ta = lax.ppermute(ta, ('row', 'span'), snake(ns, 1))  1.58 us
    ppermute x1, waiting for transfers between devices, body(): tb = lax.ppermute(tb, ('row', 'span'), snake(ns, -1))  1.58 us
    ppermute x1, waiting for transfers between devices, body(): partner = lax.ppermute(ring, 'row', [(0, 1), (1, 0)])  0.83 us
  transfers between devices with their start and end apart: 9, of which 5 were waited for; matrix products, arithmetic and copies ran while one was open for 0% of the time, Pallas kernels for 16%

profile of v6, /device:TPU:0, one launch (start us, length us, event | category | flops | bytes accessed | tf_op | source)
XLA Modules:
  0.0 24.0 jit_solution(6598559867219331163)
XLA Ops:
  0.6 1.6 %shard_map.77 = (f32[5,8,16,256]{3,2,1,0:T(8,128)S(1)}, f32[3,8,16,256]{3,2,1,0:T(8,128)S(1)}, s32[2]{0:T(128)S(1)}, f32[2,4]{1,0:T(2,128)S(1)}, f32[40,128]{1,0...) custom-call(f32[8,16,256]{2,1,0:T(8,128)} %bitcast.13, ...), custom_call_target="tpu_custom_call" | custom-call | tf_op jit(solution)/shard_map/pallas_call | solution.py:26
  2.2 0.6 %collective-permute-start.7 = (f32[13,16,256]{2,1,0:T(8,128)S(1)}, f32[13,16,256]{2,1,0:T(8,128)S(1)}, u32[]{:S(2)}, u32[]{:S(2)}) collective-permute-start(f32[13,16,256]{2,1,0:T(8,128)S(1)} %get-tuple-element.31), channel_id=1, source_target_pairs={{0,4},{4,0},{8,12},{12,8},{1,5},{5,1},{9,13},{13,9},{2,6},{6,2},{1... | collective-permute-start | bytes 638984 | tf_op jit(solution)/shard_map/ppermute | solution.py:762
  2.8 2.6 %collective-permute-start.8 = (f32[13,16,256]{2,1,0:T(8,128)S(1)}, f32[13,16,256]{2,1,0:T(8,128)S(1)}, u32[]{:S(2)}, u32[]{:S(2)}) collective-permute-start(f32[13,16,256]{2,1,0:T(8,128)S(1)} %get-tuple-element.32), channel_id=1, source_target_pairs={{4,8},{8,4},{12,0},{0,12},{5,9},{9,5},{13,1},{1,13},{6,10},{10,6},... | collective-permute-start | bytes 638984 | tf_op jit(solution)/shard_map/ppermute | solution.py:763
  5.4 1.6 %collective-permute-start = (f32[40,128]{1,0:T(8,128)S(1)}, f32[40,128]{1,0:T(8,128)S(1)}, u32[]{:S(2)}, u32[]{:S(2)}) collective-permute-start(f32[40,128]{1,0:T(8,128)S(1)} %get-tuple-element.25), channel_id=1, source_target_pairs={{0,1},{1,2},{2,3},{3,19},{19,18},{18,17},{17,16},{16,0},{4,5},{5,6... | collective-permute-start | bytes 61448 | tf_op jit(solution)/shard_map/ppermute | solution.py:758
  6.9 0.4 %collective-permute-start.1 = (f32[40,128]{1,0:T(8,128)S(1)}, f32[40,128]{1,0:T(8,128)S(1)}, u32[]{:S(2)}, u32[]{:S(2)}) collective-permute-start(f32[40,128]{1,0:T(8,128)S(1)} %get-tuple-element.26), channel_id=1, source_target_pairs={{0,16},{1,0},{2,1},{3,2},{19,3},{18,19},{17,18},{16,17},{4,20},{5,... | collective-permute-start | bytes 61448 | tf_op jit(solution)/shard_map/ppermute | solution.py:759
  7.4 1.8 %collective-permute-done.ha_ref = f32[40,128]{1,0:T(8,128)S(1)} collective-permute-done((f32[40,128]{1,0:T(8,128)S(1)}, f32[40,128]{1,0:T(8,128)S(1)}, u32[]{:S(2)}, u32[]{:S(2)}) %collective-permute-start) | collective-permute-done | bytes 20512 | tf_op jit(solution)/shard_map/ppermute | solution.py:758
  9.1 1.6 %collective-permute-done.1.hb_ref = f32[40,128]{1,0:T(8,128)S(1)} collective-permute-done((f32[40,128]{1,0:T(8,128)S(1)}, f32[40,128]{1,0:T(8,128)S(1)}, u32[]{:S(2)}, u32[]{:S(2)}) %collective-permute-start.1) | collective-permute-done | bytes 20512 | tf_op jit(solution)/shard_map/ppermute | solution.py:759
  10.7 0.4 %shard_map.78 = (f32[56,128]{1,0:T(8,128)S(1)}, f32[80,128]{1,0:T(8,128)S(1)}) custom-call(f32[5,8,16,256]{3,2,1,0:T(8,128)S(1)} %get-tuple-element.24.u_ref, f32[3,8,16,256]{3,2,1,0:T(8,128)S(1)} %get-tuple-element.23.f_ref, f32[40,128]{1,0:T(8,128)S(1)} %collective-permute-done.ha_ref, f32[40,128]{1,0:T(8,128)S(1)} %collective-permute-done.1.hb_ref), custom_call_target="tpu_custom_call" | custom-call | tf_op jit(solution)/shard_map/pallas_call | solution.py:26
  11.1 0.0 collective-permute-start.2
  11.1 1.6 %collective-permute-start.5 = (f32[13,8,256]{2,1,0:T(8,128)S(1)}, f32[13,8,256]{2,1,0:T(8,128)S(1)}, u32[]{:S(2)}, u32[]{:S(2)}) collective-permute-start(f32[13,8,256]{2,1,0:T(8,128)S(1)} %get-tuple-element.29), channel_id=1, source_target_pairs={{0,1},{1,2},{2,3},{3,19},{19,18},{18,17},{17,16},{16,0},{4,5},{5,6... | collective-permute-start | bytes 319496 | tf_op jit(solution)/shard_map/ppermute | solution.py:760
  12.7 0.4 %collective-permute-start.6 = (f32[13,8,256]{2,1,0:T(8,128)S(1)}, f32[13,8,256]{2,1,0:T(8,128)S(1)}, u32[]{:S(2)}, u32[]{:S(2)}) collective-permute-start(f32[13,8,256]{2,1,0:T(8,128)S(1)} %get-tuple-element.30), channel_id=1, source_target_pairs={{0,16},{1,0},{2,1},{3,2},{19,3},{18,19},{17,18},{16,17},{4,20},{5,... | collective-permute-start | bytes 319496 | tf_op jit(solution)/shard_map/ppermute | solution.py:761
  13.2 0.0 collective-permute-done.2.m1_ref
  13.2 0.1 collective-permute-start.3
  13.3 0.9 %shard_map.80.after_ref.one_ref = f32[5,8,16,256]{3,2,1,0:T(8,128)S(1)} custom-call(f32[5,8,16,256]{3,2,1,0:T(8,128)S(1)} %get-tuple-element.24.u_ref, f32[3,8,16,256]{3,2,1,0:T(8,128)S(1)} %get-tuple-element.23.f_ref, f32[80,128]{1,0:T(8,128)S(1)} %shard_map.79.after_ref.m2_ref), custom_call_target="tpu_custom_call" | custom-call | flops 10000000 | bytes 4000000 | tf_op jit(solution)/shard_map/pallas_call | solution.py:26
  14.2 2.8 %collective-permute-done.3.got_ref.m2_ref = f32[80,128]{1,0:T(8,128)S(1)} collective-permute-done((f32[80,128]{1,0:T(8,128)S(1)}, f32[80,128]{1,0:T(8,128)S(1)}, u32[]{:S(2)}, u32[]{:S(2)}) %collective-permute-start.3) | collective-permute-done | bytes 40992 | tf_op jit(solution)/shard_map/ppermute | solution.py:783
  17.1 0.5 %collective-permute-start.4 = (f32[4,24,128]{2,1,0:T(8,128)S(1)}, f32[4,24,128]{2,1,0:T(8,128)S(1)}, u32[]{:S(2)}, u32[]{:S(2)}) collective-permute-start(f32[4,24,128]{2,1,0:T(8,128)S(1)} %shard_map.81), channel_id=1, source_target_pairs={{0,16},{16,0},{1,17},{17,1},{2,18},{18,2},{3,19},{19,3},{4,20},{20... | collective-permute-start | bytes 147464 | tf_op jit(solution)/shard_map/ppermute | solution.py:790
  17.5 0.0 collective-permute-done.5.ha_ref
  17.5 0.3 %collective-permute-done.6.hb_ref = f32[13,8,256]{2,1,0:T(8,128)S(1)} collective-permute-done((f32[13,8,256]{2,1,0:T(8,128)S(1)}, f32[13,8,256]{2,1,0:T(8,128)S(1)}, u32[]{:S(2)}, u32[]{:S(2)}) %collective-permute-start.6) | collective-permute-done | bytes 106528 | tf_op jit(solution)/shard_map/ppermute | solution.py:761
  17.8 0.0 collective-permute-done.7.pa_ref
  17.8 0.0 collective-permute-done.8.pb_ref
  17.8 2.5 %shard_map.82 = (f32[5,10,16,128]{3,2,1,0:T(8,128)S(1)}, f32[2,5,8,128]{3,2,1,0:T(8,128)S(1)}, f32[5,8,16,128]{3,2,1,0:T(8,128)S(1)}, f32[5,8,16,128]{3,2,1,0:T(8,128)S(1)}, f32[10,8,128]{2,1,0:T(8,128)S(1)}) custom-call(s32[2]{0:T(128)S(1)} %get-tuple-element.21.off_ref, f32[2,4]{1,0:T(2,128)S(1)} %get-tuple-element.22.wt_ref, ...), custom_call_target="tpu_custom_call" | custom-call | flops 10000000 | bytes 4000000 | tf_op jit(solution)/shard_map/pallas_call | solution.py:26
  20.3 0.8 %collective-permute-done.4 = f32[4,24,128]{2,1,0:T(8,128)S(1)} collective-permute-done((f32[4,24,128]{2,1,0:T(8,128)S(1)}, f32[4,24,128]{2,1,0:T(8,128)S(1)}, u32[]{:S(2)}, u32[]{:S(2)}) %collective-permute-start.4) | collective-permute-done | bytes 49184 | tf_op jit(solution)/shard_map/ppermute | solution.py:790
  21.2 2.9 %shard_map.83 = (f32[5,8,16,256]{3,2,1,0:T(8,128)}, f32[2,5,8,16]{3,2,1,0:T(8,128)}) custom-call(s32[2]{0:T(128)S(1)} %get-tuple-element.21.off_ref, f32[2,4]{1,0:T(2,128)S(1)} %get-tuple-element.22.wt_ref, f32[3,8,16,256]{3,2,1,0:T(8,128)S(1)} %get-tuple-element.23.f_ref, f32[96,128]{1,0:T(8,128)S(1)} %bitcast.9, f32[96,128]{1,0:T(8,128)S(1)} %bitcast.10, ...), custom_call_target="tpu_custom_call" | custom-call | tf_op jit(solution)/shard_map/pallas_call | solution.py:26
  (2 shorter events, 0.0 us)
Async XLA Ops:
  2.2 15.6 %collective-permute-start.7 = (f32[13,16,256]{2,1,0:T(8,128)S(1)}, f32[13,16,256]{2,1,0:T(8,128)S(1)}, u32[]{:S(2)}, u32[]{:S(2)}) collective-permute-start(f32[13,16,256]{2,1,0:T(8,128)S(1)} %get-tuple-element.31), channel_id=1, source_target_pairs={{0,4},{4,0},{8,12},{12,8},{1,5},{5,1},{9,13},{13,9},{2,6},{6,2},{1... | collective-permute-start | bytes 638984 | tf_op jit(solution)/shard_map/ppermute | solution.py:762
  2.8 15.0 %collective-permute-start.8 = (f32[13,16,256]{2,1,0:T(8,128)S(1)}, f32[13,16,256]{2,1,0:T(8,128)S(1)}, u32[]{:S(2)}, u32[]{:S(2)}) collective-permute-start(f32[13,16,256]{2,1,0:T(8,128)S(1)} %get-tuple-element.32), channel_id=1, source_target_pairs={{4,8},{8,4},{12,0},{0,12},{5,9},{9,5},{13,1},{1,13},{6,10},{10,6},... | collective-permute-start | bytes 638984 | tf_op jit(solution)/shard_map/ppermute | solution.py:763
  5.4 3.8 %collective-permute-start = (f32[40,128]{1,0:T(8,128)S(1)}, f32[40,128]{1,0:T(8,128)S(1)}, u32[]{:S(2)}, u32[]{:S(2)}) collective-permute-start(f32[40,128]{1,0:T(8,128)S(1)} %get-tuple-element.25), channel_id=1, source_target_pairs={{0,1},{1,2},{2,3},{3,19},{19,18},{18,17},{17,16},{16,0},{4,5},{5,6... | collective-permute-start | bytes 61448 | tf_op jit(solution)/shard_map/ppermute | solution.py:758
  6.9 3.8 %collective-permute-start.1 = (f32[40,128]{1,0:T(8,128)S(1)}, f32[40,128]{1,0:T(8,128)S(1)}, u32[]{:S(2)}, u32[]{:S(2)}) collective-permute-start(f32[40,128]{1,0:T(8,128)S(1)} %get-tuple-element.26), channel_id=1, source_target_pairs={{0,16},{1,0},{2,1},{3,2},{19,3},{18,19},{17,18},{16,17},{4,20},{5,... | collective-permute-start | bytes 61448 | tf_op jit(solution)/shard_map/ppermute | solution.py:759
  11.1 2.1 %collective-permute-start.2 = (f32[56,128]{1,0:T(8,128)S(1)}, f32[56,128]{1,0:T(8,128)S(1)}, u32[]{:S(2)}, u32[]{:S(2)}) collective-permute-start(f32[56,128]{1,0:T(8,128)S(1)} %get-tuple-element.27), channel_id=1, source_target_pairs={{0,4},{4,0},{8,12},{12,8},{1,5},{5,1},{9,13},{13,9},{2,6},{6,2},{1... | collective-permute-start | bytes 86024 | tf_op jit(solution)/shard_map/ppermute | solution.py:772
  11.1 6.4 %collective-permute-start.5 = (f32[13,8,256]{2,1,0:T(8,128)S(1)}, f32[13,8,256]{2,1,0:T(8,128)S(1)}, u32[]{:S(2)}, u32[]{:S(2)}) collective-permute-start(f32[13,8,256]{2,1,0:T(8,128)S(1)} %get-tuple-element.29), channel_id=1, source_target_pairs={{0,1},{1,2},{2,3},{3,19},{19,18},{18,17},{17,16},{16,0},{4,5},{5,6... | collective-permute-start | bytes 319496 | tf_op jit(solution)/shard_map/ppermute | solution.py:760
  12.7 5.0 %collective-permute-start.6 = (f32[13,8,256]{2,1,0:T(8,128)S(1)}, f32[13,8,256]{2,1,0:T(8,128)S(1)}, u32[]{:S(2)}, u32[]{:S(2)}) collective-permute-start(f32[13,8,256]{2,1,0:T(8,128)S(1)} %get-tuple-element.30), channel_id=1, source_target_pairs={{0,16},{1,0},{2,1},{3,2},{19,3},{18,19},{17,18},{16,17},{4,20},{5,... | collective-permute-start | bytes 319496 | tf_op jit(solution)/shard_map/ppermute | solution.py:761
  13.2 3.9 %collective-permute-start.3 = (f32[80,128]{1,0:T(8,128)S(1)}, f32[80,128]{1,0:T(8,128)S(1)}, u32[]{:S(2)}, u32[]{:S(2)}) collective-permute-start(f32[80,128]{1,0:T(8,128)S(1)} %shard_map.79.after_ref.m2_ref), channel_id=1, source_target_pairs={{4,8},{8,4},{12,0},{0,12},{5,9},{9,5},{13,1},{1,13},{6,10},{10,6},... | collective-permute-start | bytes 122888 | tf_op jit(solution)/shard_map/ppermute | solution.py:783
  17.1 4.1 %collective-permute-start.4 = (f32[4,24,128]{2,1,0:T(8,128)S(1)}, f32[4,24,128]{2,1,0:T(8,128)S(1)}, u32[]{:S(2)}, u32[]{:S(2)}) collective-permute-start(f32[4,24,128]{2,1,0:T(8,128)S(1)} %shard_map.81), channel_id=1, source_target_pairs={{0,16},{16,0},{1,17},{17,1},{2,18},{18,2},{3,19},{19,3},{4,20},{20... | collective-permute-start | bytes 147464 | tf_op jit(solution)/shard_map/ppermute | solution.py:790

commit v7 on v6

--- a/solution.py
+++ b/solution.py
@@ -124,7 +124,7 @@
 def first_kernel(
     C, T,
     rho_hbm, v_hbm, p_hbm, f_hbm, off_hbm, wt_hbm,
-    u_ref, f_ref, off_ref, wt_ref, ta_ref, tb_ref, sa_ref, sb_ref, pa_ref, pb_ref,
+    u_ref, f_ref, off_ref, wt_ref, ta_ref, tb_ref,
     rho_ref, v_ref, p_ref, sem,
 ):
     copies = [
@@ -135,7 +135,7 @@
     ]
     for copy in copies:
         copy.start()
-    _, even_c, even_s, _ = place()
+    _, _, even_s, _ = place()
     for copy in copies:
         copy.wait()
     for c in range(C):
@@ -171,6 +171,10 @@
                 pick(thin, slice(r, r + 1), u_ref[k, c, 0:1, lanes], u_ref[k, c, T - 1 : T, lanes])
         zero = jnp.zeros((6, LANES), jnp.float32)
         pick(thin, slice(base + 10, base + 16), zero, zero)
+
+
+def pack_kernel(C, T, u_ref, f_ref, after_ref, sa_ref, sb_ref, pa_ref, pb_ref):
+    _, even_c, even_s, _ = place()
 
     def row(k, s):
         ref = u_ref.at[k] if k < 5 else f_ref.at[k - 5]
@@ -743,9 +747,9 @@
     rho, v, p, force = density[0], velocity[0], pressure[0], blade_force[0]
 
     thin = 16 * (A // LANES)
-    u, force, off, wt, ta, tb, sa, sb, pa, pb = call(
+    u, force, off, wt, ta, tb = call(
         functools.partial(first_kernel, C, T),
-        [(5, C, T, A), (3, C, T, A), offsets, weights, (C + thin, LANES), (C + thin, LANES), (13, C, A), (13, C, A), (13, T, A), (13, T, A)],
+        [(5, C, T, A), (3, C, T, A), offsets, weights, (C + thin, LANES), (C + thin, LANES)],
         [pltpu.with_memory_space_constraint(x, pltpu.HBM) for x in (rho, v, p, force, offsets, weights)],
         specs=[hbm()] * 6,
         scratch=[
@@ -754,6 +758,12 @@
             pltpu.VMEM((C, T, A), jnp.float32),
             pltpu.SemaphoreType.DMA((6,)),
         ],
+    )
+    sa, sb, pa, pb = call(
+        functools.partial(pack_kernel, C, T),
+        [(13, C, A), (13, C, A), (13, T, A), (13, T, A)],
+        (u, force, ta),
+        cost=pl.CostEstimate(flops=1_000_000, bytes_accessed=1_000_000, transcendentals=0),
     )
     ta = lax.ppermute(ta, ("row", "span"), snake(ns, 1))
     tb = lax.ppermute(tb, ("row", "span"), snake(ns, -1))

time: 24.2 us -> 24.3 us (level)
  starting transfers between devices: 7.83 us -> 8.96 us
  waiting for transfers between devices: 7.25 us -> 6.12 us
    ppermute x1, starting transfers between devices: 0.45 us -> 1.58 us  [body(): partner = lax.ppermute(ring, 'row', [(0, 1), (1, 0)])]
    ppermute x1, starting transfers between devices: 1.58 us -> 0.51 us  [body(): ta = lax.ppermute(ta, ('row', 'span'), snake(ns, 1))]
    ppermute x1, starting transfers between devices: 0.45 us -> 1.52 us  [body(): hb = lax.ppermute(sb, ('row', 'span'), snake(ns, -1))]
    ppermute x1, starting transfers between devices: 1.63 us -> 0.56 us  [body(): ha = lax.ppermute(sa, ('row', 'span'), snake(ns, 1))]
    ppermute x1, starting transfers between devices: 0.45 us -> 1.52 us  [body(): tb = lax.ppermute(tb, ('row', 'span'), snake(ns, -1))]
    ppermute x1, waiting for transfers between devices: 0.83 us -> 0.01 us  [body(): partner = lax.ppermute(ring, 'row', [(0, 1), (1, 0)])]
    ppermute x1, waiting for transfers between devices: 0.25 us -> 0.01 us  [body(): hb = lax.ppermute(sb, ('row', 'span'), snake(ns, -1))]
    pallas_call x7 -> x8, Pallas kernels: 8.28 us -> 8.41 us  [call(): pl.pallas_call(kernel, out_shape=[jax.ShapeDtypeStruct(s.shape, s.dtype)...]
  transfers between devices with their start and end apart: 9 -> 9, of which waited for: 5 -> 3; matrix products, arithmetic and copies ran while one was open for 0% -> 0% of each run, Pallas kernels for 16% -> 16%
where the time goes in v7:
time: 24.3 us; the launch traced here: 24.2 us
  starting transfers between devices  8.96 us (37%)
  Pallas kernels  8.41 us (35%)
  waiting for transfers between devices  6.12 us (25%)
  between operations  0.7 us (3%)
    pallas_call x8, Pallas kernels, call(): pl.pallas_call(kernel, out_shape=[jax.ShapeDtypeStruct(s.shape, s.dtype)...  8.41 us
    ppermute x1, waiting for transfers between devices, body(): got = lax.ppermute(m2, 'circ', pairs(nc, 1, True))  2.83 us
    ppermute x1, starting transfers between devices, body(): pb = lax.ppermute(pb, 'circ', pairs(nc, 1, True))  2.59 us
    ppermute x1, waiting for transfers between devices, body(): tb = lax.ppermute(tb, ('row', 'span'), snake(ns, -1))  1.76 us
    ppermute x1, starting transfers between devices, body(): partner = lax.ppermute(ring, 'row', [(0, 1), (1, 0)])  1.58 us
    ppermute x1, starting transfers between devices, body(): tb = lax.ppermute(tb, ('row', 'span'), snake(ns, -1))  1.52 us
    ppermute x1, waiting for transfers between devices, body(): ta = lax.ppermute(ta, ('row', 'span'), snake(ns, 1))  1.52 us
    ppermute x1, starting transfers between devices, body(): hb = lax.ppermute(sb, ('row', 'span'), snake(ns, -1))  1.52 us
  transfers between devices with their start and end apart: 9, of which 3 were waited for; matrix products, arithmetic and copies ran while one was open for 0% of the time, Pallas kernels for 16%

profile of v7, /device:TPU:0, one launch (start us, length us, event | category | flops | bytes accessed | tf_op | source)
XLA Modules:
  0.0 24.2 jit_solution(8813800628295694142)
XLA Ops:
  0.6 1.6 %shard_map.77 = (f32[5,8,16,256]{3,2,1,0:T(8,128)S(1)}, f32[3,8,16,256]{3,2,1,0:T(8,128)S(1)}, s32[2]{0:T(128)S(1)}, f32[2,4]{1,0:T(2,128)S(1)}, f32[40,128]{1,0:T(8,128)S(1)}, /*index=5*/f32[40,128]{1,0:T(8,128)S(1)}) custom-call(f32[8,16,256]{2,1,0:T(8,128)} %bitcast.13, f32[3,8,16,256]{3,2,1,0:T(8,128)} %bitcast.11, f32[8,16,256]{2,1,0:T(8,128)} %bitcast.14, ...), custom_call_target="tpu_custom_call" | custom-call | tf_op jit(solution)/shard_map/pallas_call | solution.py:26
  2.2 0.1 shard_map.82
  2.3 0.6 %collective-permute-start.7 = (f32[13,16,256]{2,1,0:T(8,128)S(1)}, f32[13,16,256]{2,1,0:T(8,128)S(1)}, u32[]{:S(2)}, u32[]{:S(2)}) collective-permute-start(f32[13,16,256]{2,1,0:T(8,128)S(1)} %get-tuple-element.31), channel_id=1, source_target_pairs={{0,4},{4,0},{8,12},{12,8},{1,5},{5,1},{9,13},{13,9},{2,6},{6,2},{1... | collective-permute-start | bytes 638984 | tf_op jit(solution)/shard_map/ppermute | solution.py:772
  2.9 2.6 %collective-permute-start.8 = (f32[13,16,256]{2,1,0:T(8,128)S(1)}, f32[13,16,256]{2,1,0:T(8,128)S(1)}, u32[]{:S(2)}, u32[]{:S(2)}) collective-permute-start(f32[13,16,256]{2,1,0:T(8,128)S(1)} %get-tuple-element.32), channel_id=1, source_target_pairs={{4,8},{8,4},{12,0},{0,12},{5,9},{9,5},{13,1},{1,13},{6,10},{10,6},... | collective-permute-start | bytes 638984 | tf_op jit(solution)/shard_map/ppermute | solution.py:773
  5.5 1.5 %collective-permute-start.1 = (f32[40,128]{1,0:T(8,128)S(1)}, f32[40,128]{1,0:T(8,128)S(1)}, u32[]{:S(2)}, u32[]{:S(2)}) collective-permute-start(f32[40,128]{1,0:T(8,128)S(1)} %get-tuple-element.26), channel_id=1, source_target_pairs={{0,16},{1,0},{2,1},{3,2},{19,3},{18,19},{17,18},{16,17},{4,20},{5,... | collective-permute-start | bytes 61448 | tf_op jit(solution)/shard_map/ppermute | solution.py:769
  7.0 0.5 %collective-permute-start = (f32[40,128]{1,0:T(8,128)S(1)}, f32[40,128]{1,0:T(8,128)S(1)}, u32[]{:S(2)}, u32[]{:S(2)}) collective-permute-start(f32[40,128]{1,0:T(8,128)S(1)} %get-tuple-element.25.after_ref), channel_id=1, source_target_pairs={{0,1},{1,2},{2,3},{3,19},{19,18},{18,17},{17,16},{16,0},{4,5},{5,6... | collective-permute-start | bytes 61448 | tf_op jit(solution)/shard_map/ppermute | solution.py:768
  7.5 1.8 %collective-permute-done.1.hb_ref = f32[40,128]{1,0:T(8,128)S(1)} collective-permute-done((f32[40,128]{1,0:T(8,128)S(1)}, f32[40,128]{1,0:T(8,128)S(1)}, u32[]{:S(2)}, u32[]{:S(2)}) %collective-permute-start.1) | collective-permute-done | bytes 20512 | tf_op jit(solution)/shard_map/ppermute | solution.py:769
  9.3 1.5 %collective-permute-done.ha_ref = f32[40,128]{1,0:T(8,128)S(1)} collective-permute-done((f32[40,128]{1,0:T(8,128)S(1)}, f32[40,128]{1,0:T(8,128)S(1)}, u32[]{:S(2)}, u32[]{:S(2)}) %collective-permute-start) | collective-permute-done | bytes 20512 | tf_op jit(solution)/shard_map/ppermute | solution.py:768
  10.8 0.4 %shard_map.78 = (f32[56,128]{1,0:T(8,128)S(1)}, f32[80,128]{1,0:T(8,128)S(1)}) custom-call(f32[5,8,16,256]{3,2,1,0:T(8,128)S(1)} %get-tuple-element.24.u_ref, f32[3,8,16,256]{3,2,1,0:T(8,128)S(1)} %get-tuple-element.23.f_ref, f32[40,128]{1,0:T(8,128)S(1)} %collective-permute-done.ha_ref, f32[40,128]{1,0:T(8,128)S(1)} %collective-permute-done.1.hb_ref), custom_call_target="tpu_custom_call" | custom-call | tf_op jit(solution)/shard_map/pallas_call | solution.py:26
  11.1 0.0 collective-permute-start.2
  11.2 0.6 %collective-permute-start.5 = (f32[13,8,256]{2,1,0:T(8,128)S(1)}, f32[13,8,256]{2,1,0:T(8,128)S(1)}, u32[]{:S(2)}, u32[]{:S(2)}) collective-permute-start(f32[13,8,256]{2,1,0:T(8,128)S(1)} %get-tuple-element.29), channel_id=1, source_target_pairs={{0,1},{1,2},{2,3},{3,19},{19,18},{18,17},{17,16},{16,0},{4,5},{5,6... | collective-permute-start | bytes 319496 | tf_op jit(solution)/shard_map/ppermute | solution.py:770
  11.7 1.5 %collective-permute-start.6 = (f32[13,8,256]{2,1,0:T(8,128)S(1)}, f32[13,8,256]{2,1,0:T(8,128)S(1)}, u32[]{:S(2)}, u32[]{:S(2)}) collective-permute-start(f32[13,8,256]{2,1,0:T(8,128)S(1)} %get-tuple-element.30), channel_id=1, source_target_pairs={{0,16},{1,0},{2,1},{3,2},{19,3},{18,19},{17,18},{16,17},{4,20},{5,... | collective-permute-start | bytes 319496 | tf_op jit(solution)/shard_map/ppermute | solution.py:771
  13.3 0.0 collective-permute-done.2.m1_ref
  13.3 0.1 collective-permute-start.3
  13.4 0.9 %shard_map.80.after_ref.one_ref = f32[5,8,16,256]{3,2,1,0:T(8,128)S(1)} custom-call(f32[5,8,16,256]{3,2,1,0:T(8,128)S(1)} %get-tuple-element.24.u_ref, f32[3,8,16,256]{3,2,1,0:T(8,128)S(1)} %get-tuple-element.23.f_ref, f32[80,128]{1,0:T(8,128)S(1)} %shard_map.79.after_ref.m2_ref), custom_call_target="tpu_custom_call" | custom-call | flops 10000000 | bytes 4000000 | tf_op jit(solution)/shard_map/pallas_call | solution.py:26
  14.3 2.8 %collective-permute-done.3.got_ref.m2_ref = f32[80,128]{1,0:T(8,128)S(1)} collective-permute-done((f32[80,128]{1,0:T(8,128)S(1)}, f32[80,128]{1,0:T(8,128)S(1)}, u32[]{:S(2)}, u32[]{:S(2)}) %collective-permute-start.3) | collective-permute-done | bytes 40992 | tf_op jit(solution)/shard_map/ppermute | solution.py:793
  17.1 1.6 %collective-permute-start.4 = (f32[4,24,128]{2,1,0:T(8,128)S(1)}, f32[4,24,128]{2,1,0:T(8,128)S(1)}, u32[]{:S(2)}, u32[]{:S(2)}) collective-permute-start(f32[4,24,128]{2,1,0:T(8,128)S(1)} %shard_map.81), channel_id=1, source_target_pairs={{0,16},{16,0},{1,17},{17,1},{2,18},{18,2},{3,19},{19,3},{4,20},{20... | collective-permute-start | bytes 147464 | tf_op jit(solution)/shard_map/ppermute | solution.py:800
  18.7 0.0 collective-permute-done.5.ha_ref
  18.7 0.0 collective-permute-done.6.hb_ref
  18.7 0.0 collective-permute-done.7.pa_ref
  18.7 0.0 collective-permute-done.8.pb_ref
  18.7 2.5 %shard_map.83 = (f32[5,10,16,128]{3,2,1,0:T(8,128)S(1)}, f32[2,5,8,128]{3,2,1,0:T(8,128)S(1)}, f32[5,8,16,128]{3,2,1,0:T(8,128)S(1)}, f32[5,8,16,128]{3,2,1,0:T(8,128)S(1)}, f32[10,8,128]{2,1,0:T(8,128)S(1)}) custom-call(s32[2]{0:T(128)S(1)} %get-tuple-element.21.off_ref, f32[2,4]{1,0:T(2,128)S(1)} %get-tuple-element.22.wt_ref, ...), custom_call_target="tpu_custom_call" | custom-call | flops 10000000 | bytes 4000000 | tf_op jit(solution)/shard_map/pallas_call | solution.py:26
  21.3 0.0 collective-permute-done.4
  21.3 2.9 %shard_map.84 = (f32[5,8,16,256]{3,2,1,0:T(8,128)}, f32[2,5,8,16]{3,2,1,0:T(8,128)}) custom-call(s32[2]{0:T(128)S(1)} %get-tuple-element.21.off_ref, f32[2,4]{1,0:T(2,128)S(1)} %get-tuple-element.22.wt_ref, f32[3,8,16,256]{3,2,1,0:T(8,128)S(1)} %get-tuple-element.23.f_ref, f32[96,128]{1,0:T(8,128)S(1)} %bitcast.9, f32[96,128]{1,0:T(8,128)S(1)} %bitcast.10, ...), custom_call_target="tpu_custom_call" | custom-call | tf_op jit(solution)/shard_map/pallas_call | solution.py:26
  (2 shorter events, 0.0 us)
Async XLA Ops:
  2.3 16.4 %collective-permute-start.7 = (f32[13,16,256]{2,1,0:T(8,128)S(1)}, f32[13,16,256]{2,1,0:T(8,128)S(1)}, u32[]{:S(2)}, u32[]{:S(2)}) collective-permute-start(f32[13,16,256]{2,1,0:T(8,128)S(1)} %get-tuple-element.31), channel_id=1, source_target_pairs={{0,4},{4,0},{8,12},{12,8},{1,5},{5,1},{9,13},{13,9},{2,6},{6,2},{1... | collective-permute-start | bytes 638984 | tf_op jit(solution)/shard_map/ppermute | solution.py:772
  2.9 15.9 %collective-permute-start.8 = (f32[13,16,256]{2,1,0:T(8,128)S(1)}, f32[13,16,256]{2,1,0:T(8,128)S(1)}, u32[]{:S(2)}, u32[]{:S(2)}) collective-permute-start(f32[13,16,256]{2,1,0:T(8,128)S(1)} %get-tuple-element.32), channel_id=1, source_target_pairs={{4,8},{8,4},{12,0},{0,12},{5,9},{9,5},{13,1},{1,13},{6,10},{10,6},... | collective-permute-start | bytes 638984 | tf_op jit(solution)/shard_map/ppermute | solution.py:773
  5.5 3.8 %collective-permute-start.1 = (f32[40,128]{1,0:T(8,128)S(1)}, f32[40,128]{1,0:T(8,128)S(1)}, u32[]{:S(2)}, u32[]{:S(2)}) collective-permute-start(f32[40,128]{1,0:T(8,128)S(1)} %get-tuple-element.26), channel_id=1, source_target_pairs={{0,16},{1,0},{2,1},{3,2},{19,3},{18,19},{17,18},{16,17},{4,20},{5,... | collective-permute-start | bytes 61448 | tf_op jit(solution)/shard_map/ppermute | solution.py:769
  7.0 3.8 %collective-permute-start = (f32[40,128]{1,0:T(8,128)S(1)}, f32[40,128]{1,0:T(8,128)S(1)}, u32[]{:S(2)}, u32[]{:S(2)}) collective-permute-start(f32[40,128]{1,0:T(8,128)S(1)} %get-tuple-element.25.after_ref), channel_id=1, source_target_pairs={{0,1},{1,2},{2,3},{3,19},{19,18},{18,17},{17,16},{16,0},{4,5},{5,6... | collective-permute-start | bytes 61448 | tf_op jit(solution)/shard_map/ppermute | solution.py:768
  11.1 2.1 %collective-permute-start.2 = (f32[56,128]{1,0:T(8,128)S(1)}, f32[56,128]{1,0:T(8,128)S(1)}, u32[]{:S(2)}, u32[]{:S(2)}) collective-permute-start(f32[56,128]{1,0:T(8,128)S(1)} %get-tuple-element.27), channel_id=1, source_target_pairs={{0,4},{4,0},{8,12},{12,8},{1,5},{5,1},{9,13},{13,9},{2,6},{6,2},{1... | collective-permute-start | bytes 86024 | tf_op jit(solution)/shard_map/ppermute | solution.py:782
  11.2 7.5 %collective-permute-start.5 = (f32[13,8,256]{2,1,0:T(8,128)S(1)}, f32[13,8,256]{2,1,0:T(8,128)S(1)}, u32[]{:S(2)}, u32[]{:S(2)}) collective-permute-start(f32[13,8,256]{2,1,0:T(8,128)S(1)} %get-tuple-element.29), channel_id=1, source_target_pairs={{0,1},{1,2},{2,3},{3,19},{19,18},{18,17},{17,16},{16,0},{4,5},{5,6... | collective-permute-start | bytes 319496 | tf_op jit(solution)/shard_map/ppermute | solution.py:770
  11.7 7.0 %collective-permute-start.6 = (f32[13,8,256]{2,1,0:T(8,128)S(1)}, f32[13,8,256]{2,1,0:T(8,128)S(1)}, u32[]{:S(2)}, u32[]{:S(2)}) collective-permute-start(f32[13,8,256]{2,1,0:T(8,128)S(1)} %get-tuple-element.30), channel_id=1, source_target_pairs={{0,16},{1,0},{2,1},{3,2},{19,3},{18,19},{17,18},{16,17},{4,20},{5,... | collective-permute-start | bytes 319496 | tf_op jit(solution)/shard_map/ppermute | solution.py:771
  13.3 3.9 %collective-permute-start.3 = (f32[80,128]{1,0:T(8,128)S(1)}, f32[80,128]{1,0:T(8,128)S(1)}, u32[]{:S(2)}, u32[]{:S(2)}) collective-permute-start(f32[80,128]{1,0:T(8,128)S(1)} %shard_map.79.after_ref.m2_ref), channel_id=1, source_target_pairs={{4,8},{8,4},{12,0},{0,12},{5,9},{9,5},{13,1},{1,13},{6,10},{10,6},... | collective-permute-start | bytes 122888 | tf_op jit(solution)/shard_map/ppermute | solution.py:793
  17.1 4.2 %collective-permute-start.4 = (f32[4,24,128]{2,1,0:T(8,128)S(1)}, f32[4,24,128]{2,1,0:T(8,128)S(1)}, u32[]{:S(2)}, u32[]{:S(2)}) collective-permute-start(f32[4,24,128]{2,1,0:T(8,128)S(1)} %shard_map.81), channel_id=1, source_target_pairs={{0,16},{16,0},{1,17},{17,1},{2,18},{18,2},{3,19},{19,3},{4,20},{20... | collective-permute-start | bytes 147464 | tf_op jit(solution)/shard_map/ppermute | solution.py:800
